TPU v7x, 512 devices: a whole 4x4x16 slice. The times are simulated.
512 devices in a mesh: fsdp: 64 (over z, y_hi, core), ctx: 8 (over x, y_lo).
Axes of the slice: x: 4, y: 4 (y_hi: 2, y_lo: 2; y = y_hi * 2 + y_lo), z: 16, core: 2. Of those that a mesh axis runs over, the one named last changes fastest.
Arguments:
- queries: bfloat16 [64, 1024, 1536], P('fsdp', 'ctx'), may hold values from -1.6953125 to 1.6953125
- key_states: bfloat16 [64, 1024, 1536], P('fsdp', 'ctx'), may hold values from -1.6953125 to 1.6953125
- value_states: bfloat16 [64, 1024, 1536], P('fsdp', 'ctx'), may hold values from -6 to 6
- attn_out: bfloat16 [64, 1024, 1536], P('fsdp', 'ctx'), may hold values from -6 to 6
- log_norm: bfloat16 [64, 1024, 12], P('fsdp', 'ctx'), may hold values from 3 to 4.5
- out_grad: bfloat16 [64, 1024, 3072], P('fsdp', 'ctx'), may hold values from -6 to 6
- proj_weight: bfloat16 [1536, 3072], P('fsdp', 'ctx'), may hold values from -0.109375 to 0.109375
- tile_mask: int32 [64, 12, 16, 16], P('fsdp'), may hold values from 0 to 1, as said below
Outputs:
- grad_query: bfloat16 [64, 1024, 1536], P('fsdp', 'ctx')
- grad_key: bfloat16 [64, 1024, 1536], P('fsdp', 'ctx')
- grad_value: bfloat16 [64, 1024, 1536], P('fsdp', 'ctx')
Inputs may be any that keep to these rules, and one draw needn't show every extreme that they name: tile_mask[c, h, i, j] = 1 lets the query tokens of tile i attend to the key tokens of tile j in head h; a tile is 64 consecutive tokens; every tile attends to itself.
All inputs are finite; a program needn't handle non-finite values.
Results may differ from a plain program's by a relative error of at most 0.014.
Values may be sent and summed in bfloat16 or wider, within the bound.
No kernel may reach another device: no remote copies, remote signals or barrier semaphores. Data moves between devices by JAX's collectives and lax.ppermute only.
A program may use at most 64 MiB of HBM per device.

v0:
```python
import jax
import jax.numpy as jnp
from jax import lax
from jax.sharding import PartitionSpec as P

H = 12
HD = 128
TILE = 64


def round_trip(array):
    return lax.optimization_barrier(array.astype(jnp.bfloat16)).astype(jnp.float32)


def tile_onehot(row_count, tile_count):
    tile_ids = jnp.arange(row_count, dtype=jnp.int32) // TILE
    return (tile_ids[:, None] == jnp.arange(tile_count, dtype=jnp.int32)[None, :]).astype(
        jnp.float32
    )


def score_terms(
    query_head_rows, gradient_by_head, norm_rows, dots_rows, key_head_rows, value_head_rows, allowed
):
    score_scale = HD ** (-0.5)
    scores = (
        jnp.einsum(
            "vgl,ygl->gvy", query_head_rows, key_head_rows, preferred_element_type=jnp.float32
        )
        * score_scale
    )
    attn_prob = jnp.exp(scores - norm_rows.T[:, :, None]) * allowed
    prob_grad = jnp.einsum(
        "vgl,ygl->gvy", gradient_by_head, value_head_rows, preferred_element_type=jnp.float32
    )
    score_grad = attn_prob * (prob_grad - dots_rows.T[:, :, None])
    return (attn_prob.astype(jnp.bfloat16), score_grad.astype(jnp.bfloat16))


def local(queries, key_states, value_states, attn_out, log_norm, out_grad, proj_weight, tile_mask):
    ctx_count = lax.axis_size("ctx")
    ctx_index = lax.axis_index("ctx")
    tok_rows = queries.shape[1]
    hid_width = queries.shape[2]
    score_scale = HD ** (-0.5)
    tile_table = tile_mask[0]
    tile_count = tile_table.shape[1]
    own_count = tok_rows // TILE
    grad_slab = lax.all_to_all(out_grad[0], "ctx", split_axis=1, concat_axis=0, tiled=True)
    product = lax.dot_general(
        grad_slab,
        lax.all_gather(proj_weight, "fsdp", axis=0, tiled=True),
        (((1,), (1,)), ((), ())),
        preferred_element_type=jnp.float32,
    )
    partial_value = product.astype(jnp.bfloat16)
    arrived = lax.all_to_all(
        partial_value.reshape(ctx_count, tok_rows, hid_width),
        "ctx",
        split_axis=0,
        concat_axis=0,
        tiled=True,
    )
    attn_grad = jnp.sum(arrived.astype(jnp.float32), axis=0).astype(jnp.bfloat16)
    query_head_rows = queries[0].reshape(tok_rows, H, HD)
    gradient_by_head = attn_grad.reshape(tok_rows, H, HD)
    out_heads = attn_out[0].reshape(tok_rows, H, HD)
    dots_round = jnp.sum(
        gradient_by_head.astype(jnp.float32) * out_heads.astype(jnp.float32), axis=-1
    ).astype(jnp.bfloat16)
    own_rows = jnp.repeat(
        lax.dynamic_slice_in_dim(tile_table, ctx_index * own_count, own_count, 1).astype(
            jnp.float32
        ),
        TILE,
        axis=1,
    )
    norm_rows = log_norm[0].astype(jnp.float32)
    dots_rows = lax.optimization_barrier(dots_round).astype(jnp.float32)
    key_rows = lax.all_gather(key_states[0], "ctx", axis=0, tiled=True)
    value_rows = lax.all_gather(value_states[0], "ctx", axis=0, tiled=True)
    piece_rows = key_rows.shape[0]
    sub_rows = min(piece_rows, tok_rows)
    blocks_in = piece_rows // sub_rows
    key_block = key_rows.reshape(piece_rows, H, HD)
    value_block = value_rows.reshape(piece_rows, H, HD)
    allowed = jnp.einsum("htn,mn->htm", own_rows, tile_onehot(piece_rows, tile_count))
    probability_per_round, gradient_per_round = score_terms(
        query_head_rows, gradient_by_head, norm_rows, dots_rows, key_block, value_block, allowed
    )
    value_term = jnp.einsum(
        "bve,vbt->ebt", probability_per_round, gradient_by_head, preferred_element_type=jnp.float32
    )
    key_term = (
        jnp.einsum(
            "bve,vbt->ebt", gradient_per_round, query_head_rows, preferred_element_type=jnp.float32
        )
        * score_scale
    )
    query_term = (
        jnp.einsum(
            "hmbn,bnhd->bmhd",
            gradient_per_round.reshape(H, tok_rows, blocks_in, sub_rows),
            key_block.reshape(blocks_in, sub_rows, H, HD),
            preferred_element_type=jnp.float32,
        )
        * score_scale
    )
    part_slots = query_term.reshape(blocks_in, tok_rows, hid_width)
    key_total = key_term.reshape(piece_rows, hid_width)
    value_total = value_term.reshape(piece_rows, hid_width)
    part_slots, key_total, value_total = (part_slots, key_total, value_total)
    grad_query = jnp.sum(round_trip(part_slots), axis=0).astype(jnp.bfloat16)
    key_parts, value_parts = (
        lax.all_to_all(
            key_total.astype(jnp.bfloat16).reshape(ctx_count, tok_rows, hid_width),
            "ctx",
            split_axis=0,
            concat_axis=0,
            tiled=True,
        ),
        lax.all_to_all(
            value_total.astype(jnp.bfloat16).reshape(ctx_count, tok_rows, hid_width),
            "ctx",
            split_axis=0,
            concat_axis=0,
            tiled=True,
        ),
    )
    grad_key = jnp.sum(key_parts.astype(jnp.float32), axis=0).astype(jnp.bfloat16)
    grad_value = jnp.sum(value_parts.astype(jnp.float32), axis=0).astype(jnp.bfloat16)
    return (grad_query[None], grad_key[None], grad_value[None])


def solution(mesh):
    placed = (
        P("fsdp", "ctx", None),
        P("fsdp", "ctx", None),
        P("fsdp", "ctx", None),
        P("fsdp", "ctx", None),
        P("fsdp", "ctx", None),
        P("fsdp", "ctx", None),
        P("fsdp", "ctx"),
        P("fsdp", None, None, None),
    )
    return jax.shard_map(
        local,
        mesh=mesh,
        in_specs=placed,
        out_specs=(P("fsdp", "ctx", None), P("fsdp", "ctx", None), P("fsdp", "ctx", None)),
        check_vma=False,
    )
```

profile of v0, /device:TPU:16, one launch (start us, length us, event | category | flops | bytes accessed | tf_op | source)
XLA Modules:
  0.0 475.0 jit_solution(17062249708832185526)
XLA Ops:
  7.9 1.9 copy.74
  9.9 1.9 copy.81
  11.9 1.5 copy.78
  13.4 17.4 %all_to_all.34 = bf16[128,8,384]{0,2,1:T(8,128)(2,1)S(1)} all-to-all(bf16[128,8,384]{0,2,1:T(8,128)(2,1)S(1)} %bitcast.82), channel_id=1, replica_groups=mesh['fsdp'=64,'ctx'=8] {'ctx'}, dimensions={1} | all-to-all | bytes 1572864 | tf_op jit(solution)/shard_map/all_to_all | solution.py:49
  31.1 123.9 %all-gather.6.cloned.1.call-done = bf16[1536,384]{1,0:T(8,128)(2,1)} async-done(((bf16[24,384]{1,0:T(8,128)(2,1)}), bf16[1536,384]{1,0:T(8,128)(2,1)}) %all-gather.6.cloned.1.call-update) | async-done | bytes 1179664 | tf_op jit(solution)/shard_map/all_gather | solution.py:52
  155.0 4.7 convolution_convert_fusion
  159.7 5.6 %all-to-all-start.1 = ((bf16[8,128,1536]{2,1,0:T(8,128)(2,1)}), bf16[8,128,1536]{2,1,0:T(8,128)(2,1)S(1)}, u32[]{:S(2)}, u32[]{:S(2)}) async-start(bf16[8,128,1536]{2,1,0:T(8,128)(2,1)} %bitcast.79), calls=%async_computation.1 | async-start | bytes 6291456 | tf_op jit(solution)/shard_map/all_to_all | solution.py:57
  165.3 1.2 copy.73
  168.2 1.7 broadcast_in_dim.16
  169.9 1.6 reshape.60
  171.5 1.9 copy.84
  173.5 43.7 %all-to-all-done.1 = bf16[8,128,1536]{2,1,0:T(8,128)(2,1)S(1)} async-done(((bf16[8,128,1536]{2,1,0:T(8,128)(2,1)}), bf16[8,128,1536]{2,1,0:T(8,128)(2,1)S(1)}, u32[]{:S(2)}, u32[]{:S(2)}) %all-to-all-start.1) | async-done | bytes 3145760 | tf_op jit(solution)/shard_map/all_to_all | solution.py:57
  217.1 1.3 reduce_sum.57
  220.8 48.4 %all-gather.8.cloned.1.call-done = bf16[1,1024,1536]{1,2,0:T(8,128)(2,1)} async-done(((bf16[1,128,1536]{1,2,0:T(8,128)(2,1)}), bf16[1,1024,1536]{1,2,0:T(8,128)(2,1)}) %all-gather.8.cloned.1.call-update) | async-done | bytes 3145744 | tf_op jit(solution)/shard_map/all_gather | solution.py:80
  269.2 2.9 fusion.21
  272.1 4.1 exponential_multiply_fusion
  276.3 73.7 %all-gather.10.cloned.1.call-done = bf16[1,1024,1536]{1,2,0:T(8,128)(2,1)} async-done(((bf16[1,128,1536]{1,2,0:T(8,128)(2,1)}), bf16[1,1024,1536]{1,2,0:T(8,128)(2,1)}) %all-gather.10.cloned.1.call-update) | async-done | bytes 3145744 | tf_op jit(solution)/shard_map/all_gather | solution.py:81
  349.9 4.9 %multiply_convert_fusion.2 = bf16[12,128,1024]{2,1,0:T(8,128)(2,1)S(1)} fusion(f32[12,128,1024]{2,1,0:T(8,128)} %exponential_multiply_fusion, f32[12,128]{1,0:T(8,128)S(1)} %convert_bitcast_fusion.2, bf16[128,12,128]{0,2,1:T(8,128)(2,1)S(1)} %bitcast.75, bf16[1024,12,128]{0,2,1:T(8,128)(2,1)} %bitcast.83), kind=kOutput, calls=%fused_computation.2 | convolution fusion | flops 407371776 | bytes 12982272 | tf_op jit(solution)/shard_map/vgl,ygl->gvy/dot_general | solution.py:33
  354.9 1.6 copy-done.1
  356.6 1.3 fusion
  357.9 2.9 copy.89
  360.7 2.7 copy.107
  363.4 2.2 copy.90
  365.6 5.6 %all-to-all-start.2 = ((bf16[8,128,1536]{1,2,0:T(8,128)(2,1)}), bf16[8,128,1536]{1,2,0:T(8,128)(2,1)}, u32[]{:S(2)}, u32[]{:S(2)}) async-start(bf16[8,128,1536]{1,2,0:T(8,128)(2,1)} %copy.90), calls=%async_computation.2 | async-start | bytes 6291456 | tf_op jit(solution)/shard_map/all_to_all | solution.py:115
  371.2 3.7 fusion.11
  375.7 2.2 copy.92
  377.9 38.2 %all-to-all-done.2 = bf16[8,128,1536]{1,2,0:T(8,128)(2,1)} async-done(((bf16[8,128,1536]{1,2,0:T(8,128)(2,1)}), bf16[8,128,1536]{1,2,0:T(8,128)(2,1)}, u32[]{:S(2)}, u32[]{:S(2)}) %all-to-all-start.2) | async-done | bytes 3145760 | tf_op jit(solution)/shard_map/all_to_all | solution.py:115
  416.1 4.4 all-to-all-start.3
  422.5 2.3 multiply_convert_fusion.1
  426.4 2.5 reduce_sum.60
  429.8 35.2 %all-to-all-done.3 = bf16[8,128,1536]{1,2,0:T(8,128)(2,1)} async-done(((bf16[8,128,1536]{1,2,0:T(8,128)(2,1)}), bf16[8,128,1536]{1,2,0:T(8,128)(2,1)}, u32[]{:S(2)}, u32[]{:S(2)}) %all-to-all-start.3) | async-done | bytes 3145760 | tf_op jit(solution)/shard_map/all_to_all | solution.py:122
  465.1 2.5 reduce_sum.61
  (33 shorter events, 11.3 us)
Async XLA Ops:
  7.2 147.8 %all-gather.6.cloned.1.call-start = ((), (), s32[]{:S(2)}) async-start(), calls=%async_computation.4 | async-start | bytes 1198080 | tf_op jit(solution)/shard_map/all_gather | solution.py:52
  7.9 261.3 %all-gather.8.cloned.1.call-start = ((), (), s32[]{:S(2)}) async-start(), calls=%async_computation.5 | async-start | bytes 3538944 | tf_op jit(solution)/shard_map/all_gather | solution.py:80
  9.9 340.1 %all-gather.10.cloned.1.call-start = ((), (), s32[]{:S(2)}) async-start(), calls=%async_computation.6 | async-start | bytes 3538944 | tf_op jit(solution)/shard_map/all_gather | solution.py:81
  159.7 13.7 %copy-start.6 = (bf16[1,128,12]{1,2,0:T(8,128)(2,1)S(1)}, bf16[1,128,12]{1,2,0:T(8,128)(2,1)}, u32[]{:S(2)}) copy-start(bf16[1,128,12]{1,2,0:T(8,128)(2,1)} %param.12) | copy-start | bytes 9220
  159.7 57.4 %all-to-all-start.1 = ((bf16[8,128,1536]{2,1,0:T(8,128)(2,1)}), bf16[8,128,1536]{2,1,0:T(8,128)(2,1)S(1)}, u32[]{:S(2)}, u32[]{:S(2)}) async-start(bf16[8,128,1536]{2,1,0:T(8,128)(2,1)} %bitcast.79), calls=%async_computation.1 | async-start | bytes 6291456 | tf_op jit(solution)/shard_map/all_to_all | solution.py:57
  166.5 102.7 %copy-start.3 = (bf16[1,128,1536]{1,2,0:T(8,128)(2,1)}, bf16[1,128,1536]{1,2,0:T(8,128)(2,1)S(1)}, u32[]{:S(2)}) copy-start(bf16[1,128,1536]{1,2,0:T(8,128)(2,1)S(1)} %copy.73) | copy-start | bytes 1179652
  269.2 2.9 copy-start.5
  349.9 6.6 %copy-start.4 = (bf16[1,128,1536]{1,2,0:T(8,128)(2,1)S(1)}, bf16[1,128,1536]{1,2,0:T(8,128)(2,1)}, u32[]{:S(2)}) copy-start(bf16[1,128,1536]{1,2,0:T(8,128)(2,1)} %copy-done.3) | copy-start | bytes 1179652
  354.9 1.7 copy-start.1
  365.6 50.5 %all-to-all-start.2 = ((bf16[8,128,1536]{1,2,0:T(8,128)(2,1)}), bf16[8,128,1536]{1,2,0:T(8,128)(2,1)}, u32[]{:S(2)}, u32[]{:S(2)}) async-start(bf16[8,128,1536]{1,2,0:T(8,128)(2,1)} %copy.90), calls=%async_computation.2 | async-start | bytes 6291456 | tf_op jit(solution)/shard_map/all_to_all | solution.py:115
  377.9 42.7 %copy-start = (bf16[1,1024,1536]{1,2,0:T(8,128)(2,1)S(1)}, bf16[1,1024,1536]{1,2,0:T(8,128)(2,1)}, u32[]{:S(2)}) copy-start(bf16[1,1024,1536]{1,2,0:T(8,128)(2,1)} %all-gather.8.cloned.1.call-done) | copy-start | bytes 9437188
  416.1 48.9 %all-to-all-start.3 = ((bf16[8,128,1536]{1,2,0:T(8,128)(2,1)}), bf16[8,128,1536]{1,2,0:T(8,128)(2,1)}, u32[]{:S(2)}, u32[]{:S(2)}) async-start(bf16[8,128,1536]{1,2,0:T(8,128)(2,1)} %copy.92), calls=%async_computation.3 | async-start | bytes 6291456 | tf_op jit(solution)/shard_map/all_to_all | solution.py:122
  420.6 1.9 copy-start.2
Sparse Core Ops, SparseCore 0:
  11.2 143.7 all-gather.5
  157.6 111.5 all-gather.7
  271.2 78.6 all-gather.9
where the time goes:
time: 476 us; the launch traced here: 475 us
  waiting for transfers between devices  364 us (76%)
  local copies, waits for them, and re-layouts  31.2 us (7%)
  matrix products  24.1 us (5%)
  blocking collectives  17.4 us (4%)
  starting transfers between devices  15.7 us (3%)
  between operations  13.9 us (3%)
  other arithmetic  8.98 us (2%)
    all_gather x1, waiting for transfers between devices, local(): lax.all_gather(proj_weight, 'fsdp', axis=0, tiled=True)  124 us
    all_gather x1, waiting for transfers between devices, local(): value_rows = lax.all_gather(value_states[0], 'ctx', axis=0, tiled=True)  73.7 us
    all_gather x1, waiting for transfers between devices, local(): key_rows = lax.all_gather(key_states[0], 'ctx', axis=0, tiled=True)  48.4 us
    all_to_all x1, waiting for transfers between devices, local(): lax.all_to_all(partial_value.reshape(ctx_count, tok_rows, hid_width), 'ct...  43.7 us
    all_to_all x1, waiting for transfers between devices, local(): lax.all_to_all(key_total.astype(jnp.bfloat16).reshape(ctx_count, tok_rows...  38.2 us
    all_to_all x1, waiting for transfers between devices, local(): lax.all_to_all(value_total.astype(jnp.bfloat16).reshape(ctx_count, tok_ro...  35.2 us
    unnamed x25, local copies, waits for them, and re-layouts  18.3 us
    all_to_all x1, blocking collectives, local(): lax.all_to_all(out_grad[0], 'ctx', split_axis=1, concat_axis=0, tiled=True)  17.4 us
  transfers between devices with their start and end apart: 6, of which 6 were waited for; matrix products, arithmetic and copies ran while one was open for 9% of the time, Pallas kernels for 0%

commit v1 on v0

v1 whole, which is shorter than its diff:
```python
import functools
import math

import jax
import jax.numpy as jnp
from jax import lax
from jax.experimental import pallas as pl
from jax.experimental.pallas import tpu as pltpu
from jax.sharding import Mesh, PartitionSpec as P

BF = jnp.bfloat16
F32 = jnp.float32
HD = 128
TILE = 64
SCALE = HD**-0.5
LOG2E = math.log2(math.e)

QA, KA, VA, OA, KC, VC, QC, OC, NR = 0, 128, 256, 384, 512, 640, 768, 832, 896
IN_ROWS = 912
MID = 192
GQA, GKA, GVA, GKC, GVC, GQC = 0, 128, 256, 384, 512, 640
OUT_ROWS = 704

NT_DIMS = (((1,), (1,)), ((), ()))
NN_DIMS = (((1,), (0,)), ((), ()))
TN_DIMS = (((0,), (0,)), ((), ()))


def dot(a, b, dims):
    return lax.dot_general(a, b, dims, preferred_element_type=F32)


def pack_kernel(q_ref, k_ref, v_ref, o_ref, n_ref, g_ref, in_ref, slab_ref):
    slab_ref[0] = g_ref[...]
    for j in range(2):
        own = slice(HD * j, HD * (j + 1))
        shared = slice(2 * HD, 3 * HD)
        half = slice(TILE * j, TILE * (j + 1))
        in_ref[j, QA : QA + 128] = q_ref[:, own]
        in_ref[j, KA : KA + 128] = k_ref[:, own]
        in_ref[j, VA : VA + 128] = v_ref[:, own]
        in_ref[j, OA : OA + 128] = o_ref[:, own]
        in_ref[j, KC : KC + 128] = k_ref[:, shared]
        in_ref[j, VC : VC + 128] = v_ref[:, shared]
        in_ref[j, QC : QC + 64] = q_ref[half, shared]
        in_ref[j, OC : OC + 64] = o_ref[half, shared]
        in_ref[j, NR:IN_ROWS] = n_ref[0, j]


def pack(q, k, v, o, norm_rows, out_grad):
    wide = pl.BlockSpec((128, 3 * HD), lambda i: (0, i))
    return pl.pallas_call(
        pack_kernel,
        grid=(4,),
        in_specs=[wide] * 4
        + [pl.BlockSpec((1, 2, 16, 128), lambda i: (i, 0, 0, 0)), pl.BlockSpec((128, 768), lambda i: (0, i))],
        out_specs=(
            pl.BlockSpec((2, IN_ROWS, 128), lambda i: (i, 0, 0)),
            pl.BlockSpec((1, 128, 768), lambda i: (i, 0, 0)),
        ),
        out_shape=(
            jax.ShapeDtypeStruct((8, IN_ROWS, 128), BF),
            jax.ShapeDtypeStruct((4, 128, 768), BF),
        ),
        name="pack",
    )(q, k, v, o, norm_rows, out_grad)


def project_kernel(core_ref, own_ref, other_ref, g_ref, out_ref, w_ref):
    mine = core_ref[0] == 0
    for z in range(4):
        for yh in range(2):
            for yl in range(2):
                a = own_ref[yh, yl, z]
                b = other_ref[yh, yl, z]
                for c in range(2):
                    row = 24 * (4 * z + 2 * yh + c)
                    piece = jnp.where(mine, a, b) if c == 0 else jnp.where(mine, b, a)
                    w_ref[row : row + 24, 384 * yl : 384 * (yl + 1)] = piece
    g = g_ref[...].reshape(512, 768)
    part = dot(g, w_ref[...], NT_DIMS).astype(BF)
    for x in range(4):
        rows = slice(128 * x, 128 * (x + 1))
        for j in range(2):
            base = MID * x
            out_ref[j, base : base + 128] = part[rows, HD * j : HD * (j + 1)]
            out_ref[j, base + 128 : base + MID] = part[128 * x + 64 * j : 128 * x + 64 * (j + 1), 2 * HD :]


def project(core, own, other, slab):
    shard = pl.BlockSpec((2, 2, 4, 24, 384), lambda i: (0, 0, i, 0, 0))
    return pl.pallas_call(
        project_kernel,
        grid=(4,),
        in_specs=[
            pl.BlockSpec(memory_space=pltpu.SMEM),
            shard,
            shard,
            pl.BlockSpec((4, 128, 768), lambda i: (0, 0, 0)),
        ],
        out_specs=pl.BlockSpec((2, 4 * MID, 128), lambda i: (i, 0, 0)),
        out_shape=jax.ShapeDtypeStruct((8, 4 * MID, 128), BF),
        scratch_shapes=[pltpu.VMEM((384, 768), BF)],
        name="project",
    )(core, own, other, slab)


def attend_unit(in_ref, mid_ref, mask_ref, out_ref, dk_ref, dv_ref, per, rows, norm_row, outs):
    q0, o0, k0, v0, m0 = rows
    gq0, gk0, gv0 = outs
    group = 256 // per
    keys = 1024
    chunk = 256
    for b in range(8 // group):
        sources = range(group * b, group * (b + 1))
        q = jnp.concatenate([in_ref[s, q0 : q0 + per] for s in sources], axis=0)
        o = jnp.concatenate([in_ref[s, o0 : o0 + per] for s in sources], axis=0)
        pieces = []
        for s in sources:
            base = MID * (s // 2) + m0
            total = mid_ref[s % 2, base : base + per].astype(F32)
            for x in range(1, 4):
                total = total + mid_ref[2 * x + s % 2, base : base + per].astype(F32)
            pieces.append(total.astype(BF))
        g = jnp.concatenate(pieces, axis=0)
        product = g.astype(F32) * o.astype(F32)
        dots = lax.dot_general(
            jnp.ones((8, 128), F32), product, NT_DIMS, precision=lax.Precision.HIGHEST, preferred_element_type=F32
        )[0:1]
        dots = dots.astype(BF).astype(F32)
        norm = norm_row(b)
        dq = jnp.zeros((HD, 256), F32)
        for n in range(keys // chunk):
            src = slice(2 * n, 2 * n + 2)
            k = in_ref[src, k0 : k0 + 128].reshape(chunk, HD)
            v = in_ref[src, v0 : v0 + 128].reshape(chunk, HD)
            scores = dot(k, q, NT_DIMS)
            prob = jnp.exp2(scores * (SCALE * LOG2E) - norm)
            allowed = mask_ref[4 * n : 4 * (n + 1), 256 * b : 256 * (b + 1)]
            prob = (prob.reshape(4, TILE, 256) * allowed[:, None, :]).reshape(chunk, 256)
            score_grad = prob * (dot(v, g, NT_DIMS) - dots)
            prob = prob.astype(BF)
            score_grad = score_grad.astype(BF)
            dv = dot(prob, g, NN_DIMS)
            dk = dot(score_grad, q, NN_DIMS)
            at = slice(chunk * n, chunk * (n + 1))
            if b == 0:
                dv_ref[at] = dv
                dk_ref[at] = dk
            else:
                dv_ref[at] += dv
                dk_ref[at] += dk
            dq = dq + dot(k, score_grad, TN_DIMS)
        dq = (dq.T * SCALE).astype(BF)
        for e, s in enumerate(sources):
            out_ref[s, gq0 : gq0 + per] = dq[per * e : per * (e + 1)]
    for s in range(8):
        at = slice(128 * s, 128 * (s + 1))
        out_ref[s, gk0 : gk0 + 128] = (dk_ref[at] * SCALE).astype(BF)
        out_ref[s, gv0 : gv0 + 128] = dv_ref[at].astype(BF)


def attend_kernel(y_ref, in_ref, mid_ref, mask_a_ref, mask_c_ref, out_ref, dk_ref, dv_ref):
    second = y_ref[0] == 1

    def norm_a(b):
        parts = [in_ref[s, NR : NR + 16].astype(F32)[0:1] for s in (2 * b, 2 * b + 1)]
        return jnp.concatenate(parts, axis=1) * LOG2E

    def norm_c(b):
        parts = []
        for s in range(4 * b, 4 * b + 4):
            row = in_ref[s, NR : NR + 16].astype(F32)[1:2]
            parts.append(jnp.where(second, row[:, 64:], row[:, :64]))
        return jnp.concatenate(parts, axis=1) * LOG2E

    attend_unit(
        in_ref, mid_ref, mask_a_ref, out_ref, dk_ref, dv_ref, 128, (QA, OA, KA, VA, 0), norm_a, (GQA, GKA, GVA)
    )
    attend_unit(
        in_ref, mid_ref, mask_c_ref, out_ref, dk_ref, dv_ref, 64, (QC, OC, KC, VC, 128), norm_c, (GQC, GKC, GVC)
    )


def attend(y_index, arrived, partial, mask_a, mask_c):
    whole = pl.BlockSpec(memory_space=pltpu.VMEM)
    return pl.pallas_call(
        attend_kernel,
        in_specs=[pl.BlockSpec(memory_space=pltpu.SMEM), whole, whole, whole, whole],
        out_specs=whole,
        out_shape=jax.ShapeDtypeStruct((8, OUT_ROWS, 128), BF),
        scratch_shapes=[pltpu.VMEM((1024, 128), F32), pltpu.VMEM((1024, 128), F32)],
        name="attend",
    )(y_index, arrived, partial, mask_a, mask_c)


def merge_kernel(in_ref, gq_ref, gk_ref, gv_ref):
    for j in range(2):
        own = slice(HD * j, HD * (j + 1))
        gq_ref[0, :, own] = in_ref[j, GQA : GQA + 128]
        gk_ref[0, :, own] = in_ref[j, GKA : GKA + 128]
        gv_ref[0, :, own] = in_ref[j, GVA : GVA + 128]
        gq_ref[0, TILE * j : TILE * (j + 1), 2 * HD :] = in_ref[j, GQC : GQC + 64]
    for ref, at in ((gk_ref, GKC), (gv_ref, GVC)):
        total = in_ref[0, at : at + 128].astype(F32) + in_ref[1, at : at + 128].astype(F32)
        ref[0, :, 2 * HD :] = total.astype(BF)


def merge(arrived):
    out = pl.BlockSpec((1, 128, 3 * HD), lambda i: (0, 0, i))
    shape = jax.ShapeDtypeStruct((1, 128, 1536), BF)
    return pl.pallas_call(
        merge_kernel,
        grid=(4,),
        in_specs=[pl.BlockSpec((2, OUT_ROWS, 128), lambda i: (i, 0, 0))],
        out_specs=(out, out, out),
        out_shape=(shape, shape, shape),
        name="merge",
    )(arrived)


def exchange(array, axes):
    return lax.all_to_all(array, axes, split_axis=0, concat_axis=0, tiled=True)


def spread(array, axes, count):
    return exchange(jnp.broadcast_to(array[None], (count,) + array.shape), axes)


def gather_weight(proj_weight):
    own = spread(proj_weight, "z", 16)
    own = spread(own, ("yh", "yl"), 4).reshape(2, 2, 16, 24, 384)
    other = lax.ppermute(own, "core", [(0, 1), (1, 0)])
    return own, other


def mask_rows(tile_mask):
    x, y = lax.axis_index("x"), lax.axis_index("yl")
    table = tile_mask[0].astype(F32).transpose(0, 2, 1)
    whole = lax.dynamic_index_in_dim(table, 3 * x + y, 0, keepdims=False)
    shared = lax.dynamic_index_in_dim(table, 3 * x + 2, 0, keepdims=False).reshape(16, 8, 2)
    shared = lax.dynamic_index_in_dim(shared, y, 2, keepdims=False)
    return jnp.repeat(whole, TILE, axis=1), jnp.repeat(shared, TILE, axis=1)


def norm_table(log_norm):
    rows = log_norm[0].T.reshape(4, 3, 128)
    both = jnp.stack([rows[:, :2], jnp.broadcast_to(rows[:, 2:], (4, 2, 128))], axis=2)
    return jnp.pad(both, ((0, 0), (0, 0), (0, 14), (0, 0)))


def after_weight(q, k, v, o, log_norm, out_grad, own, other, core, tile_mask):
    sent, slab = pack(q[0], k[0], v[0], o[0], norm_table(log_norm), out_grad[0])
    slab = exchange(slab, "x")
    arrived = exchange(sent, ("x", "yl"))
    partial = exchange(project(core, own, other, slab), ("x", "yl"))
    mask_a, mask_c = mask_rows(tile_mask)
    y_index = lax.axis_index("yl").reshape(1)
    result = exchange(attend(y_index, arrived, partial, mask_a, mask_c), ("x", "yl"))
    return merge(result)


def local(queries, key_states, value_states, attn_out, log_norm, out_grad, proj_weight, tile_mask):
    own, other = gather_weight(proj_weight)
    core = lax.axis_index("core").reshape(1)
    return after_weight(
        queries, key_states, value_states, attn_out, log_norm, out_grad, own, other, core, tile_mask
    )


def solution(mesh):
    inner = Mesh(mesh.devices.reshape(16, 2, 2, 4, 2), ("z", "yh", "core", "x", "yl"))
    clips, tokens = ("z", "yh", "core"), ("x", "yl")
    rows = P(clips, tokens, None)
    return jax.shard_map(
        local,
        mesh=inner,
        in_specs=(rows,) * 6 + (P(clips, tokens), P(clips, None, None, None)),
        out_specs=(rows, rows, rows),
        check_vma=False,
    )
```

time: 476 us -> 165 us (0.35)
  the two profiles are of different devices: /device:TPU:16 before, /device:TPU:32 now
where the time goes in v1:
time: 165 us; the launch traced here: 164 us
  blocking collectives  91.7 us (56%)
  waiting for transfers between devices  34.6 us (21%)
  Pallas kernels  22.2 us (13%)
  starting transfers between devices  9.1 us (6%)
  local copies, waits for them, and re-layouts  5.05 us (3%)
    all_to_all x4, blocking collectives, exchange(): return lax.all_to_all(array, axes, split_axis=0, concat_axis=0, tiled=True)  91.7 us
    all_to_all x2, waiting for transfers between devices, exchange(): return lax.all_to_all(array, axes, split_axis=0, concat_axis=0, tiled=True)  31.6 us
    pallas_call x1, Pallas kernels, attend(): pl.pallas_call(attend_kernel, in_specs=[pl.BlockSpec(memory_space=pltpu.S...  9.28 us
    all_to_all x2, starting transfers between devices, exchange(): return lax.all_to_all(array, axes, split_axis=0, concat_axis=0, tiled=True)  7.17 us
    pallas_call x1, Pallas kernels, project(): pl.pallas_call(project_kernel, grid=(4,), in_specs=[pl.BlockSpec(memory_s...  5.24 us
    pallas_call x1, Pallas kernels, pack(): pl.pallas_call(pack_kernel, grid=(4,), in_specs=[wide] * 4 + [pl.BlockSpe...  4.15 us
    pallas_call x1, Pallas kernels, merge(): pl.pallas_call(merge_kernel, grid=(4,), in_specs=[pl.BlockSpec((2, OUT_RO...  3.5 us
  transfers between devices with their start and end apart: 3, of which 3 were waited for; matrix products, arithmetic and copies ran while one was open for 1% of the time, Pallas kernels for 3%

profile of v1, /device:TPU:32, one launch (start us, length us, event | category | flops | bytes accessed | tf_op | source)
XLA Modules:
  0.0 163.9 jit_solution(9953765584289297851)
XLA Ops:
  0.6 0.7 reshape.41
  1.4 0.6 fusion.2.n_ref
  2.0 0.0 copy-start.4
  2.0 4.1 %pack.1 = (bf16[8,912,128]{2,1,0:T(8,128)(2,1)}, bf16[4,128,768]{2,1,0:T(8,128)(2,1)}) custom-call(bf16[128,1536]{1,0:T(8,128)(2,1)} %bitcast.30, bf16[128,1536]{1,0:T(8,128)(2,1)} %bitcast.31, bf16[128,1536]{1,0:T(8,128)(2,1)} %bitcast.32, bf16[128,1536]{1,0:T(8,128)(2,1)} %bitcast.33, bf16[4,2,16,128]{3,2,1,0:T(8,128)(2,1)} %fusion.2.n_ref, ...), custom_call_target="tpu_custom_call" | custom-call | tf_op jit(solution)/shard_map/pack/pallas_call | solution.py:52
  6.2 16.8 %all_to_all.30.g_ref = bf16[4,128,768]{2,1,0:T(8,128)(2,1)} all-to-all(bf16[4,128,768]{2,1,0:T(8,128)(2,1)} %get-tuple-element.6), channel_id=1, replica_groups=mesh['z'=16,'yh'=2,'core'=2,'x'=4,'yl'=2] {'x'}, dimensions={0} | all-to-all | bytes 1572864 | tf_op jit(solution)/shard_map/all_to_all | solution.py:223
  23.0 0.0 copy-done.4
  23.0 33.4 %all_to_all.31 = bf16[16,24,384]{2,1,0:T(8,128)(2,1)S(1)} all-to-all(bf16[16,24,384]{2,1,0:T(8,128)(2,1)S(1)} %broadcast_in_dim.8), channel_id=1, replica_groups=mesh['z'=16,'yh'=2,'core'=2,'x'=4,'yl'=2] {'z'}, dimensions={0} | all-to-all | bytes 589824 | tf_op jit(solution)/shard_map/all_to_all | solution.py:223
  56.5 0.1 broadcast_in_dim.9
  56.6 18.9 %all_to_all.32 = bf16[4,16,24,384]{3,2,1,0:T(8,128)(2,1)S(1)} all-to-all(bf16[4,16,24,384]{3,2,1,0:T(8,128)(2,1)S(1)} %broadcast_in_dim.9), channel_id=1, replica_groups=mesh['z'=16,'yh'=2,'core'=2,'x'=4,'yl'=2] {'yh','yl'}, dimensions={0} | all-to-all | bytes 2359296 | tf_op jit(solution)/shard_map/all_to_all | solution.py:223
  75.4 0.0 copy-start.2
  75.4 3.6 %all-to-all-start = ((bf16[8,912,128]{2,1,0:T(8,128)(2,1)}), bf16[8,912,128]{2,1,0:T(8,128)(2,1)S(1)}, u32[]{:S(2)}, u32[]{:S(2)}) async-start(bf16[8,912,128]{2,1,0:T(8,128)(2,1)} %get-tuple-element.5), calls=%async_computation | async-start | bytes 3735552 | tf_op jit(solution)/shard_map/all_to_all | solution.py:223
  79.0 0.0 copy-done.2
  79.0 1.9 %collective-permute-start = (bf16[2,2,16,24,384]{4,3,2,1,0:T(8,128)(2,1)S(1)}, bf16[2,2,16,24,384]{4,3,2,1,0:T(8,128)(2,1)}, u32[]{:S(2)}, u32[]{:S(2)}) collective-permute-start(bf16[2,2,16,24,384]{4,3,2,1,0:T(8,128)(2,1)S(1)} %bitcast.27), channel_id=1, source_target_pairs={{0,8},{8,0},{1,9},{9,1},{2,10},{10,2},{3,11},{11,3},{4,12},{12,4},... | collective-permute-start | bytes 3538952 | tf_op jit(solution)/shard_map/ppermute | solution.py:233
  81.0 2.9 %collective-permute-done.other_ref = bf16[2,2,16,24,384]{4,3,2,1,0:T(8,128)(2,1)} collective-permute-done((bf16[2,2,16,24,384]{4,3,2,1,0:T(8,128)(2,1)S(1)}, bf16[2,2,16,24,384]{4,3,2,1,0:T(8,128)(2,1)}, u32[]{:S(2)}, u32[]{:S(2)}) %collective-permute-start) | collective-permute-done | bytes 1179680 | tf_op jit(solution)/shard_map/ppermute | solution.py:233
  83.9 5.2 %project.1 = bf16[8,768,128]{2,1,0:T(8,128)(2,1)} custom-call(s32[1]{0:T(128)} %bitcast.9.core_ref, bf16[2,2,16,24,384]{4,3,2,1,0:T(8,128)(2,1)} %bitcast.28, bf16[2,2,16,24,384]{4,3,2,1,0:T(8,128)(2,1)} %collective-permute-done.other_ref, bf16[4,128,768]{2,1,0:T(8,128)(2,1)} %all_to_all.30.g_ref), custom_call_target="tpu_custom_call" | custom-call | tf_op jit(solution)/shard_map/project/pallas_call | solution.py:92
  89.2 0.0 copy-start.3
  89.2 13.0 %all-to-all-done.in_ref = bf16[8,912,128]{2,1,0:T(8,128)(2,1)S(1)} async-done(((bf16[8,912,128]{2,1,0:T(8,128)(2,1)}), bf16[8,912,128]{2,1,0:T(8,128)(2,1)S(1)}, u32[]{:S(2)}, u32[]{:S(2)}) %all-to-all-start) | async-done | bytes 1867808 | tf_op jit(solution)/shard_map/all_to_all | solution.py:223
  102.1 0.0 copy-start
  102.1 1.3 copy-done
  103.4 3.6 %all-to-all-start.4 = ((bf16[8,768,128]{2,1,0:T(8,128)(2,1)}), bf16[8,768,128]{2,1,0:T(8,128)(2,1)S(1)}, u32[]{:S(2)}, u32[]{:S(2)}) async-start(bf16[8,768,128]{2,1,0:T(8,128)(2,1)} %project.1), calls=%async_computation.4 | async-start | bytes 3145728 | tf_op jit(solution)/shard_map/all_to_all | solution.py:223
  107.0 0.0 copy-done.3
  107.1 0.1 copy.13
  107.1 0.1 broadcast_in_dim.20
  107.2 0.7 reshape.45.mask_a_ref
  108.0 0.1 copy.14
  108.0 0.1 broadcast_in_dim.21
  108.1 0.7 reshape.48.mask_c_ref
  108.8 18.6 %all-to-all-done.4.mid_ref = bf16[8,768,128]{2,1,0:T(8,128)(2,1)S(1)} async-done(((bf16[8,768,128]{2,1,0:T(8,128)(2,1)}), bf16[8,768,128]{2,1,0:T(8,128)(2,1)S(1)}, u32[]{:S(2)}, u32[]{:S(2)}) %all-to-all-start.4) | async-done | bytes 1572896 | tf_op jit(solution)/shard_map/all_to_all | solution.py:223
  127.5 1.1 copy-done.1
  128.6 9.3 %attend.1 = bf16[8,704,128]{2,1,0:T(8,128)(2,1)} custom-call(s32[1]{0:T(128)} %bitcast.y_ref, bf16[8,912,128]{2,1,0:T(8,128)(2,1)} %copy-done, bf16[8,768,128]{2,1,0:T(8,128)(2,1)} %copy-done.1, f32[16,1024]{1,0:T(8,128)} %reshape.45.mask_a_ref, f32[16,512]{1,0:T(8,128)} %reshape.48.mask_c_ref), custom_call_target="tpu_custom_call" | custom-call | tf_op jit(solution)/shard_map/attend/pallas_call | solution.py:187
  137.9 22.5 %all_to_all.33.in_ref = bf16[8,704,128]{2,1,0:T(8,128)(2,1)} all-to-all(bf16[8,704,128]{2,1,0:T(8,128)(2,1)} %attend.1), channel_id=1, replica_groups=mesh['z'=16,'yh'=2,'core'=2,'x'=4,'yl'=2] {'x','yl'}, dimensions={0} | all-to-all | bytes 2883584 | tf_op jit(solution)/shard_map/all_to_all | solution.py:223
  160.4 3.5 %merge.1 = (bf16[1,128,1536]{2,1,0:T(8,128)(2,1)}, bf16[1,128,1536]{2,1,0:T(8,128)(2,1)}, bf16[1,128,1536]{2,1,0:T(8,128)(2,1)}) custom-call(bf16[8,704,128]{2,1,0:T(8,128)(2,1)} %all_to_all.33.in_ref), custom_call_target="tpu_custom_call" | custom-call | tf_op jit(solution)/shard_map/merge/pallas_call | solution.py:212
  (10 shorter events, 0.1 us)
Async XLA Ops:
  2.0 21.0 %copy-start.4 = (bf16[24,384]{1,0:T(8,128)(2,1)S(1)}, bf16[24,384]{1,0:T(8,128)(2,1)}, u32[]{:S(2)}) copy-start(bf16[24,384]{1,0:T(8,128)(2,1)} %param.14) | copy-start | bytes 55300
  75.4 3.6 %copy-start.2 = (bf16[4,16,24,384]{3,2,1,0:T(8,128)(2,1)}, bf16[4,16,24,384]{3,2,1,0:T(8,128)(2,1)S(1)}, u32[]{:S(2)}) copy-start(bf16[4,16,24,384]{3,2,1,0:T(8,128)(2,1)S(1)} %all_to_all.32) | copy-start | bytes 3538948
  75.4 26.7 %all-to-all-start = ((bf16[8,912,128]{2,1,0:T(8,128)(2,1)}), bf16[8,912,128]{2,1,0:T(8,128)(2,1)S(1)}, u32[]{:S(2)}, u32[]{:S(2)}) async-start(bf16[8,912,128]{2,1,0:T(8,128)(2,1)} %get-tuple-element.5), calls=%async_computation | async-start | bytes 3735552 | tf_op jit(solution)/shard_map/all_to_all | solution.py:223
  79.0 4.9 %collective-permute-start = (bf16[2,2,16,24,384]{4,3,2,1,0:T(8,128)(2,1)S(1)}, bf16[2,2,16,24,384]{4,3,2,1,0:T(8,128)(2,1)}, u32[]{:S(2)}, u32[]{:S(2)}) collective-permute-start(bf16[2,2,16,24,384]{4,3,2,1,0:T(8,128)(2,1)S(1)} %bitcast.27), channel_id=1, source_target_pairs={{0,8},{8,0},{1,9},{9,1},{2,10},{10,2},{3,11},{11,3},{4,12},{12,4},... | collective-permute-start | bytes 3538952 | tf_op jit(solution)/shard_map/ppermute | solution.py:233
  89.2 17.8 %copy-start.3 = (s32[1,12,16,16]{3,2,1,0:T(8,128)S(1)}, s32[1,12,16,16]{3,2,1,0:T(8,128)}, u32[]{:S(2)}) copy-start(s32[1,12,16,16]{3,2,1,0:T(8,128)} %param.15) | copy-start | bytes 36868
  102.1 1.3 copy-start
  103.4 24.1 %all-to-all-start.4 = ((bf16[8,768,128]{2,1,0:T(8,128)(2,1)}), bf16[8,768,128]{2,1,0:T(8,128)(2,1)S(1)}, u32[]{:S(2)}, u32[]{:S(2)}) async-start(bf16[8,768,128]{2,1,0:T(8,128)(2,1)} %project.1), calls=%async_computation.4 | async-start | bytes 3145728 | tf_op jit(solution)/shard_map/all_to_all | solution.py:223
  127.5 1.1 copy-start.1

commit v2 on v1

--- a/solution.py
+++ b/solution.py
@@ -1,4 +1,3 @@
-import functools
 import math
 
 import jax
@@ -8,6 +7,7 @@
 from jax.experimental.pallas import tpu as pltpu
 from jax.sharding import Mesh, PartitionSpec as P
 
+
 BF = jnp.bfloat16
 F32 = jnp.float32
 HD = 128
@@ -17,6 +17,8 @@
 
 QA, KA, VA, OA, KC, VC, QC, OC, NR = 0, 128, 256, 384, 512, 640, 768, 832, 896
 IN_ROWS = 912
+SLAB = 768
+GRANT = 16 << 20
 MID = 192
 GQA, GKA, GVA, GKC, GVC, GQC = 0, 128, 256, 384, 512, 640
 OUT_ROWS = 704
@@ -30,44 +32,52 @@
     return lax.dot_general(a, b, dims, preferred_element_type=F32)
 
 
-def pack_kernel(q_ref, k_ref, v_ref, o_ref, n_ref, g_ref, in_ref, slab_ref):
-    slab_ref[0] = g_ref[...]
-    for j in range(2):
-        own = slice(HD * j, HD * (j + 1))
-        shared = slice(2 * HD, 3 * HD)
-        half = slice(TILE * j, TILE * (j + 1))
-        in_ref[j, QA : QA + 128] = q_ref[:, own]
-        in_ref[j, KA : KA + 128] = k_ref[:, own]
-        in_ref[j, VA : VA + 128] = v_ref[:, own]
-        in_ref[j, OA : OA + 128] = o_ref[:, own]
-        in_ref[j, KC : KC + 128] = k_ref[:, shared]
-        in_ref[j, VC : VC + 128] = v_ref[:, shared]
-        in_ref[j, QC : QC + 64] = q_ref[half, shared]
-        in_ref[j, OC : OC + 64] = o_ref[half, shared]
-        in_ref[j, NR:IN_ROWS] = n_ref[0, j]
-
-
-def pack(q, k, v, o, norm_rows, out_grad):
-    wide = pl.BlockSpec((128, 3 * HD), lambda i: (0, i))
+def pack_kernel(me_ref, q_ref, k_ref, v_ref, o_ref, n_ref, g_ref, *out_refs):
+    for d, out_ref in enumerate(out_refs):
+        to = jnp.bitwise_xor(me_ref[0], d)
+        x, y = to // 2, to % 2
+        base = 0 if d % 2 else SLAB
+        own = pl.ds(pl.multiple_of(HD * (3 * x + y), HD), HD)
+        shared = pl.ds(pl.multiple_of(HD * (3 * x + 2), HD), HD)
+        half = pl.ds(pl.multiple_of(TILE * y, TILE), TILE)
+        if base:
+            for e in range(6):
+                columns = pl.ds(pl.multiple_of(768 * x + 128 * e, 128), 128)
+                out_ref[128 * e : 128 * (e + 1)] = g_ref[:, columns]
+        for ref, at in ((q_ref, QA), (k_ref, KA), (v_ref, VA), (o_ref, OA)):
+            out_ref[base + at : base + at + 128] = ref[:, own]
+        for ref, at in ((k_ref, KC), (v_ref, VC)):
+            out_ref[base + at : base + at + 128] = ref[:, shared]
+        for ref, at in ((q_ref, QC), (o_ref, OC)):
+            out_ref[base + at : base + at + 64] = ref[half, shared]
+        line = lax.broadcasted_iota(jnp.int32, (16, 12), 0)
+        head = lax.broadcasted_iota(jnp.int32, (16, 12), 1)
+        wanted = jnp.where(line == 0, 3 * x + y, 3 * x + 2)
+        pick = jnp.where((head == wanted) & (line < 2), 1.0, 0.0).astype(BF)
+        out_ref[base + NR : base + IN_ROWS] = dot(pick, n_ref[...], NN_DIMS).astype(BF)
+
+
+def pack(me, q, k, v, o, norms, out_grad):
+    whole = pl.BlockSpec(memory_space=pltpu.VMEM)
     return pl.pallas_call(
         pack_kernel,
-        grid=(4,),
-        in_specs=[wide] * 4
-        + [pl.BlockSpec((1, 2, 16, 128), lambda i: (i, 0, 0, 0)), pl.BlockSpec((128, 768), lambda i: (0, i))],
-        out_specs=(
-            pl.BlockSpec((2, IN_ROWS, 128), lambda i: (i, 0, 0)),
-            pl.BlockSpec((1, 128, 768), lambda i: (i, 0, 0)),
-        ),
-        out_shape=(
-            jax.ShapeDtypeStruct((8, IN_ROWS, 128), BF),
-            jax.ShapeDtypeStruct((4, 128, 768), BF),
-        ),
+        in_specs=[pl.BlockSpec(memory_space=pltpu.SMEM)] + [whole] * 6,
+        out_specs=(whole,) * 8,
+        out_shape=tuple(jax.ShapeDtypeStruct((IN_ROWS + (0 if d % 2 else SLAB), 128), BF) for d in range(8)),
+        compiler_params=pltpu.CompilerParams(vmem_limit_bytes=GRANT),
         name="pack",
-    )(q, k, v, o, norm_rows, out_grad)
-
-
-def project_kernel(core_ref, own_ref, other_ref, g_ref, out_ref, w_ref):
-    mine = core_ref[0] == 0
+    )(me, q, k, v, o, norms, out_grad)
+
+
+def project_kernel(where_ref, own_ref, other_ref, g0_ref, g1_ref, g2_ref, g3_ref, out_ref, w_ref, g_ref):
+    @pl.when(pl.program_id(0) == 0)
+    def _():
+        for e, ref in enumerate((g0_ref, g1_ref, g2_ref, g3_ref)):
+            source = jnp.bitwise_xor(where_ref[1], e)
+            for n in range(6):
+                g_ref[source, :, 128 * n : 128 * (n + 1)] = ref[128 * n : 128 * (n + 1)]
+
+    mine = where_ref[0] == 0
     for z in range(4):
         for yh in range(2):
             for yl in range(2):
@@ -87,22 +97,19 @@
             out_ref[j, base + 128 : base + MID] = part[128 * x + 64 * j : 128 * x + 64 * (j + 1), 2 * HD :]
 
 
-def project(core, own, other, slab):
+def project(where, own, other, slabs):
     shard = pl.BlockSpec((2, 2, 4, 24, 384), lambda i: (0, 0, i, 0, 0))
+    slab = pl.BlockSpec((SLAB, 128), lambda i: (0, 0))
     return pl.pallas_call(
         project_kernel,
         grid=(4,),
-        in_specs=[
-            pl.BlockSpec(memory_space=pltpu.SMEM),
-            shard,
-            shard,
-            pl.BlockSpec((4, 128, 768), lambda i: (0, 0, 0)),
-        ],
+        in_specs=[pl.BlockSpec(memory_space=pltpu.SMEM), shard, shard] + [slab] * 4,
         out_specs=pl.BlockSpec((2, 4 * MID, 128), lambda i: (i, 0, 0)),
         out_shape=jax.ShapeDtypeStruct((8, 4 * MID, 128), BF),
-        scratch_shapes=[pltpu.VMEM((384, 768), BF)],
+        scratch_shapes=[pltpu.VMEM((384, 768), BF), pltpu.VMEM((4, 128, 768), BF)],
+        compiler_params=pltpu.CompilerParams(vmem_limit_bytes=GRANT),
         name="project",
-    )(core, own, other, slab)
+    )(where, own, other, *slabs)
 
 
 def attend_unit(in_ref, mid_ref, mask_ref, out_ref, dk_ref, dv_ref, per, rows, norm_row, outs):
@@ -160,8 +167,17 @@
         out_ref[s, gv0 : gv0 + 128] = dv_ref[at].astype(BF)
 
 
-def attend_kernel(y_ref, in_ref, mid_ref, mask_a_ref, mask_c_ref, out_ref, dk_ref, dv_ref):
-    second = y_ref[0] == 1
+def attend_kernel(me_ref, *refs):
+    sent_refs = refs[:8]
+    mid_ref, mask_a_ref, mask_c_ref, out_ref, in_ref, dk_ref, dv_ref, sems = refs[8:]
+    copies = []
+    for d, ref in enumerate(sent_refs):
+        source = ref if d % 2 else ref.at[pl.ds(SLAB, IN_ROWS)]
+        copies.append(pltpu.make_async_copy(source, in_ref.at[jnp.bitwise_xor(me_ref[0], d)], sems.at[d]))
+        copies[-1].start()
+    for copy in copies:
+        copy.wait()
+    second = me_ref[0] % 2 == 1
 
     def norm_a(b):
         parts = [in_ref[s, NR : NR + 16].astype(F32)[0:1] for s in (2 * b, 2 * b + 1)]
@@ -182,16 +198,24 @@
     )
 
 
-def attend(y_index, arrived, partial, mask_a, mask_c):
+def attend(me, arrived, partial, mask_a, mask_c):
     whole = pl.BlockSpec(memory_space=pltpu.VMEM)
     return pl.pallas_call(
         attend_kernel,
-        in_specs=[pl.BlockSpec(memory_space=pltpu.SMEM), whole, whole, whole, whole],
+        in_specs=[pl.BlockSpec(memory_space=pltpu.SMEM)]
+        + [pl.BlockSpec(memory_space=pl.ANY)] * 8
+        + [whole, whole, whole],
         out_specs=whole,
         out_shape=jax.ShapeDtypeStruct((8, OUT_ROWS, 128), BF),
-        scratch_shapes=[pltpu.VMEM((1024, 128), F32), pltpu.VMEM((1024, 128), F32)],
+        scratch_shapes=[
+            pltpu.VMEM((8, IN_ROWS, 128), BF),
+            pltpu.VMEM((1024, 128), F32),
+            pltpu.VMEM((1024, 128), F32),
+            pltpu.SemaphoreType.DMA((8,)),
+        ],
+        compiler_params=pltpu.CompilerParams(vmem_limit_bytes=GRANT),
         name="attend",
-    )(y_index, arrived, partial, mask_a, mask_c)
+    )(me, *arrived, partial, mask_a, mask_c)
 
 
 def merge_kernel(in_ref, gq_ref, gk_ref, gv_ref):
@@ -215,6 +239,7 @@
         in_specs=[pl.BlockSpec((2, OUT_ROWS, 128), lambda i: (i, 0, 0))],
         out_specs=(out, out, out),
         out_shape=(shape, shape, shape),
+        compiler_params=pltpu.CompilerParams(vmem_limit_bytes=GRANT),
         name="merge",
     )(arrived)
 
@@ -234,37 +259,57 @@
     return own, other
 
 
-def mask_rows(tile_mask):
+def mask_kernel(where_ref, table_ref, whole_ref, shared_ref):
+    x, y = where_ref[0] // 2, where_ref[0] % 2
+    for ref, head in ((whole_ref, 3 * x + y), (shared_ref, 3 * x + 2)):
+        tile = lax.broadcasted_iota(jnp.int32, (16, ref.shape[1]), 0)
+        group = lax.broadcasted_iota(jnp.int32, (16, ref.shape[1]), 1) // TILE
+        of_lane = group if ref is whole_ref else 2 * group + y
+        spread_out = jnp.where(tile == of_lane, 1.0, 0.0)
+        ref[...] = dot(table_ref[0, head].astype(F32), spread_out, TN_DIMS)
+
+
+def mask_rows(me, tile_mask):
+    whole = pl.BlockSpec(memory_space=pltpu.VMEM)
+    return pl.pallas_call(
+        mask_kernel,
+        in_specs=[pl.BlockSpec(memory_space=pltpu.SMEM), whole],
+        out_specs=(whole, whole),
+        out_shape=(jax.ShapeDtypeStruct((16, 1024), F32), jax.ShapeDtypeStruct((16, 512), F32)),
+        compiler_params=pltpu.CompilerParams(vmem_limit_bytes=GRANT),
+        name="mask",
+    )(me, tile_mask)
+
+
+def swap(array, d):
+    return lax.ppermute(array, ("x", "yl"), [(s, s ^ d) for s in range(8)])
+
+
+def after_weight(q, k, v, o, log_norm, out_grad, own, other, core, tile_mask):
     x, y = lax.axis_index("x"), lax.axis_index("yl")
-    table = tile_mask[0].astype(F32).transpose(0, 2, 1)
-    whole = lax.dynamic_index_in_dim(table, 3 * x + y, 0, keepdims=False)
-    shared = lax.dynamic_index_in_dim(table, 3 * x + 2, 0, keepdims=False).reshape(16, 8, 2)
-    shared = lax.dynamic_index_in_dim(shared, y, 2, keepdims=False)
-    return jnp.repeat(whole, TILE, axis=1), jnp.repeat(shared, TILE, axis=1)
-
-
-def norm_table(log_norm):
-    rows = log_norm[0].T.reshape(4, 3, 128)
-    both = jnp.stack([rows[:, :2], jnp.broadcast_to(rows[:, 2:], (4, 2, 128))], axis=2)
-    return jnp.pad(both, ((0, 0), (0, 0), (0, 14), (0, 0)))
-
-
-def after_weight(q, k, v, o, log_norm, out_grad, own, other, core, tile_mask):
-    sent, slab = pack(q[0], k[0], v[0], o[0], norm_table(log_norm), out_grad[0])
-    slab = exchange(slab, "x")
-    arrived = exchange(sent, ("x", "yl"))
-    partial = exchange(project(core, own, other, slab), ("x", "yl"))
-    mask_a, mask_c = mask_rows(tile_mask)
-    y_index = lax.axis_index("yl").reshape(1)
-    result = exchange(attend(y_index, arrived, partial, mask_a, mask_c), ("x", "yl"))
+    me = (2 * x + y).reshape(1)
+    where = jnp.stack([core, x])
+    sent = pack(me, q[0], k[0], v[0], o[0], log_norm[0].T, out_grad[0])
+    arrived = [sent[d] if d == 0 else swap(sent[d], d) for d in range(8)]
+    partial = exchange(project(where, own, other, arrived[::2]), ("x", "yl"))
+    mask_a, mask_c = mask_rows(me, tile_mask)
+    result = exchange(attend(me, arrived, partial, mask_a, mask_c), ("x", "yl"))
     return merge(result)
 
 
 def local(queries, key_states, value_states, attn_out, log_norm, out_grad, proj_weight, tile_mask):
     own, other = gather_weight(proj_weight)
-    core = lax.axis_index("core").reshape(1)
     return after_weight(
-        queries, key_states, value_states, attn_out, log_norm, out_grad, own, other, core, tile_mask
+        queries,
+        key_states,
+        value_states,
+        attn_out,
+        log_norm,
+        out_grad,
+        own,
+        other,
+        lax.axis_index("core"),
+        tile_mask,
     )
 
 

time: 165 us -> 183 us (1.11)
  starting transfers between devices: 9.1 us -> 30.6 us
  blocking collectives: 91.7 us -> 78.1 us
  waiting for transfers between devices: 34.6 us -> 43.4 us
  local copies, waits for them, and re-layouts: 5.05 us -> 11.5 us
  Pallas kernels: 22.2 us -> 17.1 us
    ppermute x0 -> x7, waiting for transfers between devices: none -> 43.4 us  [swap(): return lax.ppermute(array, ('x', 'yl'), [(s, s ^ d) for s in range(8)])]
    all_to_all x2 -> x1, waiting for transfers between devices: 31.6 us -> 0.01 us  [exchange(): return lax.all_to_all(array, axes, split_axis=0, concat_axis=0, tiled=True)]
    ppermute x0 -> x7, starting transfers between devices: none -> 25.1 us  [swap(): return lax.ppermute(array, ('x', 'yl'), [(s, s ^ d) for s in range(8)])]
    all_to_all x4 -> x3, blocking collectives: 91.7 us -> 78.1 us  [exchange(): return lax.all_to_all(array, axes, split_axis=0, concat_axis=0, tiled=True)]
    unnamed x11 -> x42, local copies, waits for them, and re-layouts: 2.43 us -> 10.6 us
    all_to_all x2 -> x1, starting transfers between devices: 7.17 us -> 3.58 us  [exchange(): return lax.all_to_all(array, axes, split_axis=0, concat_axis=0, tiled=True)]
    ppermute x1, waiting for transfers between devices: 2.94 us -> 0.01 us  [gather_weight(): other = lax.ppermute(own, 'core', [(0, 1), (1, 0)])]
    pallas_call x1 -> x2, Pallas kernels: 4.15 us -> 1.82 us  [the longest x1 1.63 us: pack(): pl.pallas_call(pack_kernel, in_specs=[pl.BlockSpec(memory_space=pltpu.SME...]
  transfers between devices with their start and end apart: 3 -> 9, of which waited for: 3 -> 4; matrix products, arithmetic and copies ran while one was open for 1% -> 0% of each run, Pallas kernels for 3% -> 1%
where the time goes in v2:
time: 183 us; the launch traced here: 182 us
  blocking collectives  78.1 us (43%)
  waiting for transfers between devices  43.4 us (24%)
  starting transfers between devices  30.6 us (17%)
  Pallas kernels  17.1 us (9%)
  local copies, waits for them, and re-layouts  11.5 us (6%)
    all_to_all x3, blocking collectives, exchange(): return lax.all_to_all(array, axes, split_axis=0, concat_axis=0, tiled=True)  78.1 us
    ppermute x7, waiting for transfers between devices, swap(): return lax.ppermute(array, ('x', 'yl'), [(s, s ^ d) for s in range(8)])  43.4 us
    ppermute x7, starting transfers between devices, swap(): return lax.ppermute(array, ('x', 'yl'), [(s, s ^ d) for s in range(8)])  25.1 us
    unnamed x42, local copies, waits for them, and re-layouts  10.6 us
    pallas_call x1, Pallas kernels, attend(): pl.pallas_call(attend_kernel, in_specs=[pl.BlockSpec(memory_space=pltpu.S...  8.65 us
    pallas_call x1, Pallas kernels, project(): pl.pallas_call(project_kernel, grid=(4,), in_specs=[pl.BlockSpec(memory_s...  5.03 us
  transfers between devices with their start and end apart: 9, of which 4 were waited for; matrix products, arithmetic and copies ran while one was open for 0% of the time, Pallas kernels for 1%

profile of v2, /device:TPU:32, one launch (start us, length us, event | category | flops | bytes accessed | tf_op | source)
XLA Modules:
  0.0 181.7 jit_solution(7658646009914485803)
XLA Ops:
  0.6 0.7 broadcast_in_dim.4
  1.4 33.8 %all_to_all.20 = bf16[16,24,384]{2,1,0:T(8,128)(2,1)S(1)} all-to-all(bf16[16,24,384]{2,1,0:T(8,128)(2,1)S(1)} %broadcast_in_dim.4), channel_id=1, replica_groups=mesh['z'=16,'yh'=2,'core'=2,'x'=4,'yl'=2] {'z'}, dimensions={0} | all-to-all | bytes 589824 | tf_op jit(solution)/shard_map/all_to_all | solution.py:248
  35.3 20.2 %all_to_all.21 = bf16[4,16,24,384]{3,2,1,0:T(8,128)(2,1)S(1)} all-to-all(bf16[4,16,24,384]{3,2,1,0:T(8,128)(2,1)S(1)} %broadcast_in_dim.5), channel_id=1, replica_groups=mesh['z'=16,'yh'=2,'core'=2,'x'=4,'yl'=2] {'yh','yl'}, dimensions={0} | all-to-all | bytes 2359296 | tf_op jit(solution)/shard_map/all_to_all | solution.py:248
  55.6 1.9 %collective-permute-start.7 = (bf16[2,2,16,24,384]{4,3,2,1,0:T(8,128)(2,1)S(1)}, bf16[2,2,16,24,384]{4,3,2,1,0:T(8,128)(2,1)}, u32[]{:S(2)}, u32[]{:S(2)}) collective-permute-start(bf16[2,2,16,24,384]{4,3,2,1,0:T(8,128)(2,1)S(1)} %bitcast.12), channel_id=1, source_target_pairs={{0,8},{8,0},{1,9},{9,1},{2,10},{10,2},{3,11},{11,3},{4,12},{12,4},... | collective-permute-start | bytes 3538952 | tf_op jit(solution)/shard_map/ppermute | solution.py:258
  57.5 1.0 copy-done.3
  58.5 1.0 copy-done.4
  59.5 1.6 pack.1
  61.2 3.4 %collective-permute-start.1 = (bf16[1680,128]{1,0:T(8,128)(2,1)}, bf16[1680,128]{1,0:T(8,128)(2,1)S(1)}, u32[]{:S(2)}, u32[]{:S(2)}) collective-permute-start(bf16[1680,128]{1,0:T(8,128)(2,1)} %get-tuple-element.15), channel_id=1, source_target_pairs={{0,2},{1,3},{2,0},{3,1},{4,6},{5,7},{6,4},{7,5},{8,10},{9,11},{10,... | collective-permute-start | bytes 1290248 | tf_op jit(solution)/shard_map/ppermute | solution.py:285
  64.6 4.6 %collective-permute-start.3 = (bf16[1680,128]{1,0:T(8,128)(2,1)}, bf16[1680,128]{1,0:T(8,128)(2,1)S(1)}, u32[]{:S(2)}, u32[]{:S(2)}) collective-permute-start(bf16[1680,128]{1,0:T(8,128)(2,1)} %get-tuple-element.17), channel_id=1, source_target_pairs={{0,4},{1,5},{2,6},{3,7},{4,0},{5,1},{6,2},{7,3},{8,12},{9,13},{10,... | collective-permute-start | bytes 1290248 | tf_op jit(solution)/shard_map/ppermute | solution.py:285
  69.3 2.4 %collective-permute-start.5 = (bf16[1680,128]{1,0:T(8,128)(2,1)}, bf16[1680,128]{1,0:T(8,128)(2,1)S(1)}, u32[]{:S(2)}, u32[]{:S(2)}) collective-permute-start(bf16[1680,128]{1,0:T(8,128)(2,1)} %get-tuple-element.19), channel_id=1, source_target_pairs={{0,6},{1,7},{2,4},{3,5},{4,2},{5,3},{6,0},{7,1},{8,14},{9,15},{10,... | collective-permute-start | bytes 1290248 | tf_op jit(solution)/shard_map/ppermute | solution.py:285
  71.7 4.3 %collective-permute-done.1.g1_ref.refs_2_ = bf16[1680,128]{1,0:T(8,128)(2,1)S(1)} collective-permute-done((bf16[1680,128]{1,0:T(8,128)(2,1)}, bf16[1680,128]{1,0:T(8,128)(2,1)S(1)}, u32[]{:S(2)}, u32[]{:S(2)}) %collective-permute-start.1) | collective-permute-done | bytes 430112 | tf_op jit(solution)/shard_map/ppermute | solution.py:285
  76.1 11.0 %collective-permute-done.3.g2_ref.refs_4_ = bf16[1680,128]{1,0:T(8,128)(2,1)S(1)} collective-permute-done((bf16[1680,128]{1,0:T(8,128)(2,1)}, bf16[1680,128]{1,0:T(8,128)(2,1)S(1)}, u32[]{:S(2)}, u32[]{:S(2)}) %collective-permute-start.3) | collective-permute-done | bytes 430112 | tf_op jit(solution)/shard_map/ppermute | solution.py:285
  87.1 6.4 %collective-permute-done.5.g3_ref.refs_6_ = bf16[1680,128]{1,0:T(8,128)(2,1)S(1)} collective-permute-done((bf16[1680,128]{1,0:T(8,128)(2,1)}, bf16[1680,128]{1,0:T(8,128)(2,1)S(1)}, u32[]{:S(2)}, u32[]{:S(2)}) %collective-permute-start.5) | collective-permute-done | bytes 430112 | tf_op jit(solution)/shard_map/ppermute | solution.py:285
  93.5 5.0 %project.1 = bf16[8,768,128]{2,1,0:T(8,128)(2,1)} custom-call(s32[2]{0:T(128)S(1)} %pad_add_fusion.where_ref, bf16[2,2,16,24,384]{4,3,2,1,0:T(8,128)(2,1)S(1)} %bitcast.13, bf16[2,2,16,24,384]{4,3,2,1,0:T(8,128)(2,1)} %collective-permute-done.7.other_ref, bf16[1680,128]{1,0:T(8,128)(2,1)S(1)} %get-tuple-element.13.g0_ref.refs_0_, ...), custom_call_target="tpu_custom_call" | custom-call | tf_op jit(solution)/shard_map/project/pallas_call | solution.py:103
  98.6 3.6 %all-to-all-start.2 = ((bf16[8,768,128]{2,1,0:T(8,128)(2,1)}), bf16[8,768,128]{2,1,0:T(8,128)(2,1)S(1)}, u32[]{:S(2)}, u32[]{:S(2)}) async-start(bf16[8,768,128]{2,1,0:T(8,128)(2,1)} %project.1), calls=%async_computation.2 | async-start | bytes 3145728 | tf_op jit(solution)/shard_map/all_to_all | solution.py:248
  102.2 3.8 %collective-permute-start = (bf16[912,128]{1,0:T(8,128)(2,1)}, bf16[912,128]{1,0:T(8,128)(2,1)S(1)}, u32[]{:S(2)}, u32[]{:S(2)}) collective-permute-start(bf16[912,128]{1,0:T(8,128)(2,1)} %copy-done.20), channel_id=1, source_target_pairs={{0,1},{1,0},{2,3},{3,2},{4,5},{5,4},{6,7},{7,6},{8,9},{9,8},{10,11... | collective-permute-start | bytes 700424 | tf_op jit(solution)/shard_map/ppermute | solution.py:285
  106.0 3.4 %collective-permute-start.2 = (bf16[912,128]{1,0:T(8,128)(2,1)}, bf16[912,128]{1,0:T(8,128)(2,1)S(1)}, u32[]{:S(2)}, u32[]{:S(2)}) collective-permute-start(bf16[912,128]{1,0:T(8,128)(2,1)} %copy-done.19), channel_id=1, source_target_pairs={{0,3},{1,2},{2,1},{3,0},{4,7},{5,6},{6,5},{7,4},{8,11},{9,10},{10,... | collective-permute-start | bytes 700424 | tf_op jit(solution)/shard_map/ppermute | solution.py:285
  109.4 5.5 %collective-permute-start.4 = (bf16[912,128]{1,0:T(8,128)(2,1)}, bf16[912,128]{1,0:T(8,128)(2,1)S(1)}, u32[]{:S(2)}, u32[]{:S(2)}) collective-permute-start(bf16[912,128]{1,0:T(8,128)(2,1)} %copy-done.18), channel_id=1, source_target_pairs={{0,5},{1,4},{2,7},{3,6},{4,1},{5,0},{6,3},{7,2},{8,13},{9,12},{10,... | collective-permute-start | bytes 700424 | tf_op jit(solution)/shard_map/ppermute | solution.py:285
  114.9 2.0 %collective-permute-start.6 = (bf16[912,128]{1,0:T(8,128)(2,1)}, bf16[912,128]{1,0:T(8,128)(2,1)S(1)}, u32[]{:S(2)}, u32[]{:S(2)}) collective-permute-start(bf16[912,128]{1,0:T(8,128)(2,1)} %copy-done.17), channel_id=1, source_target_pairs={{0,7},{1,6},{2,5},{3,4},{4,3},{5,2},{6,1},{7,0},{8,15},{9,14},{10,... | collective-permute-start | bytes 700424 | tf_op jit(solution)/shard_map/ppermute | solution.py:285
  116.9 0.9 copy-done.11
  119.2 21.6 %collective-permute-done.refs_1_ = bf16[912,128]{1,0:T(8,128)(2,1)S(1)} collective-permute-done((bf16[912,128]{1,0:T(8,128)(2,1)}, bf16[912,128]{1,0:T(8,128)(2,1)S(1)}, u32[]{:S(2)}, u32[]{:S(2)}) %collective-permute-start) | collective-permute-done | bytes 233504 | tf_op jit(solution)/shard_map/ppermute | solution.py:285
  140.8 0.7 copy-done.5
  141.5 0.7 copy-done.7
  142.2 0.7 copy-done.9
  142.9 0.9 copy-done.6
  143.8 0.9 copy-done.8
  144.8 0.9 copy-done.10
  145.7 0.8 copy-done.13
  146.6 0.8 copy-done.15
  147.3 8.6 %attend.1 = bf16[8,704,128]{2,1,0:T(8,128)(2,1)S(1)} custom-call(s32[1]{0:T(128)} %bitcast.me_ref.where_ref, bf16[1680,128]{1,0:T(8,128)(2,1)S(1)} %get-tuple-element.13.g0_ref.refs_0_, bf16[912,128]{1,0:T(8,128)(2,1)S(1)} %collective-permute-done.refs_1_, bf16[1680,128]{1,0:T(8,128)(2,1)S(1)} %collective-permute-done.1.g1_ref.refs_2_, ...), custom_call_target="tpu_custom_call" | custom-call | tf_op jit(solution)/shard_map/attend/pallas_call | solution.py:203
  156.0 24.1 %all_to_all.22.in_ref = bf16[8,704,128]{2,1,0:T(8,128)(2,1)S(1)} all-to-all(bf16[8,704,128]{2,1,0:T(8,128)(2,1)S(1)} %attend.1), channel_id=1, replica_groups=mesh['z'=16,'yh'=2,'core'=2,'x'=4,'yl'=2] {'x','yl'}, dimensions={0} | all-to-all | bytes 2883584 | tf_op jit(solution)/shard_map/all_to_all | solution.py:248
  180.1 1.6 merge.1
  (39 shorter events, 1.7 us)
Async XLA Ops:
  35.3 22.2 %copy-start = (bf16[1,128,3072]{2,1,0:T(8,128)(2,1)S(1)}, bf16[1,128,3072]{2,1,0:T(8,128)(2,1)}, u32[]{:S(2)}) copy-start(bf16[1,128,3072]{2,1,0:T(8,128)(2,1)} %param.13) | copy-start | bytes 2359300
  35.3 22.2 %copy-start.1 = (bf16[1,128,1536]{2,1,0:T(8,128)(2,1)S(1)}, bf16[1,128,1536]{2,1,0:T(8,128)(2,1)}, u32[]{:S(2)}) copy-start(bf16[1,128,1536]{2,1,0:T(8,128)(2,1)} %param.8) | copy-start | bytes 1179652
  35.3 22.2 %copy-start.2 = (bf16[1,128,1536]{2,1,0:T(8,128)(2,1)S(1)}, bf16[1,128,1536]{2,1,0:T(8,128)(2,1)}, u32[]{:S(2)}) copy-start(bf16[1,128,1536]{2,1,0:T(8,128)(2,1)} %param.9) | copy-start | bytes 1179652
  35.3 22.2 %copy-start.16 = (bf16[1,128,12]{1,2,0:T(8,128)(2,1)S(1)}, bf16[1,128,12]{1,2,0:T(8,128)(2,1)}, u32[]{:S(2)}) copy-start(bf16[1,128,12]{1,2,0:T(8,128)(2,1)} %param.12) | copy-start | bytes 9220
  55.6 38.0 %collective-permute-start.7 = (bf16[2,2,16,24,384]{4,3,2,1,0:T(8,128)(2,1)S(1)}, bf16[2,2,16,24,384]{4,3,2,1,0:T(8,128)(2,1)}, u32[]{:S(2)}, u32[]{:S(2)}) collective-permute-start(bf16[2,2,16,24,384]{4,3,2,1,0:T(8,128)(2,1)S(1)} %bitcast.12), channel_id=1, source_target_pairs={{0,8},{8,0},{1,9},{9,1},{2,10},{10,2},{3,11},{11,3},{4,12},{12,4},... | collective-permute-start | bytes 3538952 | tf_op jit(solution)/shard_map/ppermute | solution.py:258
  57.5 1.0 copy-start.3
  58.5 1.0 copy-start.4
  61.2 8.1 %copy-start.17 = (bf16[912,128]{1,0:T(8,128)(2,1)}, bf16[912,128]{1,0:T(8,128)(2,1)S(1)}, u32[]{:S(2)}) copy-start(bf16[912,128]{1,0:T(8,128)(2,1)S(1)} %get-tuple-element.20) | copy-start | bytes 700420
  61.2 8.1 %copy-start.18 = (bf16[912,128]{1,0:T(8,128)(2,1)}, bf16[912,128]{1,0:T(8,128)(2,1)S(1)}, u32[]{:S(2)}) copy-start(bf16[912,128]{1,0:T(8,128)(2,1)S(1)} %get-tuple-element.18) | copy-start | bytes 700420
  61.2 8.1 %copy-start.19 = (bf16[912,128]{1,0:T(8,128)(2,1)}, bf16[912,128]{1,0:T(8,128)(2,1)S(1)}, u32[]{:S(2)}) copy-start(bf16[912,128]{1,0:T(8,128)(2,1)S(1)} %get-tuple-element.16) | copy-start | bytes 700420
  61.2 8.1 %copy-start.20 = (bf16[912,128]{1,0:T(8,128)(2,1)}, bf16[912,128]{1,0:T(8,128)(2,1)S(1)}, u32[]{:S(2)}) copy-start(bf16[912,128]{1,0:T(8,128)(2,1)S(1)} %get-tuple-element.14) | copy-start | bytes 700420
  61.2 14.9 %collective-permute-start.1 = (bf16[1680,128]{1,0:T(8,128)(2,1)}, bf16[1680,128]{1,0:T(8,128)(2,1)S(1)}, u32[]{:S(2)}, u32[]{:S(2)}) collective-permute-start(bf16[1680,128]{1,0:T(8,128)(2,1)} %get-tuple-element.15), channel_id=1, source_target_pairs={{0,2},{1,3},{2,0},{3,1},{4,6},{5,7},{6,4},{7,5},{8,10},{9,11},{10,... | collective-permute-start | bytes 1290248 | tf_op jit(solution)/shard_map/ppermute | solution.py:285
  64.6 22.5 %collective-permute-start.3 = (bf16[1680,128]{1,0:T(8,128)(2,1)}, bf16[1680,128]{1,0:T(8,128)(2,1)S(1)}, u32[]{:S(2)}, u32[]{:S(2)}) collective-permute-start(bf16[1680,128]{1,0:T(8,128)(2,1)} %get-tuple-element.17), channel_id=1, source_target_pairs={{0,4},{1,5},{2,6},{3,7},{4,0},{5,1},{6,2},{7,3},{8,12},{9,13},{10,... | collective-permute-start | bytes 1290248 | tf_op jit(solution)/shard_map/ppermute | solution.py:285
  69.3 24.3 %collective-permute-start.5 = (bf16[1680,128]{1,0:T(8,128)(2,1)}, bf16[1680,128]{1,0:T(8,128)(2,1)S(1)}, u32[]{:S(2)}, u32[]{:S(2)}) collective-permute-start(bf16[1680,128]{1,0:T(8,128)(2,1)} %get-tuple-element.19), channel_id=1, source_target_pairs={{0,6},{1,7},{2,4},{3,5},{4,2},{5,3},{6,0},{7,1},{8,14},{9,15},{10,... | collective-permute-start | bytes 1290248 | tf_op jit(solution)/shard_map/ppermute | solution.py:285
  98.6 44.3 %all-to-all-start.2 = ((bf16[8,768,128]{2,1,0:T(8,128)(2,1)}), bf16[8,768,128]{2,1,0:T(8,128)(2,1)S(1)}, u32[]{:S(2)}, u32[]{:S(2)}) async-start(bf16[8,768,128]{2,1,0:T(8,128)(2,1)} %project.1), calls=%async_computation.2 | async-start | bytes 3145728 | tf_op jit(solution)/shard_map/all_to_all | solution.py:248
  102.2 38.6 %collective-permute-start = (bf16[912,128]{1,0:T(8,128)(2,1)}, bf16[912,128]{1,0:T(8,128)(2,1)S(1)}, u32[]{:S(2)}, u32[]{:S(2)}) collective-permute-start(bf16[912,128]{1,0:T(8,128)(2,1)} %copy-done.20), channel_id=1, source_target_pairs={{0,1},{1,0},{2,3},{3,2},{4,5},{5,4},{6,7},{7,6},{8,9},{9,8},{10,11... | collective-permute-start | bytes 700424 | tf_op jit(solution)/shard_map/ppermute | solution.py:285
  106.0 34.8 %collective-permute-start.2 = (bf16[912,128]{1,0:T(8,128)(2,1)}, bf16[912,128]{1,0:T(8,128)(2,1)S(1)}, u32[]{:S(2)}, u32[]{:S(2)}) collective-permute-start(bf16[912,128]{1,0:T(8,128)(2,1)} %copy-done.19), channel_id=1, source_target_pairs={{0,3},{1,2},{2,1},{3,0},{4,7},{5,6},{6,5},{7,4},{8,11},{9,10},{10,... | collective-permute-start | bytes 700424 | tf_op jit(solution)/shard_map/ppermute | solution.py:285
  109.4 32.1 %collective-permute-start.4 = (bf16[912,128]{1,0:T(8,128)(2,1)}, bf16[912,128]{1,0:T(8,128)(2,1)S(1)}, u32[]{:S(2)}, u32[]{:S(2)}) collective-permute-start(bf16[912,128]{1,0:T(8,128)(2,1)} %copy-done.18), channel_id=1, source_target_pairs={{0,5},{1,4},{2,7},{3,6},{4,1},{5,0},{6,3},{7,2},{8,13},{9,12},{10,... | collective-permute-start | bytes 700424 | tf_op jit(solution)/shard_map/ppermute | solution.py:285
  114.9 27.3 %collective-permute-start.6 = (bf16[912,128]{1,0:T(8,128)(2,1)}, bf16[912,128]{1,0:T(8,128)(2,1)S(1)}, u32[]{:S(2)}, u32[]{:S(2)}) collective-permute-start(bf16[912,128]{1,0:T(8,128)(2,1)} %copy-done.17), channel_id=1, source_target_pairs={{0,7},{1,6},{2,5},{3,4},{4,3},{5,2},{6,1},{7,0},{8,15},{9,14},{10,... | collective-permute-start | bytes 700424 | tf_op jit(solution)/shard_map/ppermute | solution.py:285
  116.9 0.9 copy-start.11
  118.0 0.6 copy-start.12
  118.6 0.6 copy-start.14
  140.8 0.7 copy-start.5
  141.5 0.7 copy-start.7
  142.2 0.7 copy-start.9
  142.9 0.9 copy-start.6
  143.8 0.9 copy-start.8
  144.8 0.9 copy-start.10
  145.7 0.8 copy-start.13
  146.5 0.8 copy-start.15

commit v3 on v2

--- a/solution.py
+++ b/solution.py
@@ -1,3 +1,4 @@
+import functools
 import math
 
 import jax
@@ -19,6 +20,7 @@
 IN_ROWS = 912
 SLAB = 768
 GRANT = 16 << 20
+WHOLE_GRANT = 62 << 20
 MID = 192
 GQA, GKA, GVA, GKC, GVC, GQC = 0, 128, 256, 384, 512, 640
 OUT_ROWS = 704
@@ -32,7 +34,18 @@
     return lax.dot_general(a, b, dims, preferred_element_type=F32)
 
 
-def pack_kernel(me_ref, q_ref, k_ref, v_ref, o_ref, n_ref, g_ref, *out_refs):
+def load(sources, targets, sems):
+    copies = [pltpu.make_async_copy(a, b, sems.at[n]) for n, (a, b) in enumerate(zip(sources, targets, strict=True))]
+    for copy in copies:
+        copy.start()
+    for copy in copies:
+        copy.wait()
+
+
+def pack_kernel(me_ref, q_hbm, k_hbm, v_hbm, o_hbm, n_hbm, g_hbm, *refs):
+    out_refs = refs[:8]
+    q_ref, k_ref, v_ref, o_ref, n_ref, g_ref, sems = refs[8:]
+    load((q_hbm, k_hbm, v_hbm, o_hbm, n_hbm, g_hbm), (q_ref, k_ref, v_ref, o_ref, n_ref, g_ref), sems)
     for d, out_ref in enumerate(out_refs):
         to = jnp.bitwise_xor(me_ref[0], d)
         x, y = to // 2, to % 2
@@ -61,10 +74,16 @@
     whole = pl.BlockSpec(memory_space=pltpu.VMEM)
     return pl.pallas_call(
         pack_kernel,
-        in_specs=[pl.BlockSpec(memory_space=pltpu.SMEM)] + [whole] * 6,
+        in_specs=[pl.BlockSpec(memory_space=pltpu.SMEM)] + [pl.BlockSpec(memory_space=pl.ANY)] * 6,
         out_specs=(whole,) * 8,
         out_shape=tuple(jax.ShapeDtypeStruct((IN_ROWS + (0 if d % 2 else SLAB), 128), BF) for d in range(8)),
-        compiler_params=pltpu.CompilerParams(vmem_limit_bytes=GRANT),
+        scratch_shapes=[
+            *[pltpu.VMEM((128, 1536), BF)] * 4,
+            pltpu.VMEM((12, 128), BF),
+            pltpu.VMEM((128, 3072), BF),
+            pltpu.SemaphoreType.DMA((6,)),
+        ],
+        compiler_params=pltpu.CompilerParams(vmem_limit_bytes=WHOLE_GRANT),
         name="pack",
     )(me, q, k, v, o, norms, out_grad)
 
@@ -169,14 +188,10 @@
 
 def attend_kernel(me_ref, *refs):
     sent_refs = refs[:8]
-    mid_ref, mask_a_ref, mask_c_ref, out_ref, in_ref, dk_ref, dv_ref, sems = refs[8:]
-    copies = []
-    for d, ref in enumerate(sent_refs):
-        source = ref if d % 2 else ref.at[pl.ds(SLAB, IN_ROWS)]
-        copies.append(pltpu.make_async_copy(source, in_ref.at[jnp.bitwise_xor(me_ref[0], d)], sems.at[d]))
-        copies[-1].start()
-    for copy in copies:
-        copy.wait()
+    mid_ref, mask_a_hbm, mask_c_hbm, out_ref, in_ref, dk_ref, dv_ref, mask_a_ref, mask_c_ref, sems = refs[8:]
+    sources = [ref if d % 2 else ref.at[pl.ds(SLAB, IN_ROWS)] for d, ref in enumerate(sent_refs)]
+    targets = [in_ref.at[jnp.bitwise_xor(me_ref[0], d)] for d in range(8)]
+    load((*sources, mask_a_hbm, mask_c_hbm), (*targets, mask_a_ref, mask_c_ref), sems)
     second = me_ref[0] % 2 == 1
 
     def norm_a(b):
@@ -204,14 +219,17 @@
         attend_kernel,
         in_specs=[pl.BlockSpec(memory_space=pltpu.SMEM)]
         + [pl.BlockSpec(memory_space=pl.ANY)] * 8
-        + [whole, whole, whole],
+        + [whole]
+        + [pl.BlockSpec(memory_space=pl.ANY)] * 2,
         out_specs=whole,
         out_shape=jax.ShapeDtypeStruct((8, OUT_ROWS, 128), BF),
         scratch_shapes=[
             pltpu.VMEM((8, IN_ROWS, 128), BF),
             pltpu.VMEM((1024, 128), F32),
             pltpu.VMEM((1024, 128), F32),
-            pltpu.SemaphoreType.DMA((8,)),
+            pltpu.VMEM((16, 1024), F32),
+            pltpu.VMEM((16, 512), F32),
+            pltpu.SemaphoreType.DMA((10,)),
         ],
         compiler_params=pltpu.CompilerParams(vmem_limit_bytes=GRANT),
         name="attend",
@@ -259,23 +277,22 @@
     return own, other
 
 
-def mask_kernel(where_ref, table_ref, whole_ref, shared_ref):
+def mask_kernel(shared, where_ref, table_ref, out_ref):
     x, y = where_ref[0] // 2, where_ref[0] % 2
-    for ref, head in ((whole_ref, 3 * x + y), (shared_ref, 3 * x + 2)):
-        tile = lax.broadcasted_iota(jnp.int32, (16, ref.shape[1]), 0)
-        group = lax.broadcasted_iota(jnp.int32, (16, ref.shape[1]), 1) // TILE
-        of_lane = group if ref is whole_ref else 2 * group + y
-        spread_out = jnp.where(tile == of_lane, 1.0, 0.0)
-        ref[...] = dot(table_ref[0, head].astype(F32), spread_out, TN_DIMS)
-
-
-def mask_rows(me, tile_mask):
+    tile = lax.broadcasted_iota(jnp.int32, out_ref.shape, 0)
+    group = lax.broadcasted_iota(jnp.int32, out_ref.shape, 1) // TILE
+    of_lane = 2 * group + y if shared else group
+    head = 3 * x + 2 if shared else 3 * x + y
+    out_ref[...] = dot(table_ref[0, head].astype(F32), jnp.where(tile == of_lane, 1.0, 0.0), TN_DIMS)
+
+
+def mask_rows(me, tile_mask, shared):
     whole = pl.BlockSpec(memory_space=pltpu.VMEM)
     return pl.pallas_call(
-        mask_kernel,
+        functools.partial(mask_kernel, shared),
         in_specs=[pl.BlockSpec(memory_space=pltpu.SMEM), whole],
-        out_specs=(whole, whole),
-        out_shape=(jax.ShapeDtypeStruct((16, 1024), F32), jax.ShapeDtypeStruct((16, 512), F32)),
+        out_specs=whole,
+        out_shape=jax.ShapeDtypeStruct((16, 512 if shared else 1024), F32),
         compiler_params=pltpu.CompilerParams(vmem_limit_bytes=GRANT),
         name="mask",
     )(me, tile_mask)
@@ -292,7 +309,7 @@
     sent = pack(me, q[0], k[0], v[0], o[0], log_norm[0].T, out_grad[0])
     arrived = [sent[d] if d == 0 else swap(sent[d], d) for d in range(8)]
     partial = exchange(project(where, own, other, arrived[::2]), ("x", "yl"))
-    mask_a, mask_c = mask_rows(me, tile_mask)
+    mask_a, mask_c = mask_rows(me, tile_mask, False), mask_rows(me, tile_mask, True)
     result = exchange(attend(me, arrived, partial, mask_a, mask_c), ("x", "yl"))
     return merge(result)
 

time: 183 us -> 184 us (level)
  local copies, waits for them, and re-layouts: 11.5 us -> 8.95 us
  Pallas kernels: 17.1 us -> 19.5 us
  waiting for transfers between devices: 43.4 us -> 45.3 us
    unnamed x42 -> x30, local copies, waits for them, and re-layouts: 10.6 us -> 8.09 us
    pallas_call x1, Pallas kernels: 1.63 us -> 3.71 us  [pack(): pl.pallas_call(pack_kernel, in_specs=[pl.BlockSpec(memory_space=pltpu.SME...]
    ppermute x7, waiting for transfers between devices: 43.4 us -> 45.3 us  [swap(): return lax.ppermute(array, ('x', 'yl'), [(s, s ^ d) for s in range(8)])]
  transfers between devices with their start and end apart: 9 -> 9, of which waited for: 4 -> 4; matrix products, arithmetic and copies ran while one was open for 0% -> 0% of each run, Pallas kernels for 1% -> 2%
where the time goes in v3:
time: 184 us; the launch traced here: 183 us
  blocking collectives  78 us (42%)
  waiting for transfers between devices  45.3 us (25%)
  starting transfers between devices  30.7 us (17%)
  Pallas kernels  19.5 us (11%)
  local copies, waits for them, and re-layouts  8.95 us (5%)
    all_to_all x3, blocking collectives, exchange(): return lax.all_to_all(array, axes, split_axis=0, concat_axis=0, tiled=True)  78 us
    ppermute x7, waiting for transfers between devices, swap(): return lax.ppermute(array, ('x', 'yl'), [(s, s ^ d) for s in range(8)])  45.3 us
    ppermute x7, starting transfers between devices, swap(): return lax.ppermute(array, ('x', 'yl'), [(s, s ^ d) for s in range(8)])  25.1 us
    pallas_call x1, Pallas kernels, attend(): pl.pallas_call(attend_kernel, in_specs=[pl.BlockSpec(memory_space=pltpu.S...  8.78 us
    unnamed x30, local copies, waits for them, and re-layouts  8.09 us
    pallas_call x1, Pallas kernels, project(): pl.pallas_call(project_kernel, grid=(4,), in_specs=[pl.BlockSpec(memory_s...  5.03 us
    all_to_all x1, starting transfers between devices, exchange(): return lax.all_to_all(array, axes, split_axis=0, concat_axis=0, tiled=True)  3.72 us
    pallas_call x1, Pallas kernels, pack(): pl.pallas_call(pack_kernel, in_specs=[pl.BlockSpec(memory_space=pltpu.SME...  3.71 us
  transfers between devices with their start and end apart: 9, of which 4 were waited for; matrix products, arithmetic and copies ran while one was open for 0% of the time, Pallas kernels for 2%

profile of v3, /device:TPU:32, one launch (start us, length us, event | category | flops | bytes accessed | tf_op | source)
XLA Modules:
  0.0 183.4 jit_solution(2574979356215002653)
XLA Ops:
  0.6 0.7 broadcast_in_dim.4
  1.4 33.8 %all_to_all.20 = bf16[16,24,384]{2,1,0:T(8,128)(2,1)S(1)} all-to-all(bf16[16,24,384]{2,1,0:T(8,128)(2,1)S(1)} %broadcast_in_dim.4), channel_id=1, replica_groups=mesh['z'=16,'yh'=2,'core'=2,'x'=4,'yl'=2] {'z'}, dimensions={0} | all-to-all | bytes 589824 | tf_op jit(solution)/shard_map/all_to_all | solution.py:266
  35.3 20.1 %all_to_all.21 = bf16[4,16,24,384]{3,2,1,0:T(8,128)(2,1)S(1)} all-to-all(bf16[4,16,24,384]{3,2,1,0:T(8,128)(2,1)S(1)} %broadcast_in_dim.5), channel_id=1, replica_groups=mesh['z'=16,'yh'=2,'core'=2,'x'=4,'yl'=2] {'yh','yl'}, dimensions={0} | all-to-all | bytes 2359296 | tf_op jit(solution)/shard_map/all_to_all | solution.py:266
  55.4 1.9 %collective-permute-start.7 = (bf16[2,2,16,24,384]{4,3,2,1,0:T(8,128)(2,1)S(1)}, bf16[2,2,16,24,384]{4,3,2,1,0:T(8,128)(2,1)}, u32[]{:S(2)}, u32[]{:S(2)}) collective-permute-start(bf16[2,2,16,24,384]{4,3,2,1,0:T(8,128)(2,1)S(1)} %bitcast.12), channel_id=1, source_target_pairs={{0,8},{8,0},{1,9},{9,1},{2,10},{10,2},{3,11},{11,3},{4,12},{12,4},... | collective-permute-start | bytes 3538952 | tf_op jit(solution)/shard_map/ppermute | solution.py:276
  57.3 3.7 %pack.1 = (bf16[1680,128]{1,0:T(8,128)(2,1)}, bf16[912,128]{1,0:T(8,128)(2,1)}, bf16[1680,128]{1,0:T(8,128)(2,1)}, bf16[912,128]{1,0:T(8,128)(2,1)}, bf16[1680,1...) custom-call(s32[1]{0:T(128)} %bitcast.me_ref.where_ref, ...), custom_call_target="tpu_custom_call" | custom-call | tf_op jit(solution)/shard_map/pack/pallas_call | solution.py:75
  61.0 3.4 %collective-permute-start.1 = (bf16[1680,128]{1,0:T(8,128)(2,1)}, bf16[1680,128]{1,0:T(8,128)(2,1)S(1)}, u32[]{:S(2)}, u32[]{:S(2)}) collective-permute-start(bf16[1680,128]{1,0:T(8,128)(2,1)} %get-tuple-element.13), channel_id=1, source_target_pairs={{0,2},{1,3},{2,0},{3,1},{4,6},{5,7},{6,4},{7,5},{8,10},{9,11},{10,... | collective-permute-start | bytes 1290248 | tf_op jit(solution)/shard_map/ppermute | solution.py:302
  64.4 4.6 %collective-permute-start.3 = (bf16[1680,128]{1,0:T(8,128)(2,1)}, bf16[1680,128]{1,0:T(8,128)(2,1)S(1)}, u32[]{:S(2)}, u32[]{:S(2)}) collective-permute-start(bf16[1680,128]{1,0:T(8,128)(2,1)} %get-tuple-element.15), channel_id=1, source_target_pairs={{0,4},{1,5},{2,6},{3,7},{4,0},{5,1},{6,2},{7,3},{8,12},{9,13},{10,... | collective-permute-start | bytes 1290248 | tf_op jit(solution)/shard_map/ppermute | solution.py:302
  69.1 2.4 %collective-permute-start.5 = (bf16[1680,128]{1,0:T(8,128)(2,1)}, bf16[1680,128]{1,0:T(8,128)(2,1)S(1)}, u32[]{:S(2)}, u32[]{:S(2)}) collective-permute-start(bf16[1680,128]{1,0:T(8,128)(2,1)} %get-tuple-element.17), channel_id=1, source_target_pairs={{0,6},{1,7},{2,4},{3,5},{4,2},{5,3},{6,0},{7,1},{8,14},{9,15},{10,... | collective-permute-start | bytes 1290248 | tf_op jit(solution)/shard_map/ppermute | solution.py:302
  71.5 4.4 %collective-permute-done.1.g1_ref.refs_2_ = bf16[1680,128]{1,0:T(8,128)(2,1)S(1)} collective-permute-done((bf16[1680,128]{1,0:T(8,128)(2,1)}, bf16[1680,128]{1,0:T(8,128)(2,1)S(1)}, u32[]{:S(2)}, u32[]{:S(2)}) %collective-permute-start.1) | collective-permute-done | bytes 430112 | tf_op jit(solution)/shard_map/ppermute | solution.py:302
  75.9 11.0 %collective-permute-done.3.g2_ref.refs_4_ = bf16[1680,128]{1,0:T(8,128)(2,1)S(1)} collective-permute-done((bf16[1680,128]{1,0:T(8,128)(2,1)}, bf16[1680,128]{1,0:T(8,128)(2,1)S(1)}, u32[]{:S(2)}, u32[]{:S(2)}) %collective-permute-start.3) | collective-permute-done | bytes 430112 | tf_op jit(solution)/shard_map/ppermute | solution.py:302
  86.9 6.4 %collective-permute-done.5.g3_ref.refs_6_ = bf16[1680,128]{1,0:T(8,128)(2,1)S(1)} collective-permute-done((bf16[1680,128]{1,0:T(8,128)(2,1)}, bf16[1680,128]{1,0:T(8,128)(2,1)S(1)}, u32[]{:S(2)}, u32[]{:S(2)}) %collective-permute-start.5) | collective-permute-done | bytes 430112 | tf_op jit(solution)/shard_map/ppermute | solution.py:302
  93.4 1.2 copy-done
  94.5 5.0 %project.1 = bf16[8,768,128]{2,1,0:T(8,128)(2,1)} custom-call(s32[2]{0:T(128)S(1)} %pad_add_fusion.where_ref, bf16[2,2,16,24,384]{4,3,2,1,0:T(8,128)(2,1)S(1)} %bitcast.13, bf16[2,2,16,24,384]{4,3,2,1,0:T(8,128)(2,1)} %collective-permute-done.7.other_ref, bf16[1680,128]{1,0:T(8,128)(2,1)S(1)} %copy-done, ...), custom_call_target="tpu_custom_call" | custom-call | tf_op jit(solution)/shard_map/project/pallas_call | solution.py:122
  99.6 3.7 %all-to-all-start.2 = ((bf16[8,768,128]{2,1,0:T(8,128)(2,1)}), bf16[8,768,128]{2,1,0:T(8,128)(2,1)S(1)}, u32[]{:S(2)}, u32[]{:S(2)}) async-start(bf16[8,768,128]{2,1,0:T(8,128)(2,1)} %project.1), calls=%async_computation.2 | async-start | bytes 3145728 | tf_op jit(solution)/shard_map/all_to_all | solution.py:266
  103.3 3.8 %collective-permute-start = (bf16[912,128]{1,0:T(8,128)(2,1)}, bf16[912,128]{1,0:T(8,128)(2,1)S(1)}, u32[]{:S(2)}, u32[]{:S(2)}) collective-permute-start(bf16[912,128]{1,0:T(8,128)(2,1)} %get-tuple-element.12), channel_id=1, source_target_pairs={{0,1},{1,0},{2,3},{3,2},{4,5},{5,4},{6,7},{7,6},{8,9},{9,8},{10,11... | collective-permute-start | bytes 700424 | tf_op jit(solution)/shard_map/ppermute | solution.py:302
  107.2 3.4 %collective-permute-start.2 = (bf16[912,128]{1,0:T(8,128)(2,1)}, bf16[912,128]{1,0:T(8,128)(2,1)S(1)}, u32[]{:S(2)}, u32[]{:S(2)}) collective-permute-start(bf16[912,128]{1,0:T(8,128)(2,1)} %get-tuple-element.14), channel_id=1, source_target_pairs={{0,3},{1,2},{2,1},{3,0},{4,7},{5,6},{6,5},{7,4},{8,11},{9,10},{10,... | collective-permute-start | bytes 700424 | tf_op jit(solution)/shard_map/ppermute | solution.py:302
  110.5 5.5 %collective-permute-start.4 = (bf16[912,128]{1,0:T(8,128)(2,1)S(1)}, bf16[912,128]{1,0:T(8,128)(2,1)S(1)}, u32[]{:S(2)}, u32[]{:S(2)}) collective-permute-start(bf16[912,128]{1,0:T(8,128)(2,1)S(1)} %copy-done.14), channel_id=1, source_target_pairs={{0,5},{1,4},{2,7},{3,6},{4,1},{5,0},{6,3},{7,2},{8,13},{9,12},{10,... | collective-permute-start | bytes 700424 | tf_op jit(solution)/shard_map/ppermute | solution.py:302
  116.1 2.0 %collective-permute-start.6 = (bf16[912,128]{1,0:T(8,128)(2,1)S(1)}, bf16[912,128]{1,0:T(8,128)(2,1)S(1)}, u32[]{:S(2)}, u32[]{:S(2)}) collective-permute-start(bf16[912,128]{1,0:T(8,128)(2,1)S(1)} %copy-done.13), channel_id=1, source_target_pairs={{0,7},{1,6},{2,5},{3,4},{4,3},{5,2},{6,1},{7,0},{8,15},{9,14},{10,... | collective-permute-start | bytes 700424 | tf_op jit(solution)/shard_map/ppermute | solution.py:302
  118.1 0.2 mask.2.refs_9_
  118.3 0.2 mask.3.refs_10_
  118.5 23.5 %collective-permute-done.refs_1_ = bf16[912,128]{1,0:T(8,128)(2,1)S(1)} collective-permute-done((bf16[912,128]{1,0:T(8,128)(2,1)}, bf16[912,128]{1,0:T(8,128)(2,1)S(1)}, u32[]{:S(2)}, u32[]{:S(2)}) %collective-permute-start) | collective-permute-done | bytes 233504 | tf_op jit(solution)/shard_map/ppermute | solution.py:302
  142.0 0.7 copy-done.7
  142.7 0.7 copy-done.9
  143.4 0.7 copy-done.11
  144.1 1.0 copy-done.3
  145.1 1.0 copy-done.5
  146.1 0.9 copy-done.8
  147.0 0.9 copy-done.10
  148.0 0.9 copy-done.12
  148.9 8.8 %attend.1 = bf16[8,704,128]{2,1,0:T(8,128)(2,1)S(1)} custom-call(s32[1]{0:T(128)} %bitcast.me_ref.where_ref, bf16[1680,128]{1,0:T(8,128)(2,1)S(1)} %copy-done.1, bf16[912,128]{1,0:T(8,128)(2,1)S(1)} %collective-permute-done.refs_1_, bf16[1680,128]{1,0:T(8,128)(2,1)S(1)} %collective-permute-done.1.g1_ref.refs_2_, bf16[912,128]{1,0:T(8,128)(2,1)S(1)} %copy-done.8, ...), custom_call_target="tpu_custom_call" | custom-call | tf_op jit(solution)/shard_map/attend/pallas_call | solution.py:218
  157.7 24.1 %all_to_all.22.in_ref = bf16[8,704,128]{2,1,0:T(8,128)(2,1)S(1)} all-to-all(bf16[8,704,128]{2,1,0:T(8,128)(2,1)S(1)} %attend.1), channel_id=1, replica_groups=mesh['z'=16,'yh'=2,'core'=2,'x'=4,'yl'=2] {'x','yl'}, dimensions={0} | all-to-all | bytes 2883584 | tf_op jit(solution)/shard_map/all_to_all | solution.py:266
  181.8 1.6 merge.1
  (28 shorter events, 0.2 us)
Async XLA Ops:
  55.4 38.0 %collective-permute-start.7 = (bf16[2,2,16,24,384]{4,3,2,1,0:T(8,128)(2,1)S(1)}, bf16[2,2,16,24,384]{4,3,2,1,0:T(8,128)(2,1)}, u32[]{:S(2)}, u32[]{:S(2)}) collective-permute-start(bf16[2,2,16,24,384]{4,3,2,1,0:T(8,128)(2,1)S(1)} %bitcast.12), channel_id=1, source_target_pairs={{0,8},{8,0},{1,9},{9,1},{2,10},{10,2},{3,11},{11,3},{4,12},{12,4},... | collective-permute-start | bytes 3538952 | tf_op jit(solution)/shard_map/ppermute | solution.py:276
  61.0 14.9 %collective-permute-start.1 = (bf16[1680,128]{1,0:T(8,128)(2,1)}, bf16[1680,128]{1,0:T(8,128)(2,1)S(1)}, u32[]{:S(2)}, u32[]{:S(2)}) collective-permute-start(bf16[1680,128]{1,0:T(8,128)(2,1)} %get-tuple-element.13), channel_id=1, source_target_pairs={{0,2},{1,3},{2,0},{3,1},{4,6},{5,7},{6,4},{7,5},{8,10},{9,11},{10,... | collective-permute-start | bytes 1290248 | tf_op jit(solution)/shard_map/ppermute | solution.py:302
  64.4 22.5 %collective-permute-start.3 = (bf16[1680,128]{1,0:T(8,128)(2,1)}, bf16[1680,128]{1,0:T(8,128)(2,1)S(1)}, u32[]{:S(2)}, u32[]{:S(2)}) collective-permute-start(bf16[1680,128]{1,0:T(8,128)(2,1)} %get-tuple-element.15), channel_id=1, source_target_pairs={{0,4},{1,5},{2,6},{3,7},{4,0},{5,1},{6,2},{7,3},{8,12},{9,13},{10,... | collective-permute-start | bytes 1290248 | tf_op jit(solution)/shard_map/ppermute | solution.py:302
  69.1 24.3 %collective-permute-start.5 = (bf16[1680,128]{1,0:T(8,128)(2,1)}, bf16[1680,128]{1,0:T(8,128)(2,1)S(1)}, u32[]{:S(2)}, u32[]{:S(2)}) collective-permute-start(bf16[1680,128]{1,0:T(8,128)(2,1)} %get-tuple-element.17), channel_id=1, source_target_pairs={{0,6},{1,7},{2,4},{3,5},{4,2},{5,3},{6,0},{7,1},{8,14},{9,15},{10,... | collective-permute-start | bytes 1290248 | tf_op jit(solution)/shard_map/ppermute | solution.py:302
  86.9 12.6 %copy-start.2 = (bf16[1680,128]{1,0:T(8,128)(2,1)}, bf16[1680,128]{1,0:T(8,128)(2,1)S(1)}, u32[]{:S(2)}) copy-start(bf16[1680,128]{1,0:T(8,128)(2,1)S(1)} %collective-permute-done.3.g2_ref.refs_4_) | copy-start | bytes 1290244
  93.4 6.2 %copy-start.4 = (bf16[1680,128]{1,0:T(8,128)(2,1)}, bf16[1680,128]{1,0:T(8,128)(2,1)S(1)}, u32[]{:S(2)}) copy-start(bf16[1680,128]{1,0:T(8,128)(2,1)S(1)} %collective-permute-done.5.g3_ref.refs_6_) | copy-start | bytes 1290244
  93.4 1.2 copy-start
  99.6 11.0 %copy-start.14 = (bf16[912,128]{1,0:T(8,128)(2,1)S(1)}, bf16[912,128]{1,0:T(8,128)(2,1)}, u32[]{:S(2)}) copy-start(bf16[912,128]{1,0:T(8,128)(2,1)} %get-tuple-element.16) | copy-start | bytes 700420
  99.6 16.5 %copy-start.13 = (bf16[912,128]{1,0:T(8,128)(2,1)S(1)}, bf16[912,128]{1,0:T(8,128)(2,1)}, u32[]{:S(2)}) copy-start(bf16[912,128]{1,0:T(8,128)(2,1)} %get-tuple-element.18) | copy-start | bytes 700420
  99.6 18.5 %copy-start.6 = (s32[1,12,16,16]{3,2,1,0:T(8,128)S(1)}, s32[1,12,16,16]{3,2,1,0:T(8,128)}, u32[]{:S(2)}) copy-start(s32[1,12,16,16]{3,2,1,0:T(8,128)} %table_ref.3) | copy-start | bytes 36868
  99.6 44.5 %copy-start.1 = (bf16[1680,128]{1,0:T(8,128)(2,1)S(1)}, bf16[1680,128]{1,0:T(8,128)(2,1)}, u32[]{:S(2)}) copy-start(bf16[1680,128]{1,0:T(8,128)(2,1)} %get-tuple-element.11.g0_ref.refs_0_) | copy-start | bytes 1290244
  99.6 44.5 %all-to-all-start.2 = ((bf16[8,768,128]{2,1,0:T(8,128)(2,1)}), bf16[8,768,128]{2,1,0:T(8,128)(2,1)S(1)}, u32[]{:S(2)}, u32[]{:S(2)}) async-start(bf16[8,768,128]{2,1,0:T(8,128)(2,1)} %project.1), calls=%async_computation.2 | async-start | bytes 3145728 | tf_op jit(solution)/shard_map/all_to_all | solution.py:266
  103.3 38.6 %collective-permute-start = (bf16[912,128]{1,0:T(8,128)(2,1)}, bf16[912,128]{1,0:T(8,128)(2,1)S(1)}, u32[]{:S(2)}, u32[]{:S(2)}) collective-permute-start(bf16[912,128]{1,0:T(8,128)(2,1)} %get-tuple-element.12), channel_id=1, source_target_pairs={{0,1},{1,0},{2,3},{3,2},{4,5},{5,4},{6,7},{7,6},{8,9},{9,8},{10,11... | collective-permute-start | bytes 700424 | tf_op jit(solution)/shard_map/ppermute | solution.py:302
  107.2 34.8 %collective-permute-start.2 = (bf16[912,128]{1,0:T(8,128)(2,1)}, bf16[912,128]{1,0:T(8,128)(2,1)S(1)}, u32[]{:S(2)}, u32[]{:S(2)}) collective-permute-start(bf16[912,128]{1,0:T(8,128)(2,1)} %get-tuple-element.14), channel_id=1, source_target_pairs={{0,3},{1,2},{2,1},{3,0},{4,7},{5,6},{6,5},{7,4},{8,11},{9,10},{10,... | collective-permute-start | bytes 700424 | tf_op jit(solution)/shard_map/ppermute | solution.py:302
  110.5 32.1 %collective-permute-start.4 = (bf16[912,128]{1,0:T(8,128)(2,1)S(1)}, bf16[912,128]{1,0:T(8,128)(2,1)S(1)}, u32[]{:S(2)}, u32[]{:S(2)}) collective-permute-start(bf16[912,128]{1,0:T(8,128)(2,1)S(1)} %copy-done.14), channel_id=1, source_target_pairs={{0,5},{1,4},{2,7},{3,6},{4,1},{5,0},{6,3},{7,2},{8,13},{9,12},{10,... | collective-permute-start | bytes 700424 | tf_op jit(solution)/shard_map/ppermute | solution.py:302
  116.1 27.3 %collective-permute-start.6 = (bf16[912,128]{1,0:T(8,128)(2,1)S(1)}, bf16[912,128]{1,0:T(8,128)(2,1)S(1)}, u32[]{:S(2)}, u32[]{:S(2)}) collective-permute-start(bf16[912,128]{1,0:T(8,128)(2,1)S(1)} %copy-done.13), channel_id=1, source_target_pairs={{0,7},{1,6},{2,5},{3,4},{4,3},{5,2},{6,1},{7,0},{8,15},{9,14},{10,... | collective-permute-start | bytes 700424 | tf_op jit(solution)/shard_map/ppermute | solution.py:302
  142.0 0.7 copy-start.7
  142.7 0.7 copy-start.9
  143.4 0.7 copy-start.11
  144.1 1.0 copy-start.3
  145.1 1.0 copy-start.5
  146.1 0.9 copy-start.8
  147.0 0.9 copy-start.10
  148.0 0.9 copy-start.12

commit v4 on v3

--- a/solution.py
+++ b/solution.py
@@ -21,6 +21,7 @@
 SLAB = 768
 GRANT = 16 << 20
 WHOLE_GRANT = 62 << 20
+WIDE_GRANT = 52 << 20
 MID = 192
 GQA, GKA, GVA, GKC, GVC, GQC = 0, 128, 256, 384, 512, 640
 OUT_ROWS = 704
@@ -131,12 +132,78 @@
     )(where, own, other, *slabs)
 
 
-def attend_unit(in_ref, mid_ref, mask_ref, out_ref, dk_ref, dv_ref, per, rows, norm_row, outs):
+KEYS = 1024
+CHUNK = 256
+BLOCKS = 6
+
+
+def score_unit(in_ref, mask_ref, prob_ref, copies, per, rows, block0, norm_row):
+    q0, k0 = rows
+    group = 256 // per
+    for b in range(8 // group):
+        q = jnp.concatenate([in_ref[s, q0 : q0 + per] for s in range(group * b, group * (b + 1))], axis=0)
+        norm = norm_row(b)
+        for n in range(KEYS // CHUNK):
+            k = in_ref[2 * n : 2 * n + 2, k0 : k0 + 128].reshape(CHUNK, HD)
+            prob = jnp.exp2(dot(k, q, NT_DIMS) * (SCALE * LOG2E) - norm)
+            allowed = mask_ref[4 * n : 4 * (n + 1), 256 * b : 256 * (b + 1)]
+            prob = (prob.reshape(4, TILE, 256) * allowed[:, None, :]).reshape(CHUNK, 256)
+            prob_ref[block0 + b, CHUNK * n : CHUNK * (n + 1)] = prob
+        copies[block0 + b].start()
+
+
+def score_kernel(me_ref, *refs):
+    sent_refs = refs[:8]
+    mask_a_hbm, mask_c_hbm, in_ref, prob_hbm, prob_ref, mask_a_ref, mask_c_ref, sems, prob_sems = refs[8:]
+    sources = [ref if d % 2 else ref.at[pl.ds(SLAB, IN_ROWS)] for d, ref in enumerate(sent_refs)]
+    targets = [in_ref.at[jnp.bitwise_xor(me_ref[0], d)] for d in range(8)]
+    load((*sources, mask_a_hbm, mask_c_hbm), (*targets, mask_a_ref, mask_c_ref), sems)
+    second = me_ref[0] % 2 == 1
+
+    def norm_a(b):
+        parts = [in_ref[s, NR : NR + 16].astype(F32)[0:1] for s in (2 * b, 2 * b + 1)]
+        return jnp.concatenate(parts, axis=1) * LOG2E
+
+    def norm_c(b):
+        parts = []
+        for s in range(4 * b, 4 * b + 4):
+            row = in_ref[s, NR : NR + 16].astype(F32)[1:2]
+            parts.append(jnp.where(second, row[:, 64:], row[:, :64]))
+        return jnp.concatenate(parts, axis=1) * LOG2E
+
+    copies = [pltpu.make_async_copy(prob_ref.at[b], prob_hbm.at[b], prob_sems.at[b]) for b in range(BLOCKS)]
+    score_unit(in_ref, mask_a_ref, prob_ref, copies, 128, (QA, KA), 0, norm_a)
+    score_unit(in_ref, mask_c_ref, prob_ref, copies, 64, (QC, KC), 4, norm_c)
+    for copy in copies:
+        copy.wait()
+
+
+def score(me, arrived, mask_a, mask_c):
+    whole = pl.BlockSpec(memory_space=pltpu.VMEM)
+    return pl.pallas_call(
+        score_kernel,
+        in_specs=[pl.BlockSpec(memory_space=pltpu.SMEM)] + [pl.BlockSpec(memory_space=pl.ANY)] * 10,
+        out_specs=(whole, pl.BlockSpec(memory_space=pl.ANY)),
+        out_shape=(
+            jax.ShapeDtypeStruct((8, IN_ROWS, 128), BF),
+            jax.ShapeDtypeStruct((BLOCKS, KEYS, 256), F32),
+        ),
+        scratch_shapes=[
+            pltpu.VMEM((BLOCKS, KEYS, 256), F32),
+            pltpu.VMEM((16, 1024), F32),
+            pltpu.VMEM((16, 512), F32),
+            pltpu.SemaphoreType.DMA((10,)),
+            pltpu.SemaphoreType.DMA((BLOCKS,)),
+        ],
+        compiler_params=pltpu.CompilerParams(vmem_limit_bytes=WIDE_GRANT),
+        name="score",
+    )(me, *arrived, mask_a, mask_c)
+
+
+def attend_unit(in_ref, prob_ref, copies, mid_ref, out_ref, dk_ref, dv_ref, per, rows, block0, outs):
     q0, o0, k0, v0, m0 = rows
     gq0, gk0, gv0 = outs
     group = 256 // per
-    keys = 1024
-    chunk = 256
     for b in range(8 // group):
         sources = range(group * b, group * (b + 1))
         q = jnp.concatenate([in_ref[s, q0 : q0 + per] for s in sources], axis=0)
@@ -154,22 +221,17 @@
             jnp.ones((8, 128), F32), product, NT_DIMS, precision=lax.Precision.HIGHEST, preferred_element_type=F32
         )[0:1]
         dots = dots.astype(BF).astype(F32)
-        norm = norm_row(b)
         dq = jnp.zeros((HD, 256), F32)
-        for n in range(keys // chunk):
+        copies[block0 + b].wait()
+        for n in range(KEYS // CHUNK):
             src = slice(2 * n, 2 * n + 2)
-            k = in_ref[src, k0 : k0 + 128].reshape(chunk, HD)
-            v = in_ref[src, v0 : v0 + 128].reshape(chunk, HD)
-            scores = dot(k, q, NT_DIMS)
-            prob = jnp.exp2(scores * (SCALE * LOG2E) - norm)
-            allowed = mask_ref[4 * n : 4 * (n + 1), 256 * b : 256 * (b + 1)]
-            prob = (prob.reshape(4, TILE, 256) * allowed[:, None, :]).reshape(chunk, 256)
-            score_grad = prob * (dot(v, g, NT_DIMS) - dots)
-            prob = prob.astype(BF)
-            score_grad = score_grad.astype(BF)
-            dv = dot(prob, g, NN_DIMS)
+            at = slice(CHUNK * n, CHUNK * (n + 1))
+            k = in_ref[src, k0 : k0 + 128].reshape(CHUNK, HD)
+            v = in_ref[src, v0 : v0 + 128].reshape(CHUNK, HD)
+            prob = prob_ref[block0 + b, at]
+            score_grad = (prob * (dot(v, g, NT_DIMS) - dots)).astype(BF)
+            dv = dot(prob.astype(BF), g, NN_DIMS)
             dk = dot(score_grad, q, NN_DIMS)
-            at = slice(chunk * n, chunk * (n + 1))
             if b == 0:
                 dv_ref[at] = dv
                 dk_ref[at] = dk
@@ -186,54 +248,31 @@
         out_ref[s, gv0 : gv0 + 128] = dv_ref[at].astype(BF)
 
 
-def attend_kernel(me_ref, *refs):
-    sent_refs = refs[:8]
-    mid_ref, mask_a_hbm, mask_c_hbm, out_ref, in_ref, dk_ref, dv_ref, mask_a_ref, mask_c_ref, sems = refs[8:]
-    sources = [ref if d % 2 else ref.at[pl.ds(SLAB, IN_ROWS)] for d, ref in enumerate(sent_refs)]
-    targets = [in_ref.at[jnp.bitwise_xor(me_ref[0], d)] for d in range(8)]
-    load((*sources, mask_a_hbm, mask_c_hbm), (*targets, mask_a_ref, mask_c_ref), sems)
-    second = me_ref[0] % 2 == 1
-
-    def norm_a(b):
-        parts = [in_ref[s, NR : NR + 16].astype(F32)[0:1] for s in (2 * b, 2 * b + 1)]
-        return jnp.concatenate(parts, axis=1) * LOG2E
-
-    def norm_c(b):
-        parts = []
-        for s in range(4 * b, 4 * b + 4):
-            row = in_ref[s, NR : NR + 16].astype(F32)[1:2]
-            parts.append(jnp.where(second, row[:, 64:], row[:, :64]))
-        return jnp.concatenate(parts, axis=1) * LOG2E
-
-    attend_unit(
-        in_ref, mid_ref, mask_a_ref, out_ref, dk_ref, dv_ref, 128, (QA, OA, KA, VA, 0), norm_a, (GQA, GKA, GVA)
-    )
-    attend_unit(
-        in_ref, mid_ref, mask_c_ref, out_ref, dk_ref, dv_ref, 64, (QC, OC, KC, VC, 128), norm_c, (GQC, GKC, GVC)
-    )
-
-
-def attend(me, arrived, partial, mask_a, mask_c):
+def attend_kernel(in_ref, prob_hbm, mid_ref, out_ref, prob_ref, dk_ref, dv_ref, sems):
+    copies = [pltpu.make_async_copy(prob_hbm.at[b], prob_ref.at[b], sems.at[b]) for b in range(BLOCKS)]
+    for copy in copies:
+        copy.start()
+    refs = (in_ref, prob_ref, copies, mid_ref, out_ref, dk_ref, dv_ref)
+    attend_unit(*refs, 128, (QA, OA, KA, VA, 0), 0, (GQA, GKA, GVA))
+    attend_unit(*refs, 64, (QC, OC, KC, VC, 128), 4, (GQC, GKC, GVC))
+
+
+def attend(inputs, prob, partial):
     whole = pl.BlockSpec(memory_space=pltpu.VMEM)
     return pl.pallas_call(
         attend_kernel,
-        in_specs=[pl.BlockSpec(memory_space=pltpu.SMEM)]
-        + [pl.BlockSpec(memory_space=pl.ANY)] * 8
-        + [whole]
-        + [pl.BlockSpec(memory_space=pl.ANY)] * 2,
+        in_specs=[whole, pl.BlockSpec(memory_space=pl.ANY), whole],
         out_specs=whole,
         out_shape=jax.ShapeDtypeStruct((8, OUT_ROWS, 128), BF),
         scratch_shapes=[
-            pltpu.VMEM((8, IN_ROWS, 128), BF),
-            pltpu.VMEM((1024, 128), F32),
-            pltpu.VMEM((1024, 128), F32),
-            pltpu.VMEM((16, 1024), F32),
-            pltpu.VMEM((16, 512), F32),
-            pltpu.SemaphoreType.DMA((10,)),
+            pltpu.VMEM((BLOCKS, KEYS, 256), F32),
+            pltpu.VMEM((KEYS, 128), F32),
+            pltpu.VMEM((KEYS, 128), F32),
+            pltpu.SemaphoreType.DMA((BLOCKS,)),
         ],
-        compiler_params=pltpu.CompilerParams(vmem_limit_bytes=GRANT),
+        compiler_params=pltpu.CompilerParams(vmem_limit_bytes=WIDE_GRANT),
         name="attend",
-    )(me, *arrived, partial, mask_a, mask_c)
+    )(inputs, prob, partial)
 
 
 def merge_kernel(in_ref, gq_ref, gk_ref, gv_ref):
@@ -308,9 +347,11 @@
     where = jnp.stack([core, x])
     sent = pack(me, q[0], k[0], v[0], o[0], log_norm[0].T, out_grad[0])
     arrived = [sent[d] if d == 0 else swap(sent[d], d) for d in range(8)]
-    partial = exchange(project(where, own, other, arrived[::2]), ("x", "yl"))
+    part = project(where, own, other, arrived[::2])
+    partial = exchange(part, ("x", "yl"))
     mask_a, mask_c = mask_rows(me, tile_mask, False), mask_rows(me, tile_mask, True)
-    result = exchange(attend(me, arrived, partial, mask_a, mask_c), ("x", "yl"))
+    inputs, prob = score(me, arrived, mask_a, mask_c)
+    result = exchange(attend(inputs, prob, partial), ("x", "yl"))
     return merge(result)
 
 

time: 184 us -> 186 us (1.011)
  Pallas kernels: 19.5 us -> 26.9 us
  local copies, waits for them, and re-layouts: 8.95 us -> 3.26 us
    pallas_call x1 -> x2, Pallas kernels: 8.78 us -> 16.1 us  [the longest x1 9.26 us: attend(): pl.pallas_call(attend_kernel, in_specs=[whole, pl.BlockSpec(memory_space=...]
    unnamed x30 -> x20, local copies, waits for them, and re-layouts: 8.09 us -> 2.41 us
  transfers between devices with their start and end apart: 9 -> 9, of which waited for: 4 -> 4; matrix products, arithmetic and copies ran while one was open for 0% -> 0% of each run, Pallas kernels for 2% -> 6%
where the time goes in v4:
time: 186 us; the launch traced here: 185 us
  blocking collectives  78 us (42%)
  waiting for transfers between devices  45.3 us (24%)
  starting transfers between devices  30.7 us (17%)
  Pallas kernels  26.9 us (14%)
  local copies, waits for them, and re-layouts  3.26 us (2%)
    all_to_all x3, blocking collectives, exchange(): return lax.all_to_all(array, axes, split_axis=0, concat_axis=0, tiled=True)  78 us
    ppermute x7, waiting for transfers between devices, swap(): return lax.ppermute(array, ('x', 'yl'), [(s, s ^ d) for s in range(8)])  45.3 us
    ppermute x7, starting transfers between devices, swap(): return lax.ppermute(array, ('x', 'yl'), [(s, s ^ d) for s in range(8)])  25.1 us
    pallas_call x1, Pallas kernels, attend(): pl.pallas_call(attend_kernel, in_specs=[whole, pl.BlockSpec(memory_space=...  9.26 us
    pallas_call x1, Pallas kernels, score(): pl.pallas_call(score_kernel, in_specs=[pl.BlockSpec(memory_space=pltpu.SM...  6.87 us
    pallas_call x1, Pallas kernels, project(): pl.pallas_call(project_kernel, grid=(4,), in_specs=[pl.BlockSpec(memory_s...  5.03 us
    all_to_all x1, starting transfers between devices, exchange(): return lax.all_to_all(array, axes, split_axis=0, concat_axis=0, tiled=True)  3.72 us
  transfers between devices with their start and end apart: 9, of which 4 were waited for; matrix products, arithmetic and copies ran while one was open for 0% of the time, Pallas kernels for 6%

profile of v4, /device:TPU:32, one launch (start us, length us, event | category | flops | bytes accessed | tf_op | source)
XLA Modules:
  0.0 185.1 jit_solution(8675076275741863238)
XLA Ops:
  0.6 0.7 broadcast_in_dim.4
  1.4 33.8 %all_to_all.20 = bf16[16,24,384]{2,1,0:T(8,128)(2,1)S(1)} all-to-all(bf16[16,24,384]{2,1,0:T(8,128)(2,1)S(1)} %broadcast_in_dim.4), channel_id=1, replica_groups=mesh['z'=16,'yh'=2,'core'=2,'x'=4,'yl'=2] {'z'}, dimensions={0} | all-to-all | bytes 589824 | tf_op jit(solution)/shard_map/all_to_all | solution.py:305
  35.2 0.1 broadcast_in_dim.5
  35.3 20.1 %all_to_all.21 = bf16[4,16,24,384]{3,2,1,0:T(8,128)(2,1)S(1)} all-to-all(bf16[4,16,24,384]{3,2,1,0:T(8,128)(2,1)S(1)} %broadcast_in_dim.5), channel_id=1, replica_groups=mesh['z'=16,'yh'=2,'core'=2,'x'=4,'yl'=2] {'yh','yl'}, dimensions={0} | all-to-all | bytes 2359296 | tf_op jit(solution)/shard_map/all_to_all | solution.py:305
  55.4 1.9 %collective-permute-start.7 = (bf16[2,2,16,24,384]{4,3,2,1,0:T(8,128)(2,1)S(1)}, bf16[2,2,16,24,384]{4,3,2,1,0:T(8,128)(2,1)}, u32[]{:S(2)}, u32[]{:S(2)}) collective-permute-start(bf16[2,2,16,24,384]{4,3,2,1,0:T(8,128)(2,1)S(1)} %bitcast.12), channel_id=1, source_target_pairs={{0,8},{8,0},{1,9},{9,1},{2,10},{10,2},{3,11},{11,3},{4,12},{12,4},... | collective-permute-start | bytes 3538952 | tf_op jit(solution)/shard_map/ppermute | solution.py:315
  57.3 3.7 %pack.1 = (bf16[1680,128]{1,0:T(8,128)(2,1)}, bf16[912,128]{1,0:T(8,128)(2,1)}, bf16[1680,128]{1,0:T(8,128)(2,1)}, bf16[912,128]{1,0:T(8,128)(2,1)}, bf16[1680,1...) custom-call(s32[1]{0:T(128)} %bitcast.me_ref.where_ref, ...), custom_call_target="tpu_custom_call" | custom-call | tf_op jit(solution)/shard_map/pack/pallas_call | solution.py:76
  61.0 3.4 %collective-permute-start.1 = (bf16[1680,128]{1,0:T(8,128)(2,1)}, bf16[1680,128]{1,0:T(8,128)(2,1)S(1)}, u32[]{:S(2)}, u32[]{:S(2)}) collective-permute-start(bf16[1680,128]{1,0:T(8,128)(2,1)} %get-tuple-element.15), channel_id=1, source_target_pairs={{0,2},{1,3},{2,0},{3,1},{4,6},{5,7},{6,4},{7,5},{8,10},{9,11},{10,... | collective-permute-start | bytes 1290248 | tf_op jit(solution)/shard_map/ppermute | solution.py:341
  64.4 4.6 %collective-permute-start.3 = (bf16[1680,128]{1,0:T(8,128)(2,1)}, bf16[1680,128]{1,0:T(8,128)(2,1)S(1)}, u32[]{:S(2)}, u32[]{:S(2)}) collective-permute-start(bf16[1680,128]{1,0:T(8,128)(2,1)} %get-tuple-element.17), channel_id=1, source_target_pairs={{0,4},{1,5},{2,6},{3,7},{4,0},{5,1},{6,2},{7,3},{8,12},{9,13},{10,... | collective-permute-start | bytes 1290248 | tf_op jit(solution)/shard_map/ppermute | solution.py:341
  69.1 2.4 %collective-permute-start.5 = (bf16[1680,128]{1,0:T(8,128)(2,1)}, bf16[1680,128]{1,0:T(8,128)(2,1)S(1)}, u32[]{:S(2)}, u32[]{:S(2)}) collective-permute-start(bf16[1680,128]{1,0:T(8,128)(2,1)} %get-tuple-element.19), channel_id=1, source_target_pairs={{0,6},{1,7},{2,4},{3,5},{4,2},{5,3},{6,0},{7,1},{8,14},{9,15},{10,... | collective-permute-start | bytes 1290248 | tf_op jit(solution)/shard_map/ppermute | solution.py:341
  71.5 0.1 pad_add_fusion.where_ref
  71.6 4.4 %collective-permute-done.1.refs_2_.g1_ref = bf16[1680,128]{1,0:T(8,128)(2,1)S(1)} collective-permute-done((bf16[1680,128]{1,0:T(8,128)(2,1)}, bf16[1680,128]{1,0:T(8,128)(2,1)S(1)}, u32[]{:S(2)}, u32[]{:S(2)}) %collective-permute-start.1) | collective-permute-done | bytes 430112 | tf_op jit(solution)/shard_map/ppermute | solution.py:341
  75.9 11.0 %collective-permute-done.3.refs_4_.g2_ref = bf16[1680,128]{1,0:T(8,128)(2,1)S(1)} collective-permute-done((bf16[1680,128]{1,0:T(8,128)(2,1)}, bf16[1680,128]{1,0:T(8,128)(2,1)S(1)}, u32[]{:S(2)}, u32[]{:S(2)}) %collective-permute-start.3) | collective-permute-done | bytes 430112 | tf_op jit(solution)/shard_map/ppermute | solution.py:341
  87.0 6.4 %collective-permute-done.5.refs_6_.g3_ref = bf16[1680,128]{1,0:T(8,128)(2,1)S(1)} collective-permute-done((bf16[1680,128]{1,0:T(8,128)(2,1)}, bf16[1680,128]{1,0:T(8,128)(2,1)S(1)}, u32[]{:S(2)}, u32[]{:S(2)}) %collective-permute-start.5) | collective-permute-done | bytes 430112 | tf_op jit(solution)/shard_map/ppermute | solution.py:341
  93.4 0.0 collective-permute-done.7.other_ref
  93.4 1.2 copy-done
  94.5 5.0 %project.1 = bf16[8,768,128]{2,1,0:T(8,128)(2,1)} custom-call(s32[2]{0:T(128)S(1)} %pad_add_fusion.where_ref, bf16[2,2,16,24,384]{4,3,2,1,0:T(8,128)(2,1)S(1)} %bitcast.13, bf16[2,2,16,24,384]{4,3,2,1,0:T(8,128)(2,1)} %collective-permute-done.7.other_ref, bf16[1680,128]{1,0:T(8,128)(2,1)S(1)} %copy-done, ...), custom_call_target="tpu_custom_call" | custom-call | tf_op jit(solution)/shard_map/project/pallas_call | solution.py:123
  99.6 0.0 copy-start.8
  99.6 0.0 copy-start.7
  99.6 0.0 copy-start.4
  99.6 3.7 %all-to-all-start.2 = ((bf16[8,768,128]{2,1,0:T(8,128)(2,1)}), bf16[8,768,128]{2,1,0:T(8,128)(2,1)S(1)}, u32[]{:S(2)}, u32[]{:S(2)}) async-start(bf16[8,768,128]{2,1,0:T(8,128)(2,1)} %project.1), calls=%async_computation.2 | async-start | bytes 3145728 | tf_op jit(solution)/shard_map/all_to_all | solution.py:305
  103.4 3.8 %collective-permute-start = (bf16[912,128]{1,0:T(8,128)(2,1)S(1)}, bf16[912,128]{1,0:T(8,128)(2,1)S(1)}, u32[]{:S(2)}, u32[]{:S(2)}) collective-permute-start(bf16[912,128]{1,0:T(8,128)(2,1)S(1)} %copy-done.9), channel_id=1, source_target_pairs={{0,1},{1,0},{2,3},{3,2},{4,5},{5,4},{6,7},{7,6},{8,9},{9,8},{10,11... | collective-permute-start | bytes 700424 | tf_op jit(solution)/shard_map/ppermute | solution.py:341
  107.2 3.4 %collective-permute-start.2 = (bf16[912,128]{1,0:T(8,128)(2,1)S(1)}, bf16[912,128]{1,0:T(8,128)(2,1)S(1)}, u32[]{:S(2)}, u32[]{:S(2)}) collective-permute-start(bf16[912,128]{1,0:T(8,128)(2,1)S(1)} %copy-done.8), channel_id=1, source_target_pairs={{0,3},{1,2},{2,1},{3,0},{4,7},{5,6},{6,5},{7,4},{8,11},{9,10},{10,... | collective-permute-start | bytes 700424 | tf_op jit(solution)/shard_map/ppermute | solution.py:341
  110.6 5.5 %collective-permute-start.4 = (bf16[912,128]{1,0:T(8,128)(2,1)S(1)}, bf16[912,128]{1,0:T(8,128)(2,1)S(1)}, u32[]{:S(2)}, u32[]{:S(2)}) collective-permute-start(bf16[912,128]{1,0:T(8,128)(2,1)S(1)} %copy-done.7), channel_id=1, source_target_pairs={{0,5},{1,4},{2,7},{3,6},{4,1},{5,0},{6,3},{7,2},{8,13},{9,12},{10,... | collective-permute-start | bytes 700424 | tf_op jit(solution)/shard_map/ppermute | solution.py:341
  116.1 2.0 %collective-permute-start.6 = (bf16[912,128]{1,0:T(8,128)(2,1)S(1)}, bf16[912,128]{1,0:T(8,128)(2,1)S(1)}, u32[]{:S(2)}, u32[]{:S(2)}) collective-permute-start(bf16[912,128]{1,0:T(8,128)(2,1)S(1)} %copy-done.6), channel_id=1, source_target_pairs={{0,7},{1,6},{2,5},{3,4},{4,3},{5,2},{6,1},{7,0},{8,15},{9,14},{10,... | collective-permute-start | bytes 700424 | tf_op jit(solution)/shard_map/ppermute | solution.py:341
  118.1 0.2 mask.3.refs_9_
  118.3 0.2 mask.2.refs_8_
  118.5 23.5 %collective-permute-done.refs_1_ = bf16[912,128]{1,0:T(8,128)(2,1)S(1)} collective-permute-done((bf16[912,128]{1,0:T(8,128)(2,1)S(1)}, bf16[912,128]{1,0:T(8,128)(2,1)S(1)}, u32[]{:S(2)}, u32[]{:S(2)}) %collective-permute-start) | collective-permute-done | bytes 233504 | tf_op jit(solution)/shard_map/ppermute | solution.py:341
  142.0 6.9 %score.1 = (bf16[8,912,128]{2,1,0:T(8,128)(2,1)}, f32[6,1024,256]{2,1,0:T(8,128)}) custom-call(s32[1]{0:T(128)} %bitcast.me_ref.where_ref, bf16[1680,128]{1,0:T(8,128)(2,1)S(1)} %copy-done.1, bf16[912,128]{1,0:T(8,128)(2,1)S(1)} %collective-permute-done.refs_1_, bf16[1680,128]{1,0:T(8,128)(2,1)S(1)} %collective-permute-done.1.refs_2_.g1_ref, ...), custom_call_target="tpu_custom_call" | custom-call | tf_op jit(solution)/shard_map/score/pallas_call | solution.py:183
  148.9 1.2 copy-done.5
  150.1 9.3 %attend.1 = bf16[8,704,128]{2,1,0:T(8,128)(2,1)S(1)} custom-call(bf16[8,912,128]{2,1,0:T(8,128)(2,1)} %get-tuple-element.21.in_ref, f32[6,1024,256]{2,1,0:T(8,128)} %get-tuple-element.22.prob_hbm, bf16[8,768,128]{2,1,0:T(8,128)(2,1)} %copy-done.5), custom_call_target="tpu_custom_call" | custom-call | tf_op jit(solution)/shard_map/attend/pallas_call | solution.py:262
  159.4 24.1 %all_to_all.22.in_ref = bf16[8,704,128]{2,1,0:T(8,128)(2,1)S(1)} all-to-all(bf16[8,704,128]{2,1,0:T(8,128)(2,1)S(1)} %attend.1), channel_id=1, replica_groups=mesh['z'=16,'yh'=2,'core'=2,'x'=4,'yl'=2] {'x','yl'}, dimensions={0} | all-to-all | bytes 2883584 | tf_op jit(solution)/shard_map/all_to_all | solution.py:305
  183.5 1.6 merge.1
  (19 shorter events, 0.0 us)
Async XLA Ops:
  55.4 38.0 %collective-permute-start.7 = (bf16[2,2,16,24,384]{4,3,2,1,0:T(8,128)(2,1)S(1)}, bf16[2,2,16,24,384]{4,3,2,1,0:T(8,128)(2,1)}, u32[]{:S(2)}, u32[]{:S(2)}) collective-permute-start(bf16[2,2,16,24,384]{4,3,2,1,0:T(8,128)(2,1)S(1)} %bitcast.12), channel_id=1, source_target_pairs={{0,8},{8,0},{1,9},{9,1},{2,10},{10,2},{3,11},{11,3},{4,12},{12,4},... | collective-permute-start | bytes 3538952 | tf_op jit(solution)/shard_map/ppermute | solution.py:315
  61.0 14.9 %collective-permute-start.1 = (bf16[1680,128]{1,0:T(8,128)(2,1)}, bf16[1680,128]{1,0:T(8,128)(2,1)S(1)}, u32[]{:S(2)}, u32[]{:S(2)}) collective-permute-start(bf16[1680,128]{1,0:T(8,128)(2,1)} %get-tuple-element.15), channel_id=1, source_target_pairs={{0,2},{1,3},{2,0},{3,1},{4,6},{5,7},{6,4},{7,5},{8,10},{9,11},{10,... | collective-permute-start | bytes 1290248 | tf_op jit(solution)/shard_map/ppermute | solution.py:341
  64.4 22.5 %collective-permute-start.3 = (bf16[1680,128]{1,0:T(8,128)(2,1)}, bf16[1680,128]{1,0:T(8,128)(2,1)S(1)}, u32[]{:S(2)}, u32[]{:S(2)}) collective-permute-start(bf16[1680,128]{1,0:T(8,128)(2,1)} %get-tuple-element.17), channel_id=1, source_target_pairs={{0,4},{1,5},{2,6},{3,7},{4,0},{5,1},{6,2},{7,3},{8,12},{9,13},{10,... | collective-permute-start | bytes 1290248 | tf_op jit(solution)/shard_map/ppermute | solution.py:341
  69.1 24.3 %collective-permute-start.5 = (bf16[1680,128]{1,0:T(8,128)(2,1)}, bf16[1680,128]{1,0:T(8,128)(2,1)S(1)}, u32[]{:S(2)}, u32[]{:S(2)}) collective-permute-start(bf16[1680,128]{1,0:T(8,128)(2,1)} %get-tuple-element.19), channel_id=1, source_target_pairs={{0,6},{1,7},{2,4},{3,5},{4,2},{5,3},{6,0},{7,1},{8,14},{9,15},{10,... | collective-permute-start | bytes 1290248 | tf_op jit(solution)/shard_map/ppermute | solution.py:341
  87.0 12.6 %copy-start.2 = (bf16[1680,128]{1,0:T(8,128)(2,1)}, bf16[1680,128]{1,0:T(8,128)(2,1)S(1)}, u32[]{:S(2)}) copy-start(bf16[1680,128]{1,0:T(8,128)(2,1)S(1)} %collective-permute-done.3.refs_4_.g2_ref) | copy-start | bytes 1290244
  93.4 6.2 %copy-start.3 = (bf16[1680,128]{1,0:T(8,128)(2,1)}, bf16[1680,128]{1,0:T(8,128)(2,1)S(1)}, u32[]{:S(2)}) copy-start(bf16[1680,128]{1,0:T(8,128)(2,1)S(1)} %collective-permute-done.5.refs_6_.g3_ref) | copy-start | bytes 1290244
  93.4 1.2 copy-start
  99.6 3.8 %copy-start.9 = (bf16[912,128]{1,0:T(8,128)(2,1)S(1)}, bf16[912,128]{1,0:T(8,128)(2,1)}, u32[]{:S(2)}) copy-start(bf16[912,128]{1,0:T(8,128)(2,1)} %get-tuple-element.14) | copy-start | bytes 700420
  99.6 7.6 %copy-start.8 = (bf16[912,128]{1,0:T(8,128)(2,1)S(1)}, bf16[912,128]{1,0:T(8,128)(2,1)}, u32[]{:S(2)}) copy-start(bf16[912,128]{1,0:T(8,128)(2,1)} %get-tuple-element.16) | copy-start | bytes 700420
  99.6 11.0 %copy-start.7 = (bf16[912,128]{1,0:T(8,128)(2,1)S(1)}, bf16[912,128]{1,0:T(8,128)(2,1)}, u32[]{:S(2)}) copy-start(bf16[912,128]{1,0:T(8,128)(2,1)} %get-tuple-element.18) | copy-start | bytes 700420
  99.6 16.5 %copy-start.6 = (bf16[912,128]{1,0:T(8,128)(2,1)S(1)}, bf16[912,128]{1,0:T(8,128)(2,1)}, u32[]{:S(2)}) copy-start(bf16[912,128]{1,0:T(8,128)(2,1)} %get-tuple-element.20) | copy-start | bytes 700420
  99.6 18.5 %copy-start.4 = (s32[1,12,16,16]{3,2,1,0:T(8,128)S(1)}, s32[1,12,16,16]{3,2,1,0:T(8,128)}, u32[]{:S(2)}) copy-start(s32[1,12,16,16]{3,2,1,0:T(8,128)} %table_ref.3) | copy-start | bytes 36868
  99.6 42.4 %copy-start.1 = (bf16[1680,128]{1,0:T(8,128)(2,1)S(1)}, bf16[1680,128]{1,0:T(8,128)(2,1)}, u32[]{:S(2)}) copy-start(bf16[1680,128]{1,0:T(8,128)(2,1)} %get-tuple-element.13.refs_0_.g0_ref) | copy-start | bytes 1290244
  99.6 49.3 %all-to-all-start.2 = ((bf16[8,768,128]{2,1,0:T(8,128)(2,1)}), bf16[8,768,128]{2,1,0:T(8,128)(2,1)S(1)}, u32[]{:S(2)}, u32[]{:S(2)}) async-start(bf16[8,768,128]{2,1,0:T(8,128)(2,1)} %project.1), calls=%async_computation.2 | async-start | bytes 3145728 | tf_op jit(solution)/shard_map/all_to_all | solution.py:305
  103.4 38.6 %collective-permute-start = (bf16[912,128]{1,0:T(8,128)(2,1)S(1)}, bf16[912,128]{1,0:T(8,128)(2,1)S(1)}, u32[]{:S(2)}, u32[]{:S(2)}) collective-permute-start(bf16[912,128]{1,0:T(8,128)(2,1)S(1)} %copy-done.9), channel_id=1, source_target_pairs={{0,1},{1,0},{2,3},{3,2},{4,5},{5,4},{6,7},{7,6},{8,9},{9,8},{10,11... | collective-permute-start | bytes 700424 | tf_op jit(solution)/shard_map/ppermute | solution.py:341
  107.2 34.8 %collective-permute-start.2 = (bf16[912,128]{1,0:T(8,128)(2,1)S(1)}, bf16[912,128]{1,0:T(8,128)(2,1)S(1)}, u32[]{:S(2)}, u32[]{:S(2)}) collective-permute-start(bf16[912,128]{1,0:T(8,128)(2,1)S(1)} %copy-done.8), channel_id=1, source_target_pairs={{0,3},{1,2},{2,1},{3,0},{4,7},{5,6},{6,5},{7,4},{8,11},{9,10},{10,... | collective-permute-start | bytes 700424 | tf_op jit(solution)/shard_map/ppermute | solution.py:341
  110.6 31.4 %collective-permute-start.4 = (bf16[912,128]{1,0:T(8,128)(2,1)S(1)}, bf16[912,128]{1,0:T(8,128)(2,1)S(1)}, u32[]{:S(2)}, u32[]{:S(2)}) collective-permute-start(bf16[912,128]{1,0:T(8,128)(2,1)S(1)} %copy-done.7), channel_id=1, source_target_pairs={{0,5},{1,4},{2,7},{3,6},{4,1},{5,0},{6,3},{7,2},{8,13},{9,12},{10,... | collective-permute-start | bytes 700424 | tf_op jit(solution)/shard_map/ppermute | solution.py:341
  116.1 25.9 %collective-permute-start.6 = (bf16[912,128]{1,0:T(8,128)(2,1)S(1)}, bf16[912,128]{1,0:T(8,128)(2,1)S(1)}, u32[]{:S(2)}, u32[]{:S(2)}) collective-permute-start(bf16[912,128]{1,0:T(8,128)(2,1)S(1)} %copy-done.6), channel_id=1, source_target_pairs={{0,7},{1,6},{2,5},{3,4},{4,3},{5,2},{6,1},{7,0},{8,15},{9,14},{10,... | collective-permute-start | bytes 700424 | tf_op jit(solution)/shard_map/ppermute | solution.py:341
  148.9 1.2 copy-start.5

commit v5 on v3

--- a/solution.py
+++ b/solution.py
@@ -34,18 +34,18 @@
     return lax.dot_general(a, b, dims, preferred_element_type=F32)
 
 
-def load(sources, targets, sems):
+def start(sources, targets, sems):
     copies = [pltpu.make_async_copy(a, b, sems.at[n]) for n, (a, b) in enumerate(zip(sources, targets, strict=True))]
     for copy in copies:
         copy.start()
-    for copy in copies:
-        copy.wait()
+    return copies
 
 
 def pack_kernel(me_ref, q_hbm, k_hbm, v_hbm, o_hbm, n_hbm, g_hbm, *refs):
     out_refs = refs[:8]
     q_ref, k_ref, v_ref, o_ref, n_ref, g_ref, sems = refs[8:]
-    load((q_hbm, k_hbm, v_hbm, o_hbm, n_hbm, g_hbm), (q_ref, k_ref, v_ref, o_ref, n_ref, g_ref), sems)
+    for copy in start((q_hbm, k_hbm, v_hbm, o_hbm, n_hbm, g_hbm), (q_ref, k_ref, v_ref, o_ref, n_ref, g_ref), sems):
+        copy.wait()
     for d, out_ref in enumerate(out_refs):
         to = jnp.bitwise_xor(me_ref[0], d)
         x, y = to // 2, to % 2
@@ -131,8 +131,8 @@
     )(where, own, other, *slabs)
 
 
-def attend_unit(in_ref, mid_ref, mask_ref, out_ref, dk_ref, dv_ref, per, rows, norm_row, outs):
-    q0, o0, k0, v0, m0 = rows
+def attend_unit(in_ref, g_ref, mask_ref, out_ref, dk_ref, dv_ref, per, rows, norm_row, outs):
+    q0, o0, k0, v0, g0 = rows
     gq0, gk0, gv0 = outs
     group = 256 // per
     keys = 1024
@@ -141,14 +141,7 @@
         sources = range(group * b, group * (b + 1))
         q = jnp.concatenate([in_ref[s, q0 : q0 + per] for s in sources], axis=0)
         o = jnp.concatenate([in_ref[s, o0 : o0 + per] for s in sources], axis=0)
-        pieces = []
-        for s in sources:
-            base = MID * (s // 2) + m0
-            total = mid_ref[s % 2, base : base + per].astype(F32)
-            for x in range(1, 4):
-                total = total + mid_ref[2 * x + s % 2, base : base + per].astype(F32)
-            pieces.append(total.astype(BF))
-        g = jnp.concatenate(pieces, axis=0)
+        g = g_ref[g0 + 256 * b : g0 + 256 * (b + 1)]
         product = g.astype(F32) * o.astype(F32)
         dots = lax.dot_general(
             jnp.ones((8, 128), F32), product, NT_DIMS, precision=lax.Precision.HIGHEST, preferred_element_type=F32
@@ -188,10 +181,19 @@
 
 def attend_kernel(me_ref, *refs):
     sent_refs = refs[:8]
-    mid_ref, mask_a_hbm, mask_c_hbm, out_ref, in_ref, dk_ref, dv_ref, mask_a_ref, mask_c_ref, sems = refs[8:]
+    mid_ref, mask_a_hbm, mask_c_hbm, out_ref, in_ref, g_ref, dk_ref, dv_ref, mask_a_ref, mask_c_ref, sems = refs[8:]
     sources = [ref if d % 2 else ref.at[pl.ds(SLAB, IN_ROWS)] for d, ref in enumerate(sent_refs)]
     targets = [in_ref.at[jnp.bitwise_xor(me_ref[0], d)] for d in range(8)]
-    load((*sources, mask_a_hbm, mask_c_hbm), (*targets, mask_a_ref, mask_c_ref), sems)
+    copies = start((*sources, mask_a_hbm, mask_c_hbm), (*targets, mask_a_ref, mask_c_ref), sems)
+    for per, m0, g0 in ((128, 0, 0), (64, 128, 1024)):
+        for s in range(8):
+            piece = slice(MID * (s // 2) + m0, MID * (s // 2) + m0 + per)
+            total = mid_ref[s % 2, piece].astype(F32)
+            for x in range(1, 4):
+                total = total + mid_ref[2 * x + s % 2, piece].astype(F32)
+            g_ref[g0 + per * s : g0 + per * (s + 1)] = total.astype(BF)
+    for copy in copies:
+        copy.wait()
     second = me_ref[0] % 2 == 1
 
     def norm_a(b):
@@ -206,10 +208,10 @@
         return jnp.concatenate(parts, axis=1) * LOG2E
 
     attend_unit(
-        in_ref, mid_ref, mask_a_ref, out_ref, dk_ref, dv_ref, 128, (QA, OA, KA, VA, 0), norm_a, (GQA, GKA, GVA)
+        in_ref, g_ref, mask_a_ref, out_ref, dk_ref, dv_ref, 128, (QA, OA, KA, VA, 0), norm_a, (GQA, GKA, GVA)
     )
     attend_unit(
-        in_ref, mid_ref, mask_c_ref, out_ref, dk_ref, dv_ref, 64, (QC, OC, KC, VC, 128), norm_c, (GQC, GKC, GVC)
+        in_ref, g_ref, mask_c_ref, out_ref, dk_ref, dv_ref, 64, (QC, OC, KC, VC, 1024), norm_c, (GQC, GKC, GVC)
     )
 
 
@@ -225,6 +227,7 @@
         out_shape=jax.ShapeDtypeStruct((8, OUT_ROWS, 128), BF),
         scratch_shapes=[
             pltpu.VMEM((8, IN_ROWS, 128), BF),
+            pltpu.VMEM((1536, 128), BF),
             pltpu.VMEM((1024, 128), F32),
             pltpu.VMEM((1024, 128), F32),
             pltpu.VMEM((16, 1024), F32),
@@ -307,7 +310,9 @@
     me = (2 * x + y).reshape(1)
     where = jnp.stack([core, x])
     sent = pack(me, q[0], k[0], v[0], o[0], log_norm[0].T, out_grad[0])
-    arrived = [sent[d] if d == 0 else swap(sent[d], d) for d in range(8)]
+    arrived = [sent[d] if d in (0, 4, 5) else swap(sent[d], d) for d in range(8)]
+    arrived[4] = swap(swap(sent[4], 2), 6)
+    arrived[5] = swap(swap(sent[5], 3), 6)
     partial = exchange(project(where, own, other, arrived[::2]), ("x", "yl"))
     mask_a, mask_c = mask_rows(me, tile_mask, False), mask_rows(me, tile_mask, True)
     result = exchange(attend(me, arrived, partial, mask_a, mask_c), ("x", "yl"))

time: 184 us -> 183 us (level)
  waiting for transfers between devices: 45.3 us -> 34.9 us
  starting transfers between devices: 30.7 us -> 39.4 us
    ppermute x7 -> x9, waiting for transfers between devices: 45.3 us -> 34.9 us  [swap(): return lax.ppermute(array, ('x', 'yl'), [(s, s ^ d) for s in range(8)])]
    ppermute x7 -> x9, starting transfers between devices: 25.1 us -> 33.3 us  [swap(): return lax.ppermute(array, ('x', 'yl'), [(s, s ^ d) for s in range(8)])]
    unnamed x30 -> x32, local copies, waits for them, and re-layouts: 8.09 us -> 8.1 us
  transfers between devices with their start and end apart: 9 -> 11, of which waited for: 4 -> 6; matrix products, arithmetic and copies ran while one was open for 0% -> 0% of each run, Pallas kernels for 2% -> 2%
where the time goes in v5:
time: 183 us; the launch traced here: 182 us
  blocking collectives  77.8 us (43%)
  starting transfers between devices  39.4 us (22%)
  waiting for transfers between devices  34.9 us (19%)
  Pallas kernels  19.7 us (11%)
  local copies, waits for them, and re-layouts  8.95 us (5%)
    all_to_all x3, blocking collectives, exchange(): return lax.all_to_all(array, axes, split_axis=0, concat_axis=0, tiled=True)  77.8 us
    ppermute x9, waiting for transfers between devices, swap(): return lax.ppermute(array, ('x', 'yl'), [(s, s ^ d) for s in range(8)])  34.9 us
    ppermute x9, starting transfers between devices, swap(): return lax.ppermute(array, ('x', 'yl'), [(s, s ^ d) for s in range(8)])  33.3 us
    pallas_call x1, Pallas kernels, attend(): pl.pallas_call(attend_kernel, in_specs=[pl.BlockSpec(memory_space=pltpu.S...  8.94 us
    unnamed x32, local copies, waits for them, and re-layouts  8.1 us
    pallas_call x1, Pallas kernels, project(): pl.pallas_call(project_kernel, grid=(4,), in_specs=[pl.BlockSpec(memory_s...  5.03 us
    all_to_all x1, starting transfers between devices, exchange(): return lax.all_to_all(array, axes, split_axis=0, concat_axis=0, tiled=True)  4.18 us
    pallas_call x1, Pallas kernels, pack(): pl.pallas_call(pack_kernel, in_specs=[pl.BlockSpec(memory_space=pltpu.SME...  3.74 us
  transfers between devices with their start and end apart: 11, of which 6 were waited for; matrix products, arithmetic and copies ran while one was open for 0% of the time, Pallas kernels for 2%

profile of v5, /device:TPU:32, one launch (start us, length us, event | category | flops | bytes accessed | tf_op | source)
XLA Modules:
  0.0 181.6 jit_solution(2324849282892041103)
XLA Ops:
  0.6 0.7 broadcast_in_dim.4
  1.4 33.8 %all_to_all.20 = bf16[16,24,384]{2,1,0:T(8,128)(2,1)S(1)} all-to-all(bf16[16,24,384]{2,1,0:T(8,128)(2,1)S(1)} %broadcast_in_dim.4), channel_id=1, replica_groups=mesh['z'=16,'yh'=2,'core'=2,'x'=4,'yl'=2] {'z'}, dimensions={0} | all-to-all | bytes 589824 | tf_op jit(solution)/shard_map/all_to_all | solution.py:269
  35.3 20.1 %all_to_all.21 = bf16[4,16,24,384]{3,2,1,0:T(8,128)(2,1)S(1)} all-to-all(bf16[4,16,24,384]{3,2,1,0:T(8,128)(2,1)S(1)} %broadcast_in_dim.5), channel_id=1, replica_groups=mesh['z'=16,'yh'=2,'core'=2,'x'=4,'yl'=2] {'yh','yl'}, dimensions={0} | all-to-all | bytes 2359296 | tf_op jit(solution)/shard_map/all_to_all | solution.py:269
  55.4 1.9 %collective-permute-start.9 = (bf16[2,2,16,24,384]{4,3,2,1,0:T(8,128)(2,1)S(1)}, bf16[2,2,16,24,384]{4,3,2,1,0:T(8,128)(2,1)}, u32[]{:S(2)}, u32[]{:S(2)}) collective-permute-start(bf16[2,2,16,24,384]{4,3,2,1,0:T(8,128)(2,1)S(1)} %bitcast.12), channel_id=1, source_target_pairs={{0,8},{8,0},{1,9},{9,1},{2,10},{10,2},{3,11},{11,3},{4,12},{12,4},... | collective-permute-start | bytes 3538952 | tf_op jit(solution)/shard_map/ppermute | solution.py:279
  57.3 3.7 %pack.1 = (bf16[1680,128]{1,0:T(8,128)(2,1)}, bf16[912,128]{1,0:T(8,128)(2,1)}, bf16[1680,128]{1,0:T(8,128)(2,1)}, bf16[912,128]{1,0:T(8,128)(2,1)}, bf16[1680,1...) custom-call(s32[1]{0:T(128)} %bitcast.me_ref.where_ref, ...), custom_call_target="tpu_custom_call" | custom-call | tf_op jit(solution)/shard_map/pack/pallas_call | solution.py:75
  61.1 3.4 %collective-permute-start.3 = (bf16[1680,128]{1,0:T(8,128)(2,1)}, bf16[1680,128]{1,0:T(8,128)(2,1)S(1)}, u32[]{:S(2)}, u32[]{:S(2)}) collective-permute-start(bf16[1680,128]{1,0:T(8,128)(2,1)} %get-tuple-element.15), channel_id=1, source_target_pairs={{0,2},{1,3},{2,0},{3,1},{4,6},{5,7},{6,4},{7,5},{8,10},{9,11},{10,... | collective-permute-start | bytes 1290248 | tf_op jit(solution)/shard_map/ppermute | solution.py:305
  64.5 2.4 %collective-permute-start.1 = (bf16[1680,128]{1,0:T(8,128)(2,1)}, bf16[1680,128]{1,0:T(8,128)(2,1)S(1)}, u32[]{:S(2)}, u32[]{:S(2)}) collective-permute-start(bf16[1680,128]{1,0:T(8,128)(2,1)} %get-tuple-element.13), channel_id=1, source_target_pairs={{0,2},{1,3},{2,0},{3,1},{4,6},{5,7},{6,4},{7,5},{8,10},{9,11},{10,... | collective-permute-start | bytes 1290248 | tf_op jit(solution)/shard_map/ppermute | solution.py:305
  66.9 4.7 %collective-permute-start.7 = (bf16[1680,128]{1,0:T(8,128)(2,1)}, bf16[1680,128]{1,0:T(8,128)(2,1)S(1)}, u32[]{:S(2)}, u32[]{:S(2)}) collective-permute-start(bf16[1680,128]{1,0:T(8,128)(2,1)} %get-tuple-element.17), channel_id=1, source_target_pairs={{0,6},{1,7},{2,4},{3,5},{4,2},{5,3},{6,0},{7,1},{8,14},{9,15},{10,... | collective-permute-start | bytes 1290248 | tf_op jit(solution)/shard_map/ppermute | solution.py:305
  71.6 4.4 %collective-permute-done.3 = bf16[1680,128]{1,0:T(8,128)(2,1)S(1)} collective-permute-done((bf16[1680,128]{1,0:T(8,128)(2,1)}, bf16[1680,128]{1,0:T(8,128)(2,1)S(1)}, u32[]{:S(2)}, u32[]{:S(2)}) %collective-permute-start.3) | collective-permute-done | bytes 430112 | tf_op jit(solution)/shard_map/ppermute | solution.py:305
  75.9 4.7 %collective-permute-start.4 = (bf16[1680,128]{1,0:T(8,128)(2,1)S(1)}, bf16[1680,128]{1,0:T(8,128)(2,1)S(1)}, u32[]{:S(2)}, u32[]{:S(2)}) collective-permute-start(bf16[1680,128]{1,0:T(8,128)(2,1)S(1)} %collective-permute-done.3), channel_id=1, source_target_pairs={{0,6},{1,7},{2,4},{3,5},{4,2},{5,3},{6,0},{7,1},{8,14},{9,15},{10,... | collective-permute-start | bytes 1290248 | tf_op jit(solution)/shard_map/ppermute | solution.py:305
  80.7 4.0 %collective-permute-done.1.g1_ref.refs_2_ = bf16[1680,128]{1,0:T(8,128)(2,1)S(1)} collective-permute-done((bf16[1680,128]{1,0:T(8,128)(2,1)}, bf16[1680,128]{1,0:T(8,128)(2,1)S(1)}, u32[]{:S(2)}, u32[]{:S(2)}) %collective-permute-start.1) | collective-permute-done | bytes 430112 | tf_op jit(solution)/shard_map/ppermute | solution.py:305
  84.7 6.5 %collective-permute-done.4.g2_ref.refs_4_ = bf16[1680,128]{1,0:T(8,128)(2,1)S(1)} collective-permute-done((bf16[1680,128]{1,0:T(8,128)(2,1)S(1)}, bf16[1680,128]{1,0:T(8,128)(2,1)S(1)}, u32[]{:S(2)}, u32[]{:S(2)}) %collective-permute-start.4) | collective-permute-done | bytes 430112 | tf_op jit(solution)/shard_map/ppermute | solution.py:305
  91.2 1.2 copy-done
  92.4 5.0 %project.1 = bf16[8,768,128]{2,1,0:T(8,128)(2,1)} custom-call(s32[2]{0:T(128)S(1)} %pad_add_fusion.where_ref, bf16[2,2,16,24,384]{4,3,2,1,0:T(8,128)(2,1)S(1)} %bitcast.13, bf16[2,2,16,24,384]{4,3,2,1,0:T(8,128)(2,1)} %collective-permute-done.9.other_ref, bf16[1680,128]{1,0:T(8,128)(2,1)S(1)} %copy-done, ...), custom_call_target="tpu_custom_call" | custom-call | tf_op jit(solution)/shard_map/project/pallas_call | solution.py:122
  97.4 4.2 %all-to-all-start.2 = ((bf16[8,768,128]{2,1,0:T(8,128)(2,1)}), bf16[8,768,128]{2,1,0:T(8,128)(2,1)S(1)}, u32[]{:S(2)}, u32[]{:S(2)}) async-start(bf16[8,768,128]{2,1,0:T(8,128)(2,1)} %project.1), calls=%async_computation.2 | async-start | bytes 3145728 | tf_op jit(solution)/shard_map/all_to_all | solution.py:269
  101.6 4.8 %collective-permute-start.5 = (bf16[912,128]{1,0:T(8,128)(2,1)S(1)}, bf16[912,128]{1,0:T(8,128)(2,1)S(1)}, u32[]{:S(2)}, u32[]{:S(2)}) collective-permute-start(bf16[912,128]{1,0:T(8,128)(2,1)S(1)} %copy-done.15), channel_id=1, source_target_pairs={{0,3},{1,2},{2,1},{3,0},{4,7},{5,6},{6,5},{7,4},{8,11},{9,10},{10,... | collective-permute-start | bytes 700424 | tf_op jit(solution)/shard_map/ppermute | solution.py:305
  106.5 2.5 %collective-permute-start = (bf16[912,128]{1,0:T(8,128)(2,1)}, bf16[912,128]{1,0:T(8,128)(2,1)S(1)}, u32[]{:S(2)}, u32[]{:S(2)}) collective-permute-start(bf16[912,128]{1,0:T(8,128)(2,1)} %get-tuple-element.12), channel_id=1, source_target_pairs={{0,1},{1,0},{2,3},{3,2},{4,5},{5,4},{6,7},{7,6},{8,9},{9,8},{10,11... | collective-permute-start | bytes 700424 | tf_op jit(solution)/shard_map/ppermute | solution.py:305
  108.9 3.4 %collective-permute-start.2 = (bf16[912,128]{1,0:T(8,128)(2,1)S(1)}, bf16[912,128]{1,0:T(8,128)(2,1)S(1)}, u32[]{:S(2)}, u32[]{:S(2)}) collective-permute-start(bf16[912,128]{1,0:T(8,128)(2,1)S(1)} %copy-done.14), channel_id=1, source_target_pairs={{0,3},{1,2},{2,1},{3,0},{4,7},{5,6},{6,5},{7,4},{8,11},{9,10},{10,... | collective-permute-start | bytes 700424 | tf_op jit(solution)/shard_map/ppermute | solution.py:305
  112.3 4.6 %collective-permute-start.8 = (bf16[912,128]{1,0:T(8,128)(2,1)S(1)}, bf16[912,128]{1,0:T(8,128)(2,1)S(1)}, u32[]{:S(2)}, u32[]{:S(2)}) collective-permute-start(bf16[912,128]{1,0:T(8,128)(2,1)S(1)} %copy-done.13), channel_id=1, source_target_pairs={{0,7},{1,6},{2,5},{3,4},{4,3},{5,2},{6,1},{7,0},{8,15},{9,14},{10,... | collective-permute-start | bytes 700424 | tf_op jit(solution)/shard_map/ppermute | solution.py:305
  116.9 15.6 %collective-permute-done.5 = bf16[912,128]{1,0:T(8,128)(2,1)S(1)} collective-permute-done((bf16[912,128]{1,0:T(8,128)(2,1)S(1)}, bf16[912,128]{1,0:T(8,128)(2,1)S(1)}, u32[]{:S(2)}, u32[]{:S(2)}) %collective-permute-start.5) | collective-permute-done | bytes 233504 | tf_op jit(solution)/shard_map/ppermute | solution.py:305
  132.5 2.9 %collective-permute-start.6 = (bf16[912,128]{1,0:T(8,128)(2,1)S(1)}, bf16[912,128]{1,0:T(8,128)(2,1)S(1)}, u32[]{:S(2)}, u32[]{:S(2)}) collective-permute-start(bf16[912,128]{1,0:T(8,128)(2,1)S(1)} %collective-permute-done.5), channel_id=1, source_target_pairs={{0,6},{1,7},{2,4},{3,5},{4,2},{5,3},{6,0},{7,1},{8,14},{9,15},{10,... | collective-permute-start | bytes 700424 | tf_op jit(solution)/shard_map/ppermute | solution.py:305
  135.8 4.4 %collective-permute-done.refs_1_ = bf16[912,128]{1,0:T(8,128)(2,1)S(1)} collective-permute-done((bf16[912,128]{1,0:T(8,128)(2,1)}, bf16[912,128]{1,0:T(8,128)(2,1)S(1)}, u32[]{:S(2)}, u32[]{:S(2)}) %collective-permute-start) | collective-permute-done | bytes 233504 | tf_op jit(solution)/shard_map/ppermute | solution.py:305
  140.2 0.7 copy-done.7
  140.8 0.7 copy-done.9
  142.3 1.0 copy-done.3
  143.3 1.0 copy-done.5
  144.4 0.9 copy-done.8
  145.3 0.9 copy-done.10
  146.2 0.9 copy-done.12
  147.2 8.9 %attend.1 = bf16[8,704,128]{2,1,0:T(8,128)(2,1)S(1)} custom-call(s32[1]{0:T(128)} %bitcast.me_ref.where_ref, bf16[1680,128]{1,0:T(8,128)(2,1)S(1)} %copy-done.1, bf16[912,128]{1,0:T(8,128)(2,1)S(1)} %collective-permute-done.refs_1_, bf16[1680,128]{1,0:T(8,128)(2,1)S(1)} %collective-permute-done.1.g1_ref.refs_2_, bf16[912,128]{1,0:T(8,128)(2,1)S(1)} %copy-done.8, ...), custom_call_target="tpu_custom_call" | custom-call | tf_op jit(solution)/shard_map/attend/pallas_call | solution.py:220
  156.1 23.9 %all_to_all.22.in_ref = bf16[8,704,128]{2,1,0:T(8,128)(2,1)S(1)} all-to-all(bf16[8,704,128]{2,1,0:T(8,128)(2,1)S(1)} %attend.1), channel_id=1, replica_groups=mesh['z'=16,'yh'=2,'core'=2,'x'=4,'yl'=2] {'x','yl'}, dimensions={0} | all-to-all | bytes 2883584 | tf_op jit(solution)/shard_map/all_to_all | solution.py:269
  180.0 1.6 merge.1
  (34 shorter events, 1.4 us)
Async XLA Ops:
  55.4 35.8 %collective-permute-start.9 = (bf16[2,2,16,24,384]{4,3,2,1,0:T(8,128)(2,1)S(1)}, bf16[2,2,16,24,384]{4,3,2,1,0:T(8,128)(2,1)}, u32[]{:S(2)}, u32[]{:S(2)}) collective-permute-start(bf16[2,2,16,24,384]{4,3,2,1,0:T(8,128)(2,1)S(1)} %bitcast.12), channel_id=1, source_target_pairs={{0,8},{8,0},{1,9},{9,1},{2,10},{10,2},{3,11},{11,3},{4,12},{12,4},... | collective-permute-start | bytes 3538952 | tf_op jit(solution)/shard_map/ppermute | solution.py:279
  61.1 14.9 %collective-permute-start.3 = (bf16[1680,128]{1,0:T(8,128)(2,1)}, bf16[1680,128]{1,0:T(8,128)(2,1)S(1)}, u32[]{:S(2)}, u32[]{:S(2)}) collective-permute-start(bf16[1680,128]{1,0:T(8,128)(2,1)} %get-tuple-element.15), channel_id=1, source_target_pairs={{0,2},{1,3},{2,0},{3,1},{4,6},{5,7},{6,4},{7,5},{8,10},{9,11},{10,... | collective-permute-start | bytes 1290248 | tf_op jit(solution)/shard_map/ppermute | solution.py:305
  64.5 20.2 %collective-permute-start.1 = (bf16[1680,128]{1,0:T(8,128)(2,1)}, bf16[1680,128]{1,0:T(8,128)(2,1)S(1)}, u32[]{:S(2)}, u32[]{:S(2)}) collective-permute-start(bf16[1680,128]{1,0:T(8,128)(2,1)} %get-tuple-element.13), channel_id=1, source_target_pairs={{0,2},{1,3},{2,0},{3,1},{4,6},{5,7},{6,4},{7,5},{8,10},{9,11},{10,... | collective-permute-start | bytes 1290248 | tf_op jit(solution)/shard_map/ppermute | solution.py:305
  66.9 17.8 %collective-permute-start.7 = (bf16[1680,128]{1,0:T(8,128)(2,1)}, bf16[1680,128]{1,0:T(8,128)(2,1)S(1)}, u32[]{:S(2)}, u32[]{:S(2)}) collective-permute-start(bf16[1680,128]{1,0:T(8,128)(2,1)} %get-tuple-element.17), channel_id=1, source_target_pairs={{0,6},{1,7},{2,4},{3,5},{4,2},{5,3},{6,0},{7,1},{8,14},{9,15},{10,... | collective-permute-start | bytes 1290248 | tf_op jit(solution)/shard_map/ppermute | solution.py:305
  75.9 15.3 %collective-permute-start.4 = (bf16[1680,128]{1,0:T(8,128)(2,1)S(1)}, bf16[1680,128]{1,0:T(8,128)(2,1)S(1)}, u32[]{:S(2)}, u32[]{:S(2)}) collective-permute-start(bf16[1680,128]{1,0:T(8,128)(2,1)S(1)} %collective-permute-done.3), channel_id=1, source_target_pairs={{0,6},{1,7},{2,4},{3,5},{4,2},{5,3},{6,0},{7,1},{8,14},{9,15},{10,... | collective-permute-start | bytes 1290248 | tf_op jit(solution)/shard_map/ppermute | solution.py:305
  84.7 12.7 %copy-start.2 = (bf16[1680,128]{1,0:T(8,128)(2,1)}, bf16[1680,128]{1,0:T(8,128)(2,1)S(1)}, u32[]{:S(2)}) copy-start(bf16[1680,128]{1,0:T(8,128)(2,1)S(1)} %collective-permute-done.7.g3_ref.refs_6_) | copy-start | bytes 1290244
  91.2 6.2 %copy-start.4 = (bf16[1680,128]{1,0:T(8,128)(2,1)}, bf16[1680,128]{1,0:T(8,128)(2,1)S(1)}, u32[]{:S(2)}) copy-start(bf16[1680,128]{1,0:T(8,128)(2,1)S(1)} %collective-permute-done.4.g2_ref.refs_4_) | copy-start | bytes 1290244
  91.2 1.2 copy-start
  97.4 4.2 %copy-start.15 = (bf16[912,128]{1,0:T(8,128)(2,1)S(1)}, bf16[912,128]{1,0:T(8,128)(2,1)}, u32[]{:S(2)}) copy-start(bf16[912,128]{1,0:T(8,128)(2,1)} %get-tuple-element.16) | copy-start | bytes 700420
  97.4 11.5 %copy-start.14 = (bf16[912,128]{1,0:T(8,128)(2,1)S(1)}, bf16[912,128]{1,0:T(8,128)(2,1)}, u32[]{:S(2)}) copy-start(bf16[912,128]{1,0:T(8,128)(2,1)} %get-tuple-element.14) | copy-start | bytes 700420
  97.4 14.9 %copy-start.13 = (bf16[912,128]{1,0:T(8,128)(2,1)S(1)}, bf16[912,128]{1,0:T(8,128)(2,1)}, u32[]{:S(2)}) copy-start(bf16[912,128]{1,0:T(8,128)(2,1)} %get-tuple-element.18) | copy-start | bytes 700420
  97.4 38.0 %copy-start.6 = (s32[1,12,16,16]{3,2,1,0:T(8,128)S(1)}, s32[1,12,16,16]{3,2,1,0:T(8,128)}, u32[]{:S(2)}) copy-start(s32[1,12,16,16]{3,2,1,0:T(8,128)} %table_ref.3) | copy-start | bytes 36868
  97.4 44.9 %copy-start.1 = (bf16[1680,128]{1,0:T(8,128)(2,1)S(1)}, bf16[1680,128]{1,0:T(8,128)(2,1)}, u32[]{:S(2)}) copy-start(bf16[1680,128]{1,0:T(8,128)(2,1)} %get-tuple-element.11.g0_ref.refs_0_) | copy-start | bytes 1290244
  97.4 44.9 %all-to-all-start.2 = ((bf16[8,768,128]{2,1,0:T(8,128)(2,1)}), bf16[8,768,128]{2,1,0:T(8,128)(2,1)S(1)}, u32[]{:S(2)}, u32[]{:S(2)}) async-start(bf16[8,768,128]{2,1,0:T(8,128)(2,1)} %project.1), calls=%async_computation.2 | async-start | bytes 3145728 | tf_op jit(solution)/shard_map/all_to_all | solution.py:269
  101.6 30.8 %collective-permute-start.5 = (bf16[912,128]{1,0:T(8,128)(2,1)S(1)}, bf16[912,128]{1,0:T(8,128)(2,1)S(1)}, u32[]{:S(2)}, u32[]{:S(2)}) collective-permute-start(bf16[912,128]{1,0:T(8,128)(2,1)S(1)} %copy-done.15), channel_id=1, source_target_pairs={{0,3},{1,2},{2,1},{3,0},{4,7},{5,6},{6,5},{7,4},{8,11},{9,10},{10,... | collective-permute-start | bytes 700424 | tf_op jit(solution)/shard_map/ppermute | solution.py:305
  106.5 33.7 %collective-permute-start = (bf16[912,128]{1,0:T(8,128)(2,1)}, bf16[912,128]{1,0:T(8,128)(2,1)S(1)}, u32[]{:S(2)}, u32[]{:S(2)}) collective-permute-start(bf16[912,128]{1,0:T(8,128)(2,1)} %get-tuple-element.12), channel_id=1, source_target_pairs={{0,1},{1,0},{2,3},{3,2},{4,5},{5,4},{6,7},{7,6},{8,9},{9,8},{10,11... | collective-permute-start | bytes 700424 | tf_op jit(solution)/shard_map/ppermute | solution.py:305
  108.9 31.2 %collective-permute-start.2 = (bf16[912,128]{1,0:T(8,128)(2,1)S(1)}, bf16[912,128]{1,0:T(8,128)(2,1)S(1)}, u32[]{:S(2)}, u32[]{:S(2)}) collective-permute-start(bf16[912,128]{1,0:T(8,128)(2,1)S(1)} %copy-done.14), channel_id=1, source_target_pairs={{0,3},{1,2},{2,1},{3,0},{4,7},{5,6},{6,5},{7,4},{8,11},{9,10},{10,... | collective-permute-start | bytes 700424 | tf_op jit(solution)/shard_map/ppermute | solution.py:305
  112.3 28.5 %collective-permute-start.8 = (bf16[912,128]{1,0:T(8,128)(2,1)S(1)}, bf16[912,128]{1,0:T(8,128)(2,1)S(1)}, u32[]{:S(2)}, u32[]{:S(2)}) collective-permute-start(bf16[912,128]{1,0:T(8,128)(2,1)S(1)} %copy-done.13), channel_id=1, source_target_pairs={{0,7},{1,6},{2,5},{3,4},{4,3},{5,2},{6,1},{7,0},{8,15},{9,14},{10,... | collective-permute-start | bytes 700424 | tf_op jit(solution)/shard_map/ppermute | solution.py:305
  132.5 9.2 %collective-permute-start.6 = (bf16[912,128]{1,0:T(8,128)(2,1)S(1)}, bf16[912,128]{1,0:T(8,128)(2,1)S(1)}, u32[]{:S(2)}, u32[]{:S(2)}) collective-permute-start(bf16[912,128]{1,0:T(8,128)(2,1)S(1)} %collective-permute-done.5), channel_id=1, source_target_pairs={{0,6},{1,7},{2,4},{3,5},{4,2},{5,3},{6,0},{7,1},{8,14},{9,15},{10,... | collective-permute-start | bytes 700424 | tf_op jit(solution)/shard_map/ppermute | solution.py:305
  140.2 0.7 copy-start.7
  140.8 0.7 copy-start.9
  141.6 0.7 copy-start.11
  142.3 1.0 copy-start.3
  143.3 1.0 copy-start.5
  144.3 0.9 copy-start.8
  145.3 0.9 copy-start.10
  146.2 0.9 copy-start.12

commit v6 on v5

--- a/solution.py
+++ b/solution.py
@@ -21,7 +21,6 @@
 SLAB = 768
 GRANT = 16 << 20
 WHOLE_GRANT = 62 << 20
-MID = 192
 GQA, GKA, GVA, GKC, GVC, GQC = 0, 128, 256, 384, 512, 640
 OUT_ROWS = 704
 
@@ -88,47 +87,67 @@
     )(me, q, k, v, o, norms, out_grad)
 
 
-def project_kernel(where_ref, own_ref, other_ref, g0_ref, g1_ref, g2_ref, g3_ref, out_ref, w_ref, g_ref):
-    @pl.when(pl.program_id(0) == 0)
-    def _():
-        for e, ref in enumerate((g0_ref, g1_ref, g2_ref, g3_ref)):
-            source = jnp.bitwise_xor(where_ref[1], e)
-            for n in range(6):
-                g_ref[source, :, 128 * n : 128 * (n + 1)] = ref[128 * n : 128 * (n + 1)]
-
-    mine = where_ref[0] == 0
-    for z in range(4):
-        for yh in range(2):
-            for yl in range(2):
-                a = own_ref[yh, yl, z]
-                b = other_ref[yh, yl, z]
-                for c in range(2):
-                    row = 24 * (4 * z + 2 * yh + c)
-                    piece = jnp.where(mine, a, b) if c == 0 else jnp.where(mine, b, a)
-                    w_ref[row : row + 24, 384 * yl : 384 * (yl + 1)] = piece
-    g = g_ref[...].reshape(512, 768)
-    part = dot(g, w_ref[...], NT_DIMS).astype(BF)
+def product(shard_ref, g, yh):
+    return dot(shard_ref[yh, 0], g[:, :384], NT_DIMS) + dot(shard_ref[yh, 1], g[:, 384:], NT_DIMS)
+
+
+def project_own_kernel(where_ref, own_ref, g0_ref, g1_ref, g2_ref, g3_ref, part_ref, g_ref):
+    for e, ref in enumerate((g0_ref, g1_ref, g2_ref, g3_ref)):
+        rows = pl.ds(pl.multiple_of(128 * jnp.bitwise_xor(where_ref[1], e), 128), 128)
+        for n in range(6):
+            g_ref[rows, 128 * n : 128 * (n + 1)] = ref[128 * n : 128 * (n + 1)]
+    for yh in range(2):
+        part_ref[yh] = product(own_ref, g_ref[...], yh)
+
+
+def project_own(where, own, slabs):
+    whole = pl.BlockSpec(memory_space=pltpu.VMEM)
+    slab = pl.BlockSpec((SLAB, 128), lambda i: (0, 0))
+    return pl.pallas_call(
+        project_own_kernel,
+        grid=(1,),
+        in_specs=[pl.BlockSpec(memory_space=pltpu.SMEM), whole] + [slab] * 4,
+        out_specs=(whole, whole),
+        out_shape=(jax.ShapeDtypeStruct((2, 384, 512), F32), jax.ShapeDtypeStruct((512, 768), BF)),
+        compiler_params=pltpu.CompilerParams(vmem_limit_bytes=GRANT),
+        name="project_own",
+    )(where, own, *slabs)
+
+
+def project_kernel(where_ref, part_ref, other_ref, g_ref, out_ref, t_ref):
+    core = where_ref[0]
+    for yh in range(2):
+        for c, part in ((core, part_ref[yh]), (1 - core, product(other_ref, g_ref[...], yh))):
+            for z in range(16):
+                rows = pl.ds(pl.multiple_of(24 * c + (96 * z + 48 * yh), 8), 24)
+                t_ref[rows] = part[24 * z : 24 * (z + 1)]
     for x in range(4):
-        rows = slice(128 * x, 128 * (x + 1))
         for j in range(2):
-            base = MID * x
-            out_ref[j, base : base + 128] = part[rows, HD * j : HD * (j + 1)]
-            out_ref[j, base + 128 : base + MID] = part[128 * x + 64 * j : 128 * x + 64 * (j + 1), 2 * HD :]
-
-
-def project(where, own, other, slabs):
-    shard = pl.BlockSpec((2, 2, 4, 24, 384), lambda i: (0, 0, i, 0, 0))
-    slab = pl.BlockSpec((SLAB, 128), lambda i: (0, 0))
+            head = 3 * x + j
+            block = t_ref[128 * head : 128 * (head + 1)].astype(BF)
+            for n in range(4):
+                out_ref[2 * x + j, 128 * n : 128 * (n + 1)] = block[:, 128 * n : 128 * (n + 1)]
+        head = 3 * x + 2
+        block = t_ref[128 * head : 128 * (head + 1)].astype(BF)
+        for j in range(2):
+            for e in range(2):
+                at = 256 * e + 64 * j
+                out_ref[2 * x + j, 512 + 128 * e : 640 + 128 * e] = jnp.concatenate(
+                    [block[:, at : at + 64], block[:, at + 128 : at + 192]], axis=1
+                )
+
+
+def project(where, part, other, g):
+    whole = pl.BlockSpec(memory_space=pltpu.VMEM)
     return pl.pallas_call(
         project_kernel,
-        grid=(4,),
-        in_specs=[pl.BlockSpec(memory_space=pltpu.SMEM), shard, shard] + [slab] * 4,
-        out_specs=pl.BlockSpec((2, 4 * MID, 128), lambda i: (i, 0, 0)),
-        out_shape=jax.ShapeDtypeStruct((8, 4 * MID, 128), BF),
-        scratch_shapes=[pltpu.VMEM((384, 768), BF), pltpu.VMEM((4, 128, 768), BF)],
+        in_specs=[pl.BlockSpec(memory_space=pltpu.SMEM), whole, whole, whole],
+        out_specs=whole,
+        out_shape=jax.ShapeDtypeStruct((8, 768, 128), BF),
+        scratch_shapes=[pltpu.VMEM((1536, 512), F32)],
         compiler_params=pltpu.CompilerParams(vmem_limit_bytes=GRANT),
         name="project",
-    )(where, own, other, *slabs)
+    )(where, part, other, g)
 
 
 def attend_unit(in_ref, g_ref, mask_ref, out_ref, dk_ref, dv_ref, per, rows, norm_row, outs):
@@ -185,13 +204,19 @@
     sources = [ref if d % 2 else ref.at[pl.ds(SLAB, IN_ROWS)] for d, ref in enumerate(sent_refs)]
     targets = [in_ref.at[jnp.bitwise_xor(me_ref[0], d)] for d in range(8)]
     copies = start((*sources, mask_a_hbm, mask_c_hbm), (*targets, mask_a_ref, mask_c_ref), sems)
-    for per, m0, g0 in ((128, 0, 0), (64, 128, 1024)):
-        for s in range(8):
-            piece = slice(MID * (s // 2) + m0, MID * (s // 2) + m0 + per)
-            total = mid_ref[s % 2, piece].astype(F32)
+    for y in range(2):
+        for n in range(6):
+            total = mid_ref[y, 128 * n : 128 * (n + 1)].astype(F32)
             for x in range(1, 4):
-                total = total + mid_ref[2 * x + s % 2, piece].astype(F32)
-            g_ref[g0 + per * s : g0 + per * (s + 1)] = total.astype(BF)
+                total = total + mid_ref[2 * x + y, 128 * n : 128 * (n + 1)].astype(F32)
+            total = total.astype(BF).T
+            if n < 4:
+                at = 128 * (2 * n + y)
+                g_ref[at : at + 128] = total
+            else:
+                for e in range(2):
+                    at = 1024 + 64 * (4 * (n - 4) + 2 * e + y)
+                    g_ref[at : at + 64] = total[64 * e : 64 * (e + 1)]
     for copy in copies:
         copy.wait()
     second = me_ref[0] % 2 == 1
@@ -275,7 +300,7 @@
 
 def gather_weight(proj_weight):
     own = spread(proj_weight, "z", 16)
-    own = spread(own, ("yh", "yl"), 4).reshape(2, 2, 16, 24, 384)
+    own = spread(own, ("yh", "yl"), 4).reshape(2, 2, 384, 384)
     other = lax.ppermute(own, "core", [(0, 1), (1, 0)])
     return own, other
 
@@ -311,9 +336,10 @@
     where = jnp.stack([core, x])
     sent = pack(me, q[0], k[0], v[0], o[0], log_norm[0].T, out_grad[0])
     arrived = [sent[d] if d in (0, 4, 5) else swap(sent[d], d) for d in range(8)]
-    arrived[4] = swap(swap(sent[4], 2), 6)
+    arrived[4] = swap(swap(sent[4], 6), 2)
     arrived[5] = swap(swap(sent[5], 3), 6)
-    partial = exchange(project(where, own, other, arrived[::2]), ("x", "yl"))
+    part, slab = project_own(where, own, arrived[::2])
+    partial = exchange(project(where, part, other, slab), ("x", "yl"))
     mask_a, mask_c = mask_rows(me, tile_mask, False), mask_rows(me, tile_mask, True)
     result = exchange(attend(me, arrived, partial, mask_a, mask_c), ("x", "yl"))
     return merge(result)

time: 183 us -> 180 us (0.984)
  starting transfers between devices: 39.4 us -> 36.5 us
    ppermute x9, starting transfers between devices: 33.3 us -> 30.4 us  [swap(): return lax.ppermute(array, ('x', 'yl'), [(s, s ^ d) for s in range(8)])]
    unnamed x32 -> x28, local copies, waits for them, and re-layouts: 8.1 us -> 7.07 us
    pallas_call x1 -> x2, Pallas kernels: 5.03 us -> 5.4 us  [the longest x1 3.73 us: project(): pl.pallas_call(project_kernel, in_specs=[pl.BlockSpec(memory_space=pltpu....]
  transfers between devices with their start and end apart: 11 -> 11, of which waited for: 6 -> 6; matrix products, arithmetic and copies ran while one was open for 0% -> 0% of each run, Pallas kernels for 2% -> 3%
where the time goes in v6:
time: 180 us; the launch traced here: 179 us
  blocking collectives  77.6 us (43%)
  starting transfers between devices  36.5 us (20%)
  waiting for transfers between devices  36.1 us (20%)
  Pallas kernels  20.1 us (11%)
  local copies, waits for them, and re-layouts  7.92 us (4%)
    all_to_all x3, blocking collectives, exchange(): return lax.all_to_all(array, axes, split_axis=0, concat_axis=0, tiled=True)  77.6 us
    ppermute x9, waiting for transfers between devices, swap(): return lax.ppermute(array, ('x', 'yl'), [(s, s ^ d) for s in range(8)])  36.1 us
    ppermute x9, starting transfers between devices, swap(): return lax.ppermute(array, ('x', 'yl'), [(s, s ^ d) for s in range(8)])  30.4 us
    pallas_call x1, Pallas kernels, attend(): pl.pallas_call(attend_kernel, in_specs=[pl.BlockSpec(memory_space=pltpu.S...  9.01 us
    unnamed x28, local copies, waits for them, and re-layouts  7.07 us
    all_to_all x1, starting transfers between devices, exchange(): return lax.all_to_all(array, axes, split_axis=0, concat_axis=0, tiled=True)  4.18 us
    pallas_call x1, Pallas kernels, project(): pl.pallas_call(project_kernel, in_specs=[pl.BlockSpec(memory_space=pltpu....  3.73 us
    pallas_call x1, Pallas kernels, pack(): pl.pallas_call(pack_kernel, in_specs=[pl.BlockSpec(memory_space=pltpu.SME...  3.71 us
  transfers between devices with their start and end apart: 11, of which 6 were waited for; matrix products, arithmetic and copies ran while one was open for 0% of the time, Pallas kernels for 3%

profile of v6, /device:TPU:32, one launch (start us, length us, event | category | flops | bytes accessed | tf_op | source)
XLA Modules:
  0.0 179.1 jit_solution(15233322467377990838)
XLA Ops:
  0.6 0.7 broadcast_in_dim.4
  1.4 33.8 %all_to_all.20 = bf16[16,24,384]{2,1,0:T(8,128)(2,1)S(1)} all-to-all(bf16[16,24,384]{2,1,0:T(8,128)(2,1)S(1)} %broadcast_in_dim.4), channel_id=1, replica_groups=mesh['z'=16,'yh'=2,'core'=2,'x'=4,'yl'=2] {'z'}, dimensions={0} | all-to-all | bytes 589824 | tf_op jit(solution)/shard_map/all_to_all | solution.py:294
  35.3 20.1 %all_to_all.21 = bf16[4,16,24,384]{3,2,1,0:T(8,128)(2,1)S(1)} all-to-all(bf16[4,16,24,384]{3,2,1,0:T(8,128)(2,1)S(1)} %broadcast_in_dim.5), channel_id=1, replica_groups=mesh['z'=16,'yh'=2,'core'=2,'x'=4,'yl'=2] {'yh','yl'}, dimensions={0} | all-to-all | bytes 2359296 | tf_op jit(solution)/shard_map/all_to_all | solution.py:294
  55.4 1.9 %collective-permute-start.9 = (bf16[2,2,384,384]{3,2,1,0:T(8,128)(2,1)S(1)}, bf16[2,2,384,384]{3,2,1,0:T(8,128)(2,1)}, u32[]{:S(2)}, u32[]{:S(2)}) collective-permute-start(bf16[2,2,384,384]{3,2,1,0:T(8,128)(2,1)S(1)} %bitcast.12), channel_id=1, source_target_pairs={{0,8},{8,0},{1,9},{9,1},{2,10},{10,2},{3,11},{11,3},{4,12},{12,4},... | collective-permute-start | bytes 3538952 | tf_op jit(solution)/shard_map/ppermute | solution.py:304
  57.3 3.7 %pack.1 = (bf16[1680,128]{1,0:T(8,128)(2,1)}, bf16[912,128]{1,0:T(8,128)(2,1)}, bf16[1680,128]{1,0:T(8,128)(2,1)}, bf16[912,128]{1,0:T(8,128)(2,1)}, bf16[1680,1...) custom-call(s32[1]{0:T(128)} %bitcast.me_ref.where_ref, ...), custom_call_target="tpu_custom_call" | custom-call | tf_op jit(solution)/shard_map/pack/pallas_call | solution.py:74
  61.0 4.7 %collective-permute-start.3 = (bf16[1680,128]{1,0:T(8,128)(2,1)}, bf16[1680,128]{1,0:T(8,128)(2,1)S(1)}, u32[]{:S(2)}, u32[]{:S(2)}) collective-permute-start(bf16[1680,128]{1,0:T(8,128)(2,1)} %get-tuple-element.17), channel_id=1, source_target_pairs={{0,6},{1,7},{2,4},{3,5},{4,2},{5,3},{6,0},{7,1},{8,14},{9,15},{10,... | collective-permute-start | bytes 1290248 | tf_op jit(solution)/shard_map/ppermute | solution.py:330
  65.7 2.1 %collective-permute-start.1 = (bf16[1680,128]{1,0:T(8,128)(2,1)}, bf16[1680,128]{1,0:T(8,128)(2,1)S(1)}, u32[]{:S(2)}, u32[]{:S(2)}) collective-permute-start(bf16[1680,128]{1,0:T(8,128)(2,1)} %get-tuple-element.15), channel_id=1, source_target_pairs={{0,2},{1,3},{2,0},{3,1},{4,6},{5,7},{6,4},{7,5},{8,10},{9,11},{10,... | collective-permute-start | bytes 1290248 | tf_op jit(solution)/shard_map/ppermute | solution.py:330
  67.8 3.0 %collective-permute-start.7 = (bf16[1680,128]{1,0:T(8,128)(2,1)}, bf16[1680,128]{1,0:T(8,128)(2,1)S(1)}, u32[]{:S(2)}, u32[]{:S(2)}) collective-permute-start(bf16[1680,128]{1,0:T(8,128)(2,1)} %get-tuple-element.19), channel_id=1, source_target_pairs={{0,6},{1,7},{2,4},{3,5},{4,2},{5,3},{6,0},{7,1},{8,14},{9,15},{10,... | collective-permute-start | bytes 1290248 | tf_op jit(solution)/shard_map/ppermute | solution.py:330
  70.9 6.2 %collective-permute-done.3 = bf16[1680,128]{1,0:T(8,128)(2,1)S(1)} collective-permute-done((bf16[1680,128]{1,0:T(8,128)(2,1)}, bf16[1680,128]{1,0:T(8,128)(2,1)S(1)}, u32[]{:S(2)}, u32[]{:S(2)}) %collective-permute-start.3) | collective-permute-done | bytes 430112 | tf_op jit(solution)/shard_map/ppermute | solution.py:330
  77.1 2.2 %collective-permute-start.4 = (bf16[1680,128]{1,0:T(8,128)(2,1)S(1)}, bf16[1680,128]{1,0:T(8,128)(2,1)S(1)}, u32[]{:S(2)}, u32[]{:S(2)}) collective-permute-start(bf16[1680,128]{1,0:T(8,128)(2,1)S(1)} %collective-permute-done.3), channel_id=1, source_target_pairs={{0,2},{1,3},{2,0},{3,1},{4,6},{5,7},{6,4},{7,5},{8,10},{9,11},{10,... | collective-permute-start | bytes 1290248 | tf_op jit(solution)/shard_map/ppermute | solution.py:330
  79.8 6.0 %collective-permute-done.7.g3_ref.refs_6_ = bf16[1680,128]{1,0:T(8,128)(2,1)S(1)} collective-permute-done((bf16[1680,128]{1,0:T(8,128)(2,1)}, bf16[1680,128]{1,0:T(8,128)(2,1)S(1)}, u32[]{:S(2)}, u32[]{:S(2)}) %collective-permute-start.7) | collective-permute-done | bytes 430112 | tf_op jit(solution)/shard_map/ppermute | solution.py:330
  85.9 4.1 %collective-permute-done.4.g2_ref.refs_4_ = bf16[1680,128]{1,0:T(8,128)(2,1)S(1)} collective-permute-done((bf16[1680,128]{1,0:T(8,128)(2,1)S(1)}, bf16[1680,128]{1,0:T(8,128)(2,1)S(1)}, u32[]{:S(2)}, u32[]{:S(2)}) %collective-permute-start.4) | collective-permute-done | bytes 430112 | tf_op jit(solution)/shard_map/ppermute | solution.py:330
  90.0 1.2 copy-done
  91.1 1.7 project_own.1
  92.9 3.7 %project.1 = bf16[8,768,128]{2,1,0:T(8,128)(2,1)} custom-call(s32[2]{0:T(128)S(1)} %pad_add_fusion.where_ref, f32[2,384,512]{2,1,0:T(8,128)S(1)} %get-tuple-element.21.part_ref, bf16[2,2,384,384]{3,2,1,0:T(8,128)(2,1)} %collective-permute-done.9.other_ref, bf16[512,768]{1,0:T(8,128)(2,1)S(1)} %get-tuple-element.22.g_ref), custom_call_target="tpu_custom_call" | custom-call | tf_op jit(solution)/shard_map/project/pallas_call | solution.py:142
  96.6 4.2 %all-to-all-start.2 = ((bf16[8,768,128]{2,1,0:T(8,128)(2,1)}), bf16[8,768,128]{2,1,0:T(8,128)(2,1)S(1)}, u32[]{:S(2)}, u32[]{:S(2)}) async-start(bf16[8,768,128]{2,1,0:T(8,128)(2,1)} %project.1), calls=%async_computation.2 | async-start | bytes 3145728 | tf_op jit(solution)/shard_map/all_to_all | solution.py:294
  100.8 4.8 %collective-permute-start.5 = (bf16[912,128]{1,0:T(8,128)(2,1)}, bf16[912,128]{1,0:T(8,128)(2,1)S(1)}, u32[]{:S(2)}, u32[]{:S(2)}) collective-permute-start(bf16[912,128]{1,0:T(8,128)(2,1)} %get-tuple-element.18), channel_id=1, source_target_pairs={{0,3},{1,2},{2,1},{3,0},{4,7},{5,6},{6,5},{7,4},{8,11},{9,10},{10,... | collective-permute-start | bytes 700424 | tf_op jit(solution)/shard_map/ppermute | solution.py:330
  105.6 2.5 %collective-permute-start = (bf16[912,128]{1,0:T(8,128)(2,1)}, bf16[912,128]{1,0:T(8,128)(2,1)S(1)}, u32[]{:S(2)}, u32[]{:S(2)}) collective-permute-start(bf16[912,128]{1,0:T(8,128)(2,1)} %get-tuple-element.14), channel_id=1, source_target_pairs={{0,1},{1,0},{2,3},{3,2},{4,5},{5,4},{6,7},{7,6},{8,9},{9,8},{10,11... | collective-permute-start | bytes 700424 | tf_op jit(solution)/shard_map/ppermute | solution.py:330
  108.1 3.4 %collective-permute-start.2 = (bf16[912,128]{1,0:T(8,128)(2,1)}, bf16[912,128]{1,0:T(8,128)(2,1)S(1)}, u32[]{:S(2)}, u32[]{:S(2)}) collective-permute-start(bf16[912,128]{1,0:T(8,128)(2,1)} %get-tuple-element.16), channel_id=1, source_target_pairs={{0,3},{1,2},{2,1},{3,0},{4,7},{5,6},{6,5},{7,4},{8,11},{9,10},{10,... | collective-permute-start | bytes 700424 | tf_op jit(solution)/shard_map/ppermute | solution.py:330
  111.5 4.6 %collective-permute-start.8 = (bf16[912,128]{1,0:T(8,128)(2,1)S(1)}, bf16[912,128]{1,0:T(8,128)(2,1)S(1)}, u32[]{:S(2)}, u32[]{:S(2)}) collective-permute-start(bf16[912,128]{1,0:T(8,128)(2,1)S(1)} %copy-done.13), channel_id=1, source_target_pairs={{0,7},{1,6},{2,5},{3,4},{4,3},{5,2},{6,1},{7,0},{8,15},{9,14},{10,... | collective-permute-start | bytes 700424 | tf_op jit(solution)/shard_map/ppermute | solution.py:330
  116.1 14.9 %collective-permute-done.5 = bf16[912,128]{1,0:T(8,128)(2,1)S(1)} collective-permute-done((bf16[912,128]{1,0:T(8,128)(2,1)}, bf16[912,128]{1,0:T(8,128)(2,1)S(1)}, u32[]{:S(2)}, u32[]{:S(2)}) %collective-permute-start.5) | collective-permute-done | bytes 233504 | tf_op jit(solution)/shard_map/ppermute | solution.py:330
  131.0 3.2 %collective-permute-start.6 = (bf16[912,128]{1,0:T(8,128)(2,1)S(1)}, bf16[912,128]{1,0:T(8,128)(2,1)S(1)}, u32[]{:S(2)}, u32[]{:S(2)}) collective-permute-start(bf16[912,128]{1,0:T(8,128)(2,1)S(1)} %collective-permute-done.5), channel_id=1, source_target_pairs={{0,6},{1,7},{2,4},{3,5},{4,2},{5,3},{6,0},{7,1},{8,14},{9,15},{10,... | collective-permute-start | bytes 700424 | tf_op jit(solution)/shard_map/ppermute | solution.py:330
  134.6 4.3 %collective-permute-done.refs_1_ = bf16[912,128]{1,0:T(8,128)(2,1)S(1)} collective-permute-done((bf16[912,128]{1,0:T(8,128)(2,1)}, bf16[912,128]{1,0:T(8,128)(2,1)S(1)}, u32[]{:S(2)}, u32[]{:S(2)}) %collective-permute-start) | collective-permute-done | bytes 233504 | tf_op jit(solution)/shard_map/ppermute | solution.py:330
  138.9 0.7 copy-done.7
  139.6 0.7 copy-done.9
  141.0 1.0 copy-done.5
  142.0 0.9 copy-done.8
  142.9 0.9 copy-done.10
  143.9 0.9 copy-done.12
  144.8 9.0 %attend.1 = bf16[8,704,128]{2,1,0:T(8,128)(2,1)S(1)} custom-call(s32[1]{0:T(128)} %bitcast.me_ref.where_ref, bf16[1680,128]{1,0:T(8,128)(2,1)S(1)} %copy-done.1, bf16[912,128]{1,0:T(8,128)(2,1)S(1)} %collective-permute-done.refs_1_, bf16[1680,128]{1,0:T(8,128)(2,1)S(1)} %collective-permute-done.1.g1_ref.refs_2_, bf16[912,128]{1,0:T(8,128)(2,1)S(1)} %copy-done.8, ...), custom_call_target="tpu_custom_call" | custom-call | tf_op jit(solution)/shard_map/attend/pallas_call | solution.py:245
  153.8 23.7 %all_to_all.22.in_ref = bf16[8,704,128]{2,1,0:T(8,128)(2,1)S(1)} all-to-all(bf16[8,704,128]{2,1,0:T(8,128)(2,1)S(1)} %attend.1), channel_id=1, replica_groups=mesh['z'=16,'yh'=2,'core'=2,'x'=4,'yl'=2] {'x','yl'}, dimensions={0} | all-to-all | bytes 2883584 | tf_op jit(solution)/shard_map/all_to_all | solution.py:294
  177.5 1.6 merge.1
  (31 shorter events, 1.7 us)
Async XLA Ops:
  55.4 37.5 %collective-permute-start.9 = (bf16[2,2,384,384]{3,2,1,0:T(8,128)(2,1)S(1)}, bf16[2,2,384,384]{3,2,1,0:T(8,128)(2,1)}, u32[]{:S(2)}, u32[]{:S(2)}) collective-permute-start(bf16[2,2,384,384]{3,2,1,0:T(8,128)(2,1)S(1)} %bitcast.12), channel_id=1, source_target_pairs={{0,8},{8,0},{1,9},{9,1},{2,10},{10,2},{3,11},{11,3},{4,12},{12,4},... | collective-permute-start | bytes 3538952 | tf_op jit(solution)/shard_map/ppermute | solution.py:304
  61.0 16.1 %collective-permute-start.3 = (bf16[1680,128]{1,0:T(8,128)(2,1)}, bf16[1680,128]{1,0:T(8,128)(2,1)S(1)}, u32[]{:S(2)}, u32[]{:S(2)}) collective-permute-start(bf16[1680,128]{1,0:T(8,128)(2,1)} %get-tuple-element.17), channel_id=1, source_target_pairs={{0,6},{1,7},{2,4},{3,5},{4,2},{5,3},{6,0},{7,1},{8,14},{9,15},{10,... | collective-permute-start | bytes 1290248 | tf_op jit(solution)/shard_map/ppermute | solution.py:330
  65.7 14.1 %collective-permute-start.1 = (bf16[1680,128]{1,0:T(8,128)(2,1)}, bf16[1680,128]{1,0:T(8,128)(2,1)S(1)}, u32[]{:S(2)}, u32[]{:S(2)}) collective-permute-start(bf16[1680,128]{1,0:T(8,128)(2,1)} %get-tuple-element.15), channel_id=1, source_target_pairs={{0,2},{1,3},{2,0},{3,1},{4,6},{5,7},{6,4},{7,5},{8,10},{9,11},{10,... | collective-permute-start | bytes 1290248 | tf_op jit(solution)/shard_map/ppermute | solution.py:330
  67.8 18.0 %collective-permute-start.7 = (bf16[1680,128]{1,0:T(8,128)(2,1)}, bf16[1680,128]{1,0:T(8,128)(2,1)S(1)}, u32[]{:S(2)}, u32[]{:S(2)}) collective-permute-start(bf16[1680,128]{1,0:T(8,128)(2,1)} %get-tuple-element.19), channel_id=1, source_target_pairs={{0,6},{1,7},{2,4},{3,5},{4,2},{5,3},{6,0},{7,1},{8,14},{9,15},{10,... | collective-permute-start | bytes 1290248 | tf_op jit(solution)/shard_map/ppermute | solution.py:330
  77.1 12.9 %collective-permute-start.4 = (bf16[1680,128]{1,0:T(8,128)(2,1)S(1)}, bf16[1680,128]{1,0:T(8,128)(2,1)S(1)}, u32[]{:S(2)}, u32[]{:S(2)}) collective-permute-start(bf16[1680,128]{1,0:T(8,128)(2,1)S(1)} %collective-permute-done.3), channel_id=1, source_target_pairs={{0,2},{1,3},{2,0},{3,1},{4,6},{5,7},{6,4},{7,5},{8,10},{9,11},{10,... | collective-permute-start | bytes 1290248 | tf_op jit(solution)/shard_map/ppermute | solution.py:330
  85.9 7.0 %copy-start.2 = (bf16[1680,128]{1,0:T(8,128)(2,1)}, bf16[1680,128]{1,0:T(8,128)(2,1)S(1)}, u32[]{:S(2)}) copy-start(bf16[1680,128]{1,0:T(8,128)(2,1)S(1)} %collective-permute-done.7.g3_ref.refs_6_) | copy-start | bytes 1290244
  90.0 2.9 %copy-start.4 = (bf16[1680,128]{1,0:T(8,128)(2,1)}, bf16[1680,128]{1,0:T(8,128)(2,1)S(1)}, u32[]{:S(2)}) copy-start(bf16[1680,128]{1,0:T(8,128)(2,1)S(1)} %collective-permute-done.4.g2_ref.refs_4_) | copy-start | bytes 1290244
  90.0 1.2 copy-start
  96.6 14.9 %copy-start.13 = (bf16[912,128]{1,0:T(8,128)(2,1)S(1)}, bf16[912,128]{1,0:T(8,128)(2,1)}, u32[]{:S(2)}) copy-start(bf16[912,128]{1,0:T(8,128)(2,1)} %get-tuple-element.20) | copy-start | bytes 700420
  96.6 37.6 %copy-start.6 = (s32[1,12,16,16]{3,2,1,0:T(8,128)S(1)}, s32[1,12,16,16]{3,2,1,0:T(8,128)}, u32[]{:S(2)}) copy-start(s32[1,12,16,16]{3,2,1,0:T(8,128)} %table_ref.3) | copy-start | bytes 36868
  96.6 44.4 %copy-start.1 = (bf16[1680,128]{1,0:T(8,128)(2,1)S(1)}, bf16[1680,128]{1,0:T(8,128)(2,1)}, u32[]{:S(2)}) copy-start(bf16[1680,128]{1,0:T(8,128)(2,1)} %get-tuple-element.13.g0_ref.refs_0_) | copy-start | bytes 1290244
  96.6 44.4 %copy-start.3 = (bf16[1680,128]{1,0:T(8,128)(2,1)S(1)}, bf16[1680,128]{1,0:T(8,128)(2,1)}, u32[]{:S(2)}) copy-start(bf16[1680,128]{1,0:T(8,128)(2,1)} %copy-done.2) | copy-start | bytes 1290244
  96.6 44.4 %all-to-all-start.2 = ((bf16[8,768,128]{2,1,0:T(8,128)(2,1)}), bf16[8,768,128]{2,1,0:T(8,128)(2,1)S(1)}, u32[]{:S(2)}, u32[]{:S(2)}) async-start(bf16[8,768,128]{2,1,0:T(8,128)(2,1)} %project.1), calls=%async_computation.2 | async-start | bytes 3145728 | tf_op jit(solution)/shard_map/all_to_all | solution.py:294
  100.8 30.2 %collective-permute-start.5 = (bf16[912,128]{1,0:T(8,128)(2,1)}, bf16[912,128]{1,0:T(8,128)(2,1)S(1)}, u32[]{:S(2)}, u32[]{:S(2)}) collective-permute-start(bf16[912,128]{1,0:T(8,128)(2,1)} %get-tuple-element.18), channel_id=1, source_target_pairs={{0,3},{1,2},{2,1},{3,0},{4,7},{5,6},{6,5},{7,4},{8,11},{9,10},{10,... | collective-permute-start | bytes 700424 | tf_op jit(solution)/shard_map/ppermute | solution.py:330
  105.6 33.3 %collective-permute-start = (bf16[912,128]{1,0:T(8,128)(2,1)}, bf16[912,128]{1,0:T(8,128)(2,1)S(1)}, u32[]{:S(2)}, u32[]{:S(2)}) collective-permute-start(bf16[912,128]{1,0:T(8,128)(2,1)} %get-tuple-element.14), channel_id=1, source_target_pairs={{0,1},{1,0},{2,3},{3,2},{4,5},{5,4},{6,7},{7,6},{8,9},{9,8},{10,11... | collective-permute-start | bytes 700424 | tf_op jit(solution)/shard_map/ppermute | solution.py:330
  108.1 30.8 %collective-permute-start.2 = (bf16[912,128]{1,0:T(8,128)(2,1)}, bf16[912,128]{1,0:T(8,128)(2,1)S(1)}, u32[]{:S(2)}, u32[]{:S(2)}) collective-permute-start(bf16[912,128]{1,0:T(8,128)(2,1)} %get-tuple-element.16), channel_id=1, source_target_pairs={{0,3},{1,2},{2,1},{3,0},{4,7},{5,6},{6,5},{7,4},{8,11},{9,10},{10,... | collective-permute-start | bytes 700424 | tf_op jit(solution)/shard_map/ppermute | solution.py:330
  111.5 28.1 %collective-permute-start.8 = (bf16[912,128]{1,0:T(8,128)(2,1)S(1)}, bf16[912,128]{1,0:T(8,128)(2,1)S(1)}, u32[]{:S(2)}, u32[]{:S(2)}) collective-permute-start(bf16[912,128]{1,0:T(8,128)(2,1)S(1)} %copy-done.13), channel_id=1, source_target_pairs={{0,7},{1,6},{2,5},{3,4},{4,3},{5,2},{6,1},{7,0},{8,15},{9,14},{10,... | collective-permute-start | bytes 700424 | tf_op jit(solution)/shard_map/ppermute | solution.py:330
  131.0 9.3 %collective-permute-start.6 = (bf16[912,128]{1,0:T(8,128)(2,1)S(1)}, bf16[912,128]{1,0:T(8,128)(2,1)S(1)}, u32[]{:S(2)}, u32[]{:S(2)}) collective-permute-start(bf16[912,128]{1,0:T(8,128)(2,1)S(1)} %collective-permute-done.5), channel_id=1, source_target_pairs={{0,6},{1,7},{2,4},{3,5},{4,2},{5,3},{6,0},{7,1},{8,14},{9,15},{10,... | collective-permute-start | bytes 700424 | tf_op jit(solution)/shard_map/ppermute | solution.py:330
  138.9 0.7 copy-start.7
  139.6 0.7 copy-start.9
  140.3 0.7 copy-start.11
  141.0 1.0 copy-start.5
  142.0 0.9 copy-start.8
  142.9 0.9 copy-start.10
  143.9 0.9 copy-start.12

commit v7 on v6

--- a/solution.py
+++ b/solution.py
@@ -155,7 +155,7 @@
     gq0, gk0, gv0 = outs
     group = 256 // per
     keys = 1024
-    chunk = 256
+    chunk = 1024
     for b in range(8 // group):
         sources = range(group * b, group * (b + 1))
         q = jnp.concatenate([in_ref[s, q0 : q0 + per] for s in sources], axis=0)
@@ -169,13 +169,13 @@
         norm = norm_row(b)
         dq = jnp.zeros((HD, 256), F32)
         for n in range(keys // chunk):
-            src = slice(2 * n, 2 * n + 2)
+            src = slice(chunk // 128 * n, chunk // 128 * (n + 1))
             k = in_ref[src, k0 : k0 + 128].reshape(chunk, HD)
             v = in_ref[src, v0 : v0 + 128].reshape(chunk, HD)
             scores = dot(k, q, NT_DIMS)
             prob = jnp.exp2(scores * (SCALE * LOG2E) - norm)
-            allowed = mask_ref[4 * n : 4 * (n + 1), 256 * b : 256 * (b + 1)]
-            prob = (prob.reshape(4, TILE, 256) * allowed[:, None, :]).reshape(chunk, 256)
+            allowed = mask_ref[chunk // TILE * n : chunk // TILE * (n + 1), 256 * b : 256 * (b + 1)]
+            prob = (prob.reshape(chunk // TILE, TILE, 256) * allowed[:, None, :]).reshape(chunk, 256)
             score_grad = prob * (dot(v, g, NT_DIMS) - dots)
             prob = prob.astype(BF)
             score_grad = score_grad.astype(BF)
@@ -339,7 +339,8 @@
     arrived[4] = swap(swap(sent[4], 6), 2)
     arrived[5] = swap(swap(sent[5], 3), 6)
     part, slab = project_own(where, own, arrived[::2])
-    partial = exchange(project(where, part, other, slab), ("x", "yl"))
+    part = project(where, part, other, slab)
+    partial = exchange(part, ("x", "yl"))
     mask_a, mask_c = mask_rows(me, tile_mask, False), mask_rows(me, tile_mask, True)
     result = exchange(attend(me, arrived, partial, mask_a, mask_c), ("x", "yl"))
     return merge(result)

time: 180 us -> 178 us (0.989)
  no operation moved by 1% of the time
where the time goes in v7:
time: 178 us; the launch traced here: 177 us
  blocking collectives  77.6 us (44%)
  starting transfers between devices  36.5 us (21%)
  waiting for transfers between devices  36.1 us (20%)
  Pallas kernels  18.5 us (10%)
  local copies, waits for them, and re-layouts  7.92 us (4%)
    all_to_all x3, blocking collectives, exchange(): return lax.all_to_all(array, axes, split_axis=0, concat_axis=0, tiled=True)  77.6 us
    ppermute x9, waiting for transfers between devices, swap(): return lax.ppermute(array, ('x', 'yl'), [(s, s ^ d) for s in range(8)])  36.1 us
    ppermute x9, starting transfers between devices, swap(): return lax.ppermute(array, ('x', 'yl'), [(s, s ^ d) for s in range(8)])  30.4 us
    pallas_call x1, Pallas kernels, attend(): pl.pallas_call(attend_kernel, in_specs=[pl.BlockSpec(memory_space=pltpu.S...  7.41 us
    unnamed x28, local copies, waits for them, and re-layouts  7.07 us
    all_to_all x1, starting transfers between devices, exchange(): return lax.all_to_all(array, axes, split_axis=0, concat_axis=0, tiled=True)  4.18 us
    pallas_call x1, Pallas kernels, project(): pl.pallas_call(project_kernel, in_specs=[pl.BlockSpec(memory_space=pltpu....  3.73 us
    pallas_call x1, Pallas kernels, pack(): pl.pallas_call(pack_kernel, in_specs=[pl.BlockSpec(memory_space=pltpu.SME...  3.71 us
  transfers between devices with their start and end apart: 11, of which 6 were waited for; matrix products, arithmetic and copies ran while one was open for 0% of the time, Pallas kernels for 3%

profile of v7, /device:TPU:32, one launch (start us, length us, event | category | flops | bytes accessed | tf_op | source)
XLA Modules:
  0.0 177.5 jit_solution(1478992491488466511)
XLA Ops:
  0.6 0.7 broadcast_in_dim.4
  1.4 33.8 %all_to_all.20 = bf16[16,24,384]{2,1,0:T(8,128)(2,1)S(1)} all-to-all(bf16[16,24,384]{2,1,0:T(8,128)(2,1)S(1)} %broadcast_in_dim.4), channel_id=1, replica_groups=mesh['z'=16,'yh'=2,'core'=2,'x'=4,'yl'=2] {'z'}, dimensions={0} | all-to-all | bytes 589824 | tf_op jit(solution)/shard_map/all_to_all | solution.py:294
  35.3 20.1 %all_to_all.21 = bf16[4,16,24,384]{3,2,1,0:T(8,128)(2,1)S(1)} all-to-all(bf16[4,16,24,384]{3,2,1,0:T(8,128)(2,1)S(1)} %broadcast_in_dim.5), channel_id=1, replica_groups=mesh['z'=16,'yh'=2,'core'=2,'x'=4,'yl'=2] {'yh','yl'}, dimensions={0} | all-to-all | bytes 2359296 | tf_op jit(solution)/shard_map/all_to_all | solution.py:294
  55.4 1.9 %collective-permute-start.9 = (bf16[2,2,384,384]{3,2,1,0:T(8,128)(2,1)S(1)}, bf16[2,2,384,384]{3,2,1,0:T(8,128)(2,1)}, u32[]{:S(2)}, u32[]{:S(2)}) collective-permute-start(bf16[2,2,384,384]{3,2,1,0:T(8,128)(2,1)S(1)} %bitcast.12), channel_id=1, source_target_pairs={{0,8},{8,0},{1,9},{9,1},{2,10},{10,2},{3,11},{11,3},{4,12},{12,4},... | collective-permute-start | bytes 3538952 | tf_op jit(solution)/shard_map/ppermute | solution.py:304
  57.3 3.7 %pack.1 = (bf16[1680,128]{1,0:T(8,128)(2,1)}, bf16[912,128]{1,0:T(8,128)(2,1)}, bf16[1680,128]{1,0:T(8,128)(2,1)}, bf16[912,128]{1,0:T(8,128)(2,1)}, bf16[1680,1...) custom-call(s32[1]{0:T(128)} %bitcast.me_ref.where_ref, ...), custom_call_target="tpu_custom_call" | custom-call | tf_op jit(solution)/shard_map/pack/pallas_call | solution.py:74
  61.0 4.7 %collective-permute-start.3 = (bf16[1680,128]{1,0:T(8,128)(2,1)}, bf16[1680,128]{1,0:T(8,128)(2,1)S(1)}, u32[]{:S(2)}, u32[]{:S(2)}) collective-permute-start(bf16[1680,128]{1,0:T(8,128)(2,1)} %get-tuple-element.17), channel_id=1, source_target_pairs={{0,6},{1,7},{2,4},{3,5},{4,2},{5,3},{6,0},{7,1},{8,14},{9,15},{10,... | collective-permute-start | bytes 1290248 | tf_op jit(solution)/shard_map/ppermute | solution.py:330
  65.7 2.1 %collective-permute-start.1 = (bf16[1680,128]{1,0:T(8,128)(2,1)}, bf16[1680,128]{1,0:T(8,128)(2,1)S(1)}, u32[]{:S(2)}, u32[]{:S(2)}) collective-permute-start(bf16[1680,128]{1,0:T(8,128)(2,1)} %get-tuple-element.15), channel_id=1, source_target_pairs={{0,2},{1,3},{2,0},{3,1},{4,6},{5,7},{6,4},{7,5},{8,10},{9,11},{10,... | collective-permute-start | bytes 1290248 | tf_op jit(solution)/shard_map/ppermute | solution.py:330
  67.8 3.0 %collective-permute-start.7 = (bf16[1680,128]{1,0:T(8,128)(2,1)}, bf16[1680,128]{1,0:T(8,128)(2,1)S(1)}, u32[]{:S(2)}, u32[]{:S(2)}) collective-permute-start(bf16[1680,128]{1,0:T(8,128)(2,1)} %get-tuple-element.19), channel_id=1, source_target_pairs={{0,6},{1,7},{2,4},{3,5},{4,2},{5,3},{6,0},{7,1},{8,14},{9,15},{10,... | collective-permute-start | bytes 1290248 | tf_op jit(solution)/shard_map/ppermute | solution.py:330
  70.9 6.2 %collective-permute-done.3 = bf16[1680,128]{1,0:T(8,128)(2,1)S(1)} collective-permute-done((bf16[1680,128]{1,0:T(8,128)(2,1)}, bf16[1680,128]{1,0:T(8,128)(2,1)S(1)}, u32[]{:S(2)}, u32[]{:S(2)}) %collective-permute-start.3) | collective-permute-done | bytes 430112 | tf_op jit(solution)/shard_map/ppermute | solution.py:330
  77.1 2.2 %collective-permute-start.4 = (bf16[1680,128]{1,0:T(8,128)(2,1)S(1)}, bf16[1680,128]{1,0:T(8,128)(2,1)S(1)}, u32[]{:S(2)}, u32[]{:S(2)}) collective-permute-start(bf16[1680,128]{1,0:T(8,128)(2,1)S(1)} %collective-permute-done.3), channel_id=1, source_target_pairs={{0,2},{1,3},{2,0},{3,1},{4,6},{5,7},{6,4},{7,5},{8,10},{9,11},{10,... | collective-permute-start | bytes 1290248 | tf_op jit(solution)/shard_map/ppermute | solution.py:330
  79.8 6.0 %collective-permute-done.7.g3_ref.refs_6_ = bf16[1680,128]{1,0:T(8,128)(2,1)S(1)} collective-permute-done((bf16[1680,128]{1,0:T(8,128)(2,1)}, bf16[1680,128]{1,0:T(8,128)(2,1)S(1)}, u32[]{:S(2)}, u32[]{:S(2)}) %collective-permute-start.7) | collective-permute-done | bytes 430112 | tf_op jit(solution)/shard_map/ppermute | solution.py:330
  85.9 4.1 %collective-permute-done.4.g2_ref.refs_4_ = bf16[1680,128]{1,0:T(8,128)(2,1)S(1)} collective-permute-done((bf16[1680,128]{1,0:T(8,128)(2,1)S(1)}, bf16[1680,128]{1,0:T(8,128)(2,1)S(1)}, u32[]{:S(2)}, u32[]{:S(2)}) %collective-permute-start.4) | collective-permute-done | bytes 430112 | tf_op jit(solution)/shard_map/ppermute | solution.py:330
  90.0 1.2 copy-done
  91.1 1.7 project_own.1
  92.9 3.7 %project.1 = bf16[8,768,128]{2,1,0:T(8,128)(2,1)} custom-call(s32[2]{0:T(128)S(1)} %pad_add_fusion.where_ref, f32[2,384,512]{2,1,0:T(8,128)S(1)} %get-tuple-element.21.part_ref, bf16[2,2,384,384]{3,2,1,0:T(8,128)(2,1)} %collective-permute-done.9.other_ref, bf16[512,768]{1,0:T(8,128)(2,1)S(1)} %get-tuple-element.22.g_ref), custom_call_target="tpu_custom_call" | custom-call | tf_op jit(solution)/shard_map/project/pallas_call | solution.py:142
  96.6 4.2 %all-to-all-start.2 = ((bf16[8,768,128]{2,1,0:T(8,128)(2,1)}), bf16[8,768,128]{2,1,0:T(8,128)(2,1)S(1)}, u32[]{:S(2)}, u32[]{:S(2)}) async-start(bf16[8,768,128]{2,1,0:T(8,128)(2,1)} %project.1), calls=%async_computation.2 | async-start | bytes 3145728 | tf_op jit(solution)/shard_map/all_to_all | solution.py:294
  100.8 4.8 %collective-permute-start.5 = (bf16[912,128]{1,0:T(8,128)(2,1)}, bf16[912,128]{1,0:T(8,128)(2,1)S(1)}, u32[]{:S(2)}, u32[]{:S(2)}) collective-permute-start(bf16[912,128]{1,0:T(8,128)(2,1)} %get-tuple-element.18), channel_id=1, source_target_pairs={{0,3},{1,2},{2,1},{3,0},{4,7},{5,6},{6,5},{7,4},{8,11},{9,10},{10,... | collective-permute-start | bytes 700424 | tf_op jit(solution)/shard_map/ppermute | solution.py:330
  105.6 2.5 %collective-permute-start = (bf16[912,128]{1,0:T(8,128)(2,1)}, bf16[912,128]{1,0:T(8,128)(2,1)S(1)}, u32[]{:S(2)}, u32[]{:S(2)}) collective-permute-start(bf16[912,128]{1,0:T(8,128)(2,1)} %get-tuple-element.14), channel_id=1, source_target_pairs={{0,1},{1,0},{2,3},{3,2},{4,5},{5,4},{6,7},{7,6},{8,9},{9,8},{10,11... | collective-permute-start | bytes 700424 | tf_op jit(solution)/shard_map/ppermute | solution.py:330
  108.1 3.4 %collective-permute-start.2 = (bf16[912,128]{1,0:T(8,128)(2,1)}, bf16[912,128]{1,0:T(8,128)(2,1)S(1)}, u32[]{:S(2)}, u32[]{:S(2)}) collective-permute-start(bf16[912,128]{1,0:T(8,128)(2,1)} %get-tuple-element.16), channel_id=1, source_target_pairs={{0,3},{1,2},{2,1},{3,0},{4,7},{5,6},{6,5},{7,4},{8,11},{9,10},{10,... | collective-permute-start | bytes 700424 | tf_op jit(solution)/shard_map/ppermute | solution.py:330
  111.5 4.6 %collective-permute-start.8 = (bf16[912,128]{1,0:T(8,128)(2,1)S(1)}, bf16[912,128]{1,0:T(8,128)(2,1)S(1)}, u32[]{:S(2)}, u32[]{:S(2)}) collective-permute-start(bf16[912,128]{1,0:T(8,128)(2,1)S(1)} %copy-done.13), channel_id=1, source_target_pairs={{0,7},{1,6},{2,5},{3,4},{4,3},{5,2},{6,1},{7,0},{8,15},{9,14},{10,... | collective-permute-start | bytes 700424 | tf_op jit(solution)/shard_map/ppermute | solution.py:330
  116.1 14.9 %collective-permute-done.5 = bf16[912,128]{1,0:T(8,128)(2,1)S(1)} collective-permute-done((bf16[912,128]{1,0:T(8,128)(2,1)}, bf16[912,128]{1,0:T(8,128)(2,1)S(1)}, u32[]{:S(2)}, u32[]{:S(2)}) %collective-permute-start.5) | collective-permute-done | bytes 233504 | tf_op jit(solution)/shard_map/ppermute | solution.py:330
  131.0 3.2 %collective-permute-start.6 = (bf16[912,128]{1,0:T(8,128)(2,1)S(1)}, bf16[912,128]{1,0:T(8,128)(2,1)S(1)}, u32[]{:S(2)}, u32[]{:S(2)}) collective-permute-start(bf16[912,128]{1,0:T(8,128)(2,1)S(1)} %collective-permute-done.5), channel_id=1, source_target_pairs={{0,6},{1,7},{2,4},{3,5},{4,2},{5,3},{6,0},{7,1},{8,14},{9,15},{10,... | collective-permute-start | bytes 700424 | tf_op jit(solution)/shard_map/ppermute | solution.py:330
  134.6 4.3 %collective-permute-done.refs_1_ = bf16[912,128]{1,0:T(8,128)(2,1)S(1)} collective-permute-done((bf16[912,128]{1,0:T(8,128)(2,1)}, bf16[912,128]{1,0:T(8,128)(2,1)S(1)}, u32[]{:S(2)}, u32[]{:S(2)}) %collective-permute-start) | collective-permute-done | bytes 233504 | tf_op jit(solution)/shard_map/ppermute | solution.py:330
  138.9 0.7 copy-done.7
  139.6 0.7 copy-done.9
  141.0 1.0 copy-done.5
  142.0 0.9 copy-done.8
  142.9 0.9 copy-done.10
  143.9 0.9 copy-done.12
  144.8 7.4 %attend.1 = bf16[8,704,128]{2,1,0:T(8,128)(2,1)S(1)} custom-call(s32[1]{0:T(128)} %bitcast.me_ref.where_ref, bf16[1680,128]{1,0:T(8,128)(2,1)S(1)} %copy-done.1, bf16[912,128]{1,0:T(8,128)(2,1)S(1)} %collective-permute-done.refs_1_, bf16[1680,128]{1,0:T(8,128)(2,1)S(1)} %collective-permute-done.1.g1_ref.refs_2_, bf16[912,128]{1,0:T(8,128)(2,1)S(1)} %copy-done.8, ...), custom_call_target="tpu_custom_call" | custom-call | tf_op jit(solution)/shard_map/attend/pallas_call | solution.py:245
  152.2 23.7 %all_to_all.22.in_ref = bf16[8,704,128]{2,1,0:T(8,128)(2,1)S(1)} all-to-all(bf16[8,704,128]{2,1,0:T(8,128)(2,1)S(1)} %attend.1), channel_id=1, replica_groups=mesh['z'=16,'yh'=2,'core'=2,'x'=4,'yl'=2] {'x','yl'}, dimensions={0} | all-to-all | bytes 2883584 | tf_op jit(solution)/shard_map/all_to_all | solution.py:294
  175.9 1.6 merge.1
  (31 shorter events, 1.7 us)
Async XLA Ops:
  55.4 37.5 %collective-permute-start.9 = (bf16[2,2,384,384]{3,2,1,0:T(8,128)(2,1)S(1)}, bf16[2,2,384,384]{3,2,1,0:T(8,128)(2,1)}, u32[]{:S(2)}, u32[]{:S(2)}) collective-permute-start(bf16[2,2,384,384]{3,2,1,0:T(8,128)(2,1)S(1)} %bitcast.12), channel_id=1, source_target_pairs={{0,8},{8,0},{1,9},{9,1},{2,10},{10,2},{3,11},{11,3},{4,12},{12,4},... | collective-permute-start | bytes 3538952 | tf_op jit(solution)/shard_map/ppermute | solution.py:304
  61.0 16.1 %collective-permute-start.3 = (bf16[1680,128]{1,0:T(8,128)(2,1)}, bf16[1680,128]{1,0:T(8,128)(2,1)S(1)}, u32[]{:S(2)}, u32[]{:S(2)}) collective-permute-start(bf16[1680,128]{1,0:T(8,128)(2,1)} %get-tuple-element.17), channel_id=1, source_target_pairs={{0,6},{1,7},{2,4},{3,5},{4,2},{5,3},{6,0},{7,1},{8,14},{9,15},{10,... | collective-permute-start | bytes 1290248 | tf_op jit(solution)/shard_map/ppermute | solution.py:330
  65.7 14.1 %collective-permute-start.1 = (bf16[1680,128]{1,0:T(8,128)(2,1)}, bf16[1680,128]{1,0:T(8,128)(2,1)S(1)}, u32[]{:S(2)}, u32[]{:S(2)}) collective-permute-start(bf16[1680,128]{1,0:T(8,128)(2,1)} %get-tuple-element.15), channel_id=1, source_target_pairs={{0,2},{1,3},{2,0},{3,1},{4,6},{5,7},{6,4},{7,5},{8,10},{9,11},{10,... | collective-permute-start | bytes 1290248 | tf_op jit(solution)/shard_map/ppermute | solution.py:330
  67.8 18.0 %collective-permute-start.7 = (bf16[1680,128]{1,0:T(8,128)(2,1)}, bf16[1680,128]{1,0:T(8,128)(2,1)S(1)}, u32[]{:S(2)}, u32[]{:S(2)}) collective-permute-start(bf16[1680,128]{1,0:T(8,128)(2,1)} %get-tuple-element.19), channel_id=1, source_target_pairs={{0,6},{1,7},{2,4},{3,5},{4,2},{5,3},{6,0},{7,1},{8,14},{9,15},{10,... | collective-permute-start | bytes 1290248 | tf_op jit(solution)/shard_map/ppermute | solution.py:330
  77.1 12.9 %collective-permute-start.4 = (bf16[1680,128]{1,0:T(8,128)(2,1)S(1)}, bf16[1680,128]{1,0:T(8,128)(2,1)S(1)}, u32[]{:S(2)}, u32[]{:S(2)}) collective-permute-start(bf16[1680,128]{1,0:T(8,128)(2,1)S(1)} %collective-permute-done.3), channel_id=1, source_target_pairs={{0,2},{1,3},{2,0},{3,1},{4,6},{5,7},{6,4},{7,5},{8,10},{9,11},{10,... | collective-permute-start | bytes 1290248 | tf_op jit(solution)/shard_map/ppermute | solution.py:330
  85.9 7.0 %copy-start.2 = (bf16[1680,128]{1,0:T(8,128)(2,1)}, bf16[1680,128]{1,0:T(8,128)(2,1)S(1)}, u32[]{:S(2)}) copy-start(bf16[1680,128]{1,0:T(8,128)(2,1)S(1)} %collective-permute-done.7.g3_ref.refs_6_) | copy-start | bytes 1290244
  90.0 2.9 %copy-start.4 = (bf16[1680,128]{1,0:T(8,128)(2,1)}, bf16[1680,128]{1,0:T(8,128)(2,1)S(1)}, u32[]{:S(2)}) copy-start(bf16[1680,128]{1,0:T(8,128)(2,1)S(1)} %collective-permute-done.4.g2_ref.refs_4_) | copy-start | bytes 1290244
  90.0 1.2 copy-start
  96.6 14.9 %copy-start.13 = (bf16[912,128]{1,0:T(8,128)(2,1)S(1)}, bf16[912,128]{1,0:T(8,128)(2,1)}, u32[]{:S(2)}) copy-start(bf16[912,128]{1,0:T(8,128)(2,1)} %get-tuple-element.20) | copy-start | bytes 700420
  96.6 37.6 %copy-start.6 = (s32[1,12,16,16]{3,2,1,0:T(8,128)S(1)}, s32[1,12,16,16]{3,2,1,0:T(8,128)}, u32[]{:S(2)}) copy-start(s32[1,12,16,16]{3,2,1,0:T(8,128)} %table_ref.3) | copy-start | bytes 36868
  96.6 44.4 %copy-start.1 = (bf16[1680,128]{1,0:T(8,128)(2,1)S(1)}, bf16[1680,128]{1,0:T(8,128)(2,1)}, u32[]{:S(2)}) copy-start(bf16[1680,128]{1,0:T(8,128)(2,1)} %get-tuple-element.13.g0_ref.refs_0_) | copy-start | bytes 1290244
  96.6 44.4 %copy-start.3 = (bf16[1680,128]{1,0:T(8,128)(2,1)S(1)}, bf16[1680,128]{1,0:T(8,128)(2,1)}, u32[]{:S(2)}) copy-start(bf16[1680,128]{1,0:T(8,128)(2,1)} %copy-done.2) | copy-start | bytes 1290244
  96.6 44.4 %all-to-all-start.2 = ((bf16[8,768,128]{2,1,0:T(8,128)(2,1)}), bf16[8,768,128]{2,1,0:T(8,128)(2,1)S(1)}, u32[]{:S(2)}, u32[]{:S(2)}) async-start(bf16[8,768,128]{2,1,0:T(8,128)(2,1)} %project.1), calls=%async_computation.2 | async-start | bytes 3145728 | tf_op jit(solution)/shard_map/all_to_all | solution.py:294
  100.8 30.2 %collective-permute-start.5 = (bf16[912,128]{1,0:T(8,128)(2,1)}, bf16[912,128]{1,0:T(8,128)(2,1)S(1)}, u32[]{:S(2)}, u32[]{:S(2)}) collective-permute-start(bf16[912,128]{1,0:T(8,128)(2,1)} %get-tuple-element.18), channel_id=1, source_target_pairs={{0,3},{1,2},{2,1},{3,0},{4,7},{5,6},{6,5},{7,4},{8,11},{9,10},{10,... | collective-permute-start | bytes 700424 | tf_op jit(solution)/shard_map/ppermute | solution.py:330
  105.6 33.3 %collective-permute-start = (bf16[912,128]{1,0:T(8,128)(2,1)}, bf16[912,128]{1,0:T(8,128)(2,1)S(1)}, u32[]{:S(2)}, u32[]{:S(2)}) collective-permute-start(bf16[912,128]{1,0:T(8,128)(2,1)} %get-tuple-element.14), channel_id=1, source_target_pairs={{0,1},{1,0},{2,3},{3,2},{4,5},{5,4},{6,7},{7,6},{8,9},{9,8},{10,11... | collective-permute-start | bytes 700424 | tf_op jit(solution)/shard_map/ppermute | solution.py:330
  108.1 30.8 %collective-permute-start.2 = (bf16[912,128]{1,0:T(8,128)(2,1)}, bf16[912,128]{1,0:T(8,128)(2,1)S(1)}, u32[]{:S(2)}, u32[]{:S(2)}) collective-permute-start(bf16[912,128]{1,0:T(8,128)(2,1)} %get-tuple-element.16), channel_id=1, source_target_pairs={{0,3},{1,2},{2,1},{3,0},{4,7},{5,6},{6,5},{7,4},{8,11},{9,10},{10,... | collective-permute-start | bytes 700424 | tf_op jit(solution)/shard_map/ppermute | solution.py:330
  111.5 28.1 %collective-permute-start.8 = (bf16[912,128]{1,0:T(8,128)(2,1)S(1)}, bf16[912,128]{1,0:T(8,128)(2,1)S(1)}, u32[]{:S(2)}, u32[]{:S(2)}) collective-permute-start(bf16[912,128]{1,0:T(8,128)(2,1)S(1)} %copy-done.13), channel_id=1, source_target_pairs={{0,7},{1,6},{2,5},{3,4},{4,3},{5,2},{6,1},{7,0},{8,15},{9,14},{10,... | collective-permute-start | bytes 700424 | tf_op jit(solution)/shard_map/ppermute | solution.py:330
  131.0 9.3 %collective-permute-start.6 = (bf16[912,128]{1,0:T(8,128)(2,1)S(1)}, bf16[912,128]{1,0:T(8,128)(2,1)S(1)}, u32[]{:S(2)}, u32[]{:S(2)}) collective-permute-start(bf16[912,128]{1,0:T(8,128)(2,1)S(1)} %collective-permute-done.5), channel_id=1, source_target_pairs={{0,6},{1,7},{2,4},{3,5},{4,2},{5,3},{6,0},{7,1},{8,14},{9,15},{10,... | collective-permute-start | bytes 700424 | tf_op jit(solution)/shard_map/ppermute | solution.py:330
  138.9 0.7 copy-start.7
  139.6 0.7 copy-start.9
  140.3 0.7 copy-start.11
  141.0 1.0 copy-start.5
  142.0 0.9 copy-start.8
  142.9 0.9 copy-start.10
  143.9 0.9 copy-start.12

commit v8 on v7

--- a/solution.py
+++ b/solution.py
@@ -24,6 +24,8 @@
 GQA, GKA, GVA, GKC, GVC, GQC = 0, 128, 256, 384, 512, 640
 OUT_ROWS = 704
 
+PARTNERS = ((0, 0), (1, 3), (2, 6), (3, 7), (6, 2), (7, 1), (4, 4), (5, 5))
+
 NT_DIMS = (((1,), (1,)), ((), ()))
 NN_DIMS = (((1,), (0,)), ((), ()))
 TN_DIMS = (((0,), (0,)), ((), ()))
@@ -31,6 +33,11 @@
 
 def dot(a, b, dims):
     return lax.dot_general(a, b, dims, preferred_element_type=F32)
+
+
+def partner(me_ref, slot):
+    first, second = PARTNERS[slot]
+    return jnp.bitwise_xor(me_ref[0], jnp.where(me_ref[1] == 0, first, second))
 
 
 def start(sources, targets, sems):
@@ -46,7 +53,7 @@
     for copy in start((q_hbm, k_hbm, v_hbm, o_hbm, n_hbm, g_hbm), (q_ref, k_ref, v_ref, o_ref, n_ref, g_ref), sems):
         copy.wait()
     for d, out_ref in enumerate(out_refs):
-        to = jnp.bitwise_xor(me_ref[0], d)
+        to = partner(me_ref, d)
         x, y = to // 2, to % 2
         base = 0 if d % 2 else SLAB
         own = pl.ds(pl.multiple_of(HD * (3 * x + y), HD), HD)
@@ -91,16 +98,16 @@
     return dot(shard_ref[yh, 0], g[:, :384], NT_DIMS) + dot(shard_ref[yh, 1], g[:, 384:], NT_DIMS)
 
 
-def project_own_kernel(where_ref, own_ref, g0_ref, g1_ref, g2_ref, g3_ref, part_ref, g_ref):
+def project_own_kernel(me_ref, own_ref, g0_ref, g1_ref, g2_ref, g3_ref, part_ref, g_ref):
     for e, ref in enumerate((g0_ref, g1_ref, g2_ref, g3_ref)):
-        rows = pl.ds(pl.multiple_of(128 * jnp.bitwise_xor(where_ref[1], e), 128), 128)
+        rows = pl.ds(pl.multiple_of(128 * (partner(me_ref, 2 * e) // 2), 128), 128)
         for n in range(6):
             g_ref[rows, 128 * n : 128 * (n + 1)] = ref[128 * n : 128 * (n + 1)]
     for yh in range(2):
         part_ref[yh] = product(own_ref, g_ref[...], yh)
 
 
-def project_own(where, own, slabs):
+def project_own(me, own, slabs):
     whole = pl.BlockSpec(memory_space=pltpu.VMEM)
     slab = pl.BlockSpec((SLAB, 128), lambda i: (0, 0))
     return pl.pallas_call(
@@ -111,11 +118,11 @@
         out_shape=(jax.ShapeDtypeStruct((2, 384, 512), F32), jax.ShapeDtypeStruct((512, 768), BF)),
         compiler_params=pltpu.CompilerParams(vmem_limit_bytes=GRANT),
         name="project_own",
-    )(where, own, *slabs)
-
-
-def project_kernel(where_ref, part_ref, other_ref, g_ref, out_ref, t_ref):
-    core = where_ref[0]
+    )(me, own, *slabs)
+
+
+def project_kernel(me_ref, part_ref, other_ref, g_ref, out_ref, t_ref):
+    core = me_ref[1]
     for yh in range(2):
         for c, part in ((core, part_ref[yh]), (1 - core, product(other_ref, g_ref[...], yh))):
             for z in range(16):
@@ -137,7 +144,7 @@
                 )
 
 
-def project(where, part, other, g):
+def project(me, part, other, g):
     whole = pl.BlockSpec(memory_space=pltpu.VMEM)
     return pl.pallas_call(
         project_kernel,
@@ -147,7 +154,7 @@
         scratch_shapes=[pltpu.VMEM((1536, 512), F32)],
         compiler_params=pltpu.CompilerParams(vmem_limit_bytes=GRANT),
         name="project",
-    )(where, part, other, g)
+    )(me, part, other, g)
 
 
 def attend_unit(in_ref, g_ref, mask_ref, out_ref, dk_ref, dv_ref, per, rows, norm_row, outs):
@@ -202,7 +209,7 @@
     sent_refs = refs[:8]
     mid_ref, mask_a_hbm, mask_c_hbm, out_ref, in_ref, g_ref, dk_ref, dv_ref, mask_a_ref, mask_c_ref, sems = refs[8:]
     sources = [ref if d % 2 else ref.at[pl.ds(SLAB, IN_ROWS)] for d, ref in enumerate(sent_refs)]
-    targets = [in_ref.at[jnp.bitwise_xor(me_ref[0], d)] for d in range(8)]
+    targets = [in_ref.at[partner(me_ref, d)] for d in range(8)]
     copies = start((*sources, mask_a_hbm, mask_c_hbm), (*targets, mask_a_ref, mask_c_ref), sems)
     for y in range(2):
         for n in range(6):
@@ -326,21 +333,20 @@
     )(me, tile_mask)
 
 
-def swap(array, d):
-    return lax.ppermute(array, ("x", "yl"), [(s, s ^ d) for s in range(8)])
+def swap(array, partners):
+    pairs = [(8 * core + s, 8 * core + (s ^ partners[core])) for core in range(2) for s in range(8)]
+    return lax.ppermute(array, ("core", "x", "yl"), pairs)
 
 
 def after_weight(q, k, v, o, log_norm, out_grad, own, other, core, tile_mask):
     x, y = lax.axis_index("x"), lax.axis_index("yl")
-    me = (2 * x + y).reshape(1)
-    where = jnp.stack([core, x])
+    me = jnp.stack([2 * x + y, core])
     sent = pack(me, q[0], k[0], v[0], o[0], log_norm[0].T, out_grad[0])
-    arrived = [sent[d] if d in (0, 4, 5) else swap(sent[d], d) for d in range(8)]
-    arrived[4] = swap(swap(sent[4], 6), 2)
-    arrived[5] = swap(swap(sent[5], 3), 6)
-    part, slab = project_own(where, own, arrived[::2])
-    part = project(where, part, other, slab)
-    partial = exchange(part, ("x", "yl"))
+    arrived = [sent[0]] + [swap(sent[d], PARTNERS[d]) for d in range(1, 6)]
+    arrived.append(swap(swap(sent[6], (6, 2)), (2, 6)))
+    arrived.append(swap(swap(sent[7], (3, 7)), (6, 2)))
+    part, slab = project_own(me, own, arrived[::2])
+    partial = exchange(project(me, part, other, slab), ("x", "yl"))
     mask_a, mask_c = mask_rows(me, tile_mask, False), mask_rows(me, tile_mask, True)
     result = exchange(attend(me, arrived, partial, mask_a, mask_c), ("x", "yl"))
     return merge(result)

time: 178 us -> 178 us (level)
  waiting for transfers between devices: 36.1 us -> 28.9 us
  starting transfers between devices: 36.5 us -> 42.3 us
  Pallas kernels: 18.5 us -> 21 us
  blocking collectives: 77.6 us -> 75.2 us
    ppermute x9, waiting for transfers between devices: 36.1 us -> 28.9 us  [swap(): return lax.ppermute(array, ('core', 'x', 'yl'), pairs)]
    ppermute x9, starting transfers between devices: 30.4 us -> 36.2 us  [swap(): return lax.ppermute(array, ('core', 'x', 'yl'), pairs)]
    all_to_all x3, blocking collectives: 77.6 us -> 75.2 us  [exchange(): return lax.all_to_all(array, axes, split_axis=0, concat_axis=0, tiled=True)]
    unnamed x28 -> x30, local copies, waits for them, and re-layouts: 7.07 us -> 7.07 us
  transfers between devices with their start and end apart: 11 -> 11, of which waited for: 6 -> 6; matrix products, arithmetic and copies ran while one was open for 0% -> 0% of each run, Pallas kernels for 3% -> 4%
where the time goes in v8:
time: 178 us; the launch traced here: 177 us
  blocking collectives  75.2 us (42%)
  starting transfers between devices  42.3 us (24%)
  waiting for transfers between devices  28.9 us (16%)
  Pallas kernels  21 us (12%)
  local copies, waits for them, and re-layouts  7.92 us (4%)
    all_to_all x3, blocking collectives, exchange(): return lax.all_to_all(array, axes, split_axis=0, concat_axis=0, tiled=True)  75.2 us
    ppermute x9, starting transfers between devices, swap(): return lax.ppermute(array, ('core', 'x', 'yl'), pairs)  36.2 us
    ppermute x9, waiting for transfers between devices, swap(): return lax.ppermute(array, ('core', 'x', 'yl'), pairs)  28.9 us
    pallas_call x1, Pallas kernels, attend(): pl.pallas_call(attend_kernel, in_specs=[pl.BlockSpec(memory_space=pltpu.S...  8 us
    unnamed x30, local copies, waits for them, and re-layouts  7.07 us
    pallas_call x1, Pallas kernels, pack(): pl.pallas_call(pack_kernel, in_specs=[pl.BlockSpec(memory_space=pltpu.SME...  4.48 us
    all_to_all x1, starting transfers between devices, exchange(): return lax.all_to_all(array, axes, split_axis=0, concat_axis=0, tiled=True)  4.17 us
    pallas_call x1, Pallas kernels, project(): pl.pallas_call(project_kernel, in_specs=[pl.BlockSpec(memory_space=pltpu....  3.73 us
  transfers between devices with their start and end apart: 11, of which 6 were waited for; matrix products, arithmetic and copies ran while one was open for 0% of the time, Pallas kernels for 4%

profile of v8, /device:TPU:32, one launch (start us, length us, event | category | flops | bytes accessed | tf_op | source)
XLA Modules:
  0.0 176.7 jit_solution(7690602486756514376)
XLA Ops:
  0.6 0.7 broadcast_in_dim.4
  1.4 33.8 %all_to_all.20 = bf16[16,24,384]{2,1,0:T(8,128)(2,1)S(1)} all-to-all(bf16[16,24,384]{2,1,0:T(8,128)(2,1)S(1)} %broadcast_in_dim.4), channel_id=1, replica_groups=mesh['z'=16,'yh'=2,'core'=2,'x'=4,'yl'=2] {'z'}, dimensions={0} | all-to-all | bytes 589824 | tf_op jit(solution)/shard_map/all_to_all | solution.py:301
  35.3 20.1 %all_to_all.21 = bf16[4,16,24,384]{3,2,1,0:T(8,128)(2,1)S(1)} all-to-all(bf16[4,16,24,384]{3,2,1,0:T(8,128)(2,1)S(1)} %broadcast_in_dim.5), channel_id=1, replica_groups=mesh['z'=16,'yh'=2,'core'=2,'x'=4,'yl'=2] {'yh','yl'}, dimensions={0} | all-to-all | bytes 2359296 | tf_op jit(solution)/shard_map/all_to_all | solution.py:301
  55.4 1.9 %collective-permute-start.9 = (bf16[2,2,384,384]{3,2,1,0:T(8,128)(2,1)S(1)}, bf16[2,2,384,384]{3,2,1,0:T(8,128)(2,1)}, u32[]{:S(2)}, u32[]{:S(2)}) collective-permute-start(bf16[2,2,384,384]{3,2,1,0:T(8,128)(2,1)S(1)} %bitcast.11), channel_id=1, source_target_pairs={{0,8},{8,0},{1,9},{9,1},{2,10},{10,2},{3,11},{11,3},{4,12},{12,4},... | collective-permute-start | bytes 3538952 | tf_op jit(solution)/shard_map/ppermute | solution.py:311
  58.0 4.5 %pack.1 = (bf16[1680,128]{1,0:T(8,128)(2,1)}, bf16[912,128]{1,0:T(8,128)(2,1)}, bf16[1680,128]{1,0:T(8,128)(2,1)}, bf16[912,128]{1,0:T(8,128)(2,1)}, bf16[1680,1...) custom-call(s32[2]{0:T(128)} %pad_add_fusion.me_ref.where_ref, ...), custom_call_target="tpu_custom_call" | custom-call | tf_op jit(solution)/shard_map/pack/pallas_call | solution.py:81
  62.5 4.7 %collective-permute-start.5 = (bf16[1680,128]{1,0:T(8,128)(2,1)}, bf16[1680,128]{1,0:T(8,128)(2,1)S(1)}, u32[]{:S(2)}, u32[]{:S(2)}) collective-permute-start(bf16[1680,128]{1,0:T(8,128)(2,1)} %get-tuple-element.19), channel_id=1, source_target_pairs={{0,6},{1,7},{2,4},{3,5},{4,2},{5,3},{6,0},{7,1},{8,10},{9,11},{10,... | collective-permute-start | bytes 1290248 | tf_op jit(solution)/shard_map/ppermute | solution.py:338
  67.1 2.1 %collective-permute-start.1 = (bf16[1680,128]{1,0:T(8,128)(2,1)}, bf16[1680,128]{1,0:T(8,128)(2,1)S(1)}, u32[]{:S(2)}, u32[]{:S(2)}) collective-permute-start(bf16[1680,128]{1,0:T(8,128)(2,1)} %get-tuple-element.15), channel_id=1, source_target_pairs={{0,2},{1,3},{2,0},{3,1},{4,6},{5,7},{6,4},{7,5},{8,14},{9,15},{10,... | collective-permute-start | bytes 1290248 | tf_op jit(solution)/shard_map/ppermute | solution.py:338
  69.3 3.0 %collective-permute-start.3 = (bf16[1680,128]{1,0:T(8,128)(2,1)}, bf16[1680,128]{1,0:T(8,128)(2,1)S(1)}, u32[]{:S(2)}, u32[]{:S(2)}) collective-permute-start(bf16[1680,128]{1,0:T(8,128)(2,1)} %get-tuple-element.17), channel_id=1, source_target_pairs={{0,6},{1,7},{2,4},{3,5},{4,2},{5,3},{6,0},{7,1},{8,10},{9,11},{10,... | collective-permute-start | bytes 1290248 | tf_op jit(solution)/shard_map/ppermute | solution.py:338
  72.3 3.6 %collective-permute-done.5 = bf16[1680,128]{1,0:T(8,128)(2,1)S(1)} collective-permute-done((bf16[1680,128]{1,0:T(8,128)(2,1)}, bf16[1680,128]{1,0:T(8,128)(2,1)S(1)}, u32[]{:S(2)}, u32[]{:S(2)}) %collective-permute-start.5) | collective-permute-done | bytes 430112 | tf_op jit(solution)/shard_map/ppermute | solution.py:338
  75.9 2.7 %collective-permute-start.6 = (bf16[1680,128]{1,0:T(8,128)(2,1)S(1)}, bf16[1680,128]{1,0:T(8,128)(2,1)S(1)}, u32[]{:S(2)}, u32[]{:S(2)}) collective-permute-start(bf16[1680,128]{1,0:T(8,128)(2,1)S(1)} %collective-permute-done.5), channel_id=1, source_target_pairs={{0,2},{1,3},{2,0},{3,1},{4,6},{5,7},{6,4},{7,5},{8,14},{9,15},{10,... | collective-permute-start | bytes 1290248 | tf_op jit(solution)/shard_map/ppermute | solution.py:338
  78.6 1.7 collective-permute-done.1.g1_ref.refs_2_
  80.3 5.1 %collective-permute-done.3.g2_ref.refs_4_ = bf16[1680,128]{1,0:T(8,128)(2,1)S(1)} collective-permute-done((bf16[1680,128]{1,0:T(8,128)(2,1)}, bf16[1680,128]{1,0:T(8,128)(2,1)S(1)}, u32[]{:S(2)}, u32[]{:S(2)}) %collective-permute-start.3) | collective-permute-done | bytes 430112 | tf_op jit(solution)/shard_map/ppermute | solution.py:338
  85.4 1.3 collective-permute-done.6.g3_ref.refs_6_
  86.6 1.2 copy-done
  87.8 1.7 project_own.1
  89.5 3.7 %project.1 = bf16[8,768,128]{2,1,0:T(8,128)(2,1)} custom-call(s32[2]{0:T(128)S(1)} %copy-done.13, f32[2,384,512]{2,1,0:T(8,128)S(1)} %get-tuple-element.21.part_ref, bf16[2,2,384,384]{3,2,1,0:T(8,128)(2,1)} %collective-permute-done.9.other_ref, bf16[512,768]{1,0:T(8,128)(2,1)S(1)} %get-tuple-element.22.g_ref), custom_call_target="tpu_custom_call" | custom-call | tf_op jit(solution)/shard_map/project/pallas_call | solution.py:149
  93.3 4.2 %all-to-all-start.2 = ((bf16[8,768,128]{2,1,0:T(8,128)(2,1)}), bf16[8,768,128]{2,1,0:T(8,128)(2,1)S(1)}, u32[]{:S(2)}, u32[]{:S(2)}) async-start(bf16[8,768,128]{2,1,0:T(8,128)(2,1)} %project.1), calls=%async_computation.2 | async-start | bytes 3145728 | tf_op jit(solution)/shard_map/all_to_all | solution.py:301
  97.4 4.8 %collective-permute-start.7 = (bf16[912,128]{1,0:T(8,128)(2,1)}, bf16[912,128]{1,0:T(8,128)(2,1)S(1)}, u32[]{:S(2)}, u32[]{:S(2)}) collective-permute-start(bf16[912,128]{1,0:T(8,128)(2,1)} %get-tuple-element.20), channel_id=1, source_target_pairs={{0,3},{1,2},{2,1},{3,0},{4,7},{5,6},{6,5},{7,4},{8,15},{9,14},{10,... | collective-permute-start | bytes 700424 | tf_op jit(solution)/shard_map/ppermute | solution.py:338
  102.3 2.5 %collective-permute-start = (bf16[912,128]{1,0:T(8,128)(2,1)}, bf16[912,128]{1,0:T(8,128)(2,1)S(1)}, u32[]{:S(2)}, u32[]{:S(2)}) collective-permute-start(bf16[912,128]{1,0:T(8,128)(2,1)} %get-tuple-element.14), channel_id=1, source_target_pairs={{0,1},{1,0},{2,3},{3,2},{4,5},{5,4},{6,7},{7,6},{8,11},{9,10},{10,... | collective-permute-start | bytes 700424 | tf_op jit(solution)/shard_map/ppermute | solution.py:338
  104.7 3.4 %collective-permute-start.2 = (bf16[912,128]{1,0:T(8,128)(2,1)}, bf16[912,128]{1,0:T(8,128)(2,1)S(1)}, u32[]{:S(2)}, u32[]{:S(2)}) collective-permute-start(bf16[912,128]{1,0:T(8,128)(2,1)} %get-tuple-element.16), channel_id=1, source_target_pairs={{0,3},{1,2},{2,1},{3,0},{4,7},{5,6},{6,5},{7,4},{8,15},{9,14},{10,... | collective-permute-start | bytes 700424 | tf_op jit(solution)/shard_map/ppermute | solution.py:338
  108.1 4.6 %collective-permute-start.4 = (bf16[912,128]{1,0:T(8,128)(2,1)S(1)}, bf16[912,128]{1,0:T(8,128)(2,1)S(1)}, u32[]{:S(2)}, u32[]{:S(2)}) collective-permute-start(bf16[912,128]{1,0:T(8,128)(2,1)S(1)} %copy-done.14), channel_id=1, source_target_pairs={{0,7},{1,6},{2,5},{3,4},{4,3},{5,2},{6,1},{7,0},{8,9},{9,8},{10,11... | collective-permute-start | bytes 700424 | tf_op jit(solution)/shard_map/ppermute | solution.py:338
  112.7 16.2 %collective-permute-done.7 = bf16[912,128]{1,0:T(8,128)(2,1)S(1)} collective-permute-done((bf16[912,128]{1,0:T(8,128)(2,1)}, bf16[912,128]{1,0:T(8,128)(2,1)S(1)}, u32[]{:S(2)}, u32[]{:S(2)}) %collective-permute-start.7) | collective-permute-done | bytes 233504 | tf_op jit(solution)/shard_map/ppermute | solution.py:338
  128.9 8.4 %collective-permute-start.8 = (bf16[912,128]{1,0:T(8,128)(2,1)S(1)}, bf16[912,128]{1,0:T(8,128)(2,1)S(1)}, u32[]{:S(2)}, u32[]{:S(2)}) collective-permute-start(bf16[912,128]{1,0:T(8,128)(2,1)S(1)} %collective-permute-done.7), channel_id=1, source_target_pairs={{0,6},{1,7},{2,4},{3,5},{4,2},{5,3},{6,0},{7,1},{8,10},{9,11},{10,... | collective-permute-start | bytes 700424 | tf_op jit(solution)/shard_map/ppermute | solution.py:338
  137.3 0.7 mask.2.refs_9_
  140.2 1.1 collective-permute-done.8.refs_7_
  142.0 1.0 copy-done.5
  143.0 0.9 copy-done.8
  144.0 0.9 copy-done.10
  144.9 0.9 copy-done.12
  145.8 8.0 %attend.1 = bf16[8,704,128]{2,1,0:T(8,128)(2,1)S(1)} custom-call(s32[2]{0:T(128)S(1)} %copy-done.13, bf16[1680,128]{1,0:T(8,128)(2,1)S(1)} %copy-done.1, bf16[912,128]{1,0:T(8,128)(2,1)S(1)} %collective-permute-done.refs_1_, bf16[1680,128]{1,0:T(8,128)(2,1)S(1)} %collective-permute-done.1.g1_ref.refs_2_, bf16[912,128]{1,0:T(8,128)(2,1)S(1)} %copy-done.8, ...), custom_call_target="tpu_custom_call" | custom-call | tf_op jit(solution)/shard_map/attend/pallas_call | solution.py:252
  153.8 21.3 %all_to_all.22.in_ref = bf16[8,704,128]{2,1,0:T(8,128)(2,1)S(1)} all-to-all(bf16[8,704,128]{2,1,0:T(8,128)(2,1)S(1)} %attend.1), channel_id=1, replica_groups=mesh['z'=16,'yh'=2,'core'=2,'x'=4,'yl'=2] {'x','yl'}, dimensions={0} | all-to-all | bytes 2883584 | tf_op jit(solution)/shard_map/all_to_all | solution.py:301
  175.1 1.6 merge.1
  (33 shorter events, 3.6 us)
Async XLA Ops:
  55.4 34.1 %collective-permute-start.9 = (bf16[2,2,384,384]{3,2,1,0:T(8,128)(2,1)S(1)}, bf16[2,2,384,384]{3,2,1,0:T(8,128)(2,1)}, u32[]{:S(2)}, u32[]{:S(2)}) collective-permute-start(bf16[2,2,384,384]{3,2,1,0:T(8,128)(2,1)S(1)} %bitcast.11), channel_id=1, source_target_pairs={{0,8},{8,0},{1,9},{9,1},{2,10},{10,2},{3,11},{11,3},{4,12},{12,4},... | collective-permute-start | bytes 3538952 | tf_op jit(solution)/shard_map/ppermute | solution.py:311
  58.0 28.6 %copy-start.13 = (s32[2]{0:T(128)S(1)}, s32[2]{0:T(128)}, u32[]{:S(2)}) copy-start(s32[2]{0:T(128)} %pad_add_fusion.me_ref.where_ref) | copy-start | bytes 28
  62.5 13.4 %collective-permute-start.5 = (bf16[1680,128]{1,0:T(8,128)(2,1)}, bf16[1680,128]{1,0:T(8,128)(2,1)S(1)}, u32[]{:S(2)}, u32[]{:S(2)}) collective-permute-start(bf16[1680,128]{1,0:T(8,128)(2,1)} %get-tuple-element.19), channel_id=1, source_target_pairs={{0,6},{1,7},{2,4},{3,5},{4,2},{5,3},{6,0},{7,1},{8,10},{9,11},{10,... | collective-permute-start | bytes 1290248 | tf_op jit(solution)/shard_map/ppermute | solution.py:338
  67.1 13.2 %collective-permute-start.1 = (bf16[1680,128]{1,0:T(8,128)(2,1)}, bf16[1680,128]{1,0:T(8,128)(2,1)S(1)}, u32[]{:S(2)}, u32[]{:S(2)}) collective-permute-start(bf16[1680,128]{1,0:T(8,128)(2,1)} %get-tuple-element.15), channel_id=1, source_target_pairs={{0,2},{1,3},{2,0},{3,1},{4,6},{5,7},{6,4},{7,5},{8,14},{9,15},{10,... | collective-permute-start | bytes 1290248 | tf_op jit(solution)/shard_map/ppermute | solution.py:338
  69.3 16.1 %collective-permute-start.3 = (bf16[1680,128]{1,0:T(8,128)(2,1)}, bf16[1680,128]{1,0:T(8,128)(2,1)S(1)}, u32[]{:S(2)}, u32[]{:S(2)}) collective-permute-start(bf16[1680,128]{1,0:T(8,128)(2,1)} %get-tuple-element.17), channel_id=1, source_target_pairs={{0,6},{1,7},{2,4},{3,5},{4,2},{5,3},{6,0},{7,1},{8,10},{9,11},{10,... | collective-permute-start | bytes 1290248 | tf_op jit(solution)/shard_map/ppermute | solution.py:338
  75.9 10.7 %collective-permute-start.6 = (bf16[1680,128]{1,0:T(8,128)(2,1)S(1)}, bf16[1680,128]{1,0:T(8,128)(2,1)S(1)}, u32[]{:S(2)}, u32[]{:S(2)}) collective-permute-start(bf16[1680,128]{1,0:T(8,128)(2,1)S(1)} %collective-permute-done.5), channel_id=1, source_target_pairs={{0,2},{1,3},{2,0},{3,1},{4,6},{5,7},{6,4},{7,5},{8,14},{9,15},{10,... | collective-permute-start | bytes 1290248 | tf_op jit(solution)/shard_map/ppermute | solution.py:338
  85.4 4.1 %copy-start.2 = (bf16[1680,128]{1,0:T(8,128)(2,1)}, bf16[1680,128]{1,0:T(8,128)(2,1)S(1)}, u32[]{:S(2)}) copy-start(bf16[1680,128]{1,0:T(8,128)(2,1)S(1)} %collective-permute-done.3.g2_ref.refs_4_) | copy-start | bytes 1290244
  86.6 2.9 %copy-start.4 = (bf16[1680,128]{1,0:T(8,128)(2,1)}, bf16[1680,128]{1,0:T(8,128)(2,1)S(1)}, u32[]{:S(2)}) copy-start(bf16[1680,128]{1,0:T(8,128)(2,1)S(1)} %collective-permute-done.6.g3_ref.refs_6_) | copy-start | bytes 1290244
  86.6 1.2 copy-start
  93.2 14.9 %copy-start.14 = (bf16[912,128]{1,0:T(8,128)(2,1)S(1)}, bf16[912,128]{1,0:T(8,128)(2,1)}, u32[]{:S(2)}) copy-start(bf16[912,128]{1,0:T(8,128)(2,1)} %get-tuple-element.18) | copy-start | bytes 700420
  93.3 44.0 %copy-start.6 = (s32[1,12,16,16]{3,2,1,0:T(8,128)S(1)}, s32[1,12,16,16]{3,2,1,0:T(8,128)}, u32[]{:S(2)}) copy-start(s32[1,12,16,16]{3,2,1,0:T(8,128)} %table_ref.3) | copy-start | bytes 36868
  93.3 48.8 %copy-start.1 = (bf16[1680,128]{1,0:T(8,128)(2,1)S(1)}, bf16[1680,128]{1,0:T(8,128)(2,1)}, u32[]{:S(2)}) copy-start(bf16[1680,128]{1,0:T(8,128)(2,1)} %get-tuple-element.13.g0_ref.refs_0_) | copy-start | bytes 1290244
  93.3 48.8 %copy-start.3 = (bf16[1680,128]{1,0:T(8,128)(2,1)S(1)}, bf16[1680,128]{1,0:T(8,128)(2,1)}, u32[]{:S(2)}) copy-start(bf16[1680,128]{1,0:T(8,128)(2,1)} %copy-done.2) | copy-start | bytes 1290244
  93.3 48.7 %all-to-all-start.2 = ((bf16[8,768,128]{2,1,0:T(8,128)(2,1)}), bf16[8,768,128]{2,1,0:T(8,128)(2,1)S(1)}, u32[]{:S(2)}, u32[]{:S(2)}) async-start(bf16[8,768,128]{2,1,0:T(8,128)(2,1)} %project.1), calls=%async_computation.2 | async-start | bytes 3145728 | tf_op jit(solution)/shard_map/all_to_all | solution.py:301
  97.4 31.4 %collective-permute-start.7 = (bf16[912,128]{1,0:T(8,128)(2,1)}, bf16[912,128]{1,0:T(8,128)(2,1)S(1)}, u32[]{:S(2)}, u32[]{:S(2)}) collective-permute-start(bf16[912,128]{1,0:T(8,128)(2,1)} %get-tuple-element.20), channel_id=1, source_target_pairs={{0,3},{1,2},{2,1},{3,0},{4,7},{5,6},{6,5},{7,4},{8,15},{9,14},{10,... | collective-permute-start | bytes 700424 | tf_op jit(solution)/shard_map/ppermute | solution.py:338
  102.3 36.5 %collective-permute-start = (bf16[912,128]{1,0:T(8,128)(2,1)}, bf16[912,128]{1,0:T(8,128)(2,1)S(1)}, u32[]{:S(2)}, u32[]{:S(2)}) collective-permute-start(bf16[912,128]{1,0:T(8,128)(2,1)} %get-tuple-element.14), channel_id=1, source_target_pairs={{0,1},{1,0},{2,3},{3,2},{4,5},{5,4},{6,7},{7,6},{8,11},{9,10},{10,... | collective-permute-start | bytes 700424 | tf_op jit(solution)/shard_map/ppermute | solution.py:338
  104.7 34.0 %collective-permute-start.2 = (bf16[912,128]{1,0:T(8,128)(2,1)}, bf16[912,128]{1,0:T(8,128)(2,1)S(1)}, u32[]{:S(2)}, u32[]{:S(2)}) collective-permute-start(bf16[912,128]{1,0:T(8,128)(2,1)} %get-tuple-element.16), channel_id=1, source_target_pairs={{0,3},{1,2},{2,1},{3,0},{4,7},{5,6},{6,5},{7,4},{8,15},{9,14},{10,... | collective-permute-start | bytes 700424 | tf_op jit(solution)/shard_map/ppermute | solution.py:338
  108.1 31.4 %collective-permute-start.4 = (bf16[912,128]{1,0:T(8,128)(2,1)S(1)}, bf16[912,128]{1,0:T(8,128)(2,1)S(1)}, u32[]{:S(2)}, u32[]{:S(2)}) collective-permute-start(bf16[912,128]{1,0:T(8,128)(2,1)S(1)} %copy-done.14), channel_id=1, source_target_pairs={{0,7},{1,6},{2,5},{3,4},{4,3},{5,2},{6,1},{7,0},{8,9},{9,8},{10,11... | collective-permute-start | bytes 700424 | tf_op jit(solution)/shard_map/ppermute | solution.py:338
  128.9 12.4 %collective-permute-start.8 = (bf16[912,128]{1,0:T(8,128)(2,1)S(1)}, bf16[912,128]{1,0:T(8,128)(2,1)S(1)}, u32[]{:S(2)}, u32[]{:S(2)}) collective-permute-start(bf16[912,128]{1,0:T(8,128)(2,1)S(1)} %collective-permute-done.7), channel_id=1, source_target_pairs={{0,6},{1,7},{2,4},{3,5},{4,2},{5,3},{6,0},{7,1},{8,10},{9,11},{10,... | collective-permute-start | bytes 700424 | tf_op jit(solution)/shard_map/ppermute | solution.py:338
  138.8 0.7 copy-start.7
  139.5 0.7 copy-start.9
  141.3 0.7 copy-start.11
  142.0 1.0 copy-start.5
  143.0 0.9 copy-start.8
  144.0 0.9 copy-start.10
  144.9 0.9 copy-start.12
